TPU v7x, 256 devices: a whole 4x4x8 slice. The times are simulated.
256 devices in a mesh: dom: 128 (over x, y, z), col: 2 (over core).
Axes of the slice: x: 4, y: 4, z: 8, core: 2. Of those that a mesh axis runs over, the one named last changes fastest.
Arguments:
- features: bfloat16 [196608, 512], P('dom', 'col'), may hold values from -6 to 6
- cotangent: bfloat16 [196608, 512], P('dom', 'col'), may hold values from -6 to 6
- w_self: bfloat16 [512, 512], P('col'), may hold values from -0.25 to 0.25
- w_neigh: bfloat16 [512, 512], P('col'), may hold values from -0.25 to 0.25
- hub_rows: int32 [4096], P('dom'), may hold values from 0 to 1535, as said below
- send_rows: int32 [128, 128, 32], P('dom'), may hold values from 0 to 1535
- neighbours: int32 [196608, 12], P('dom'), may hold values from 0 to 9727, as said below
- counts: int32 [196608], P('dom'), may hold values from 8 to 12
Outputs:
- layer_out: bfloat16 [196608, 512], P('dom', 'col')
- grad_self: float32 [512, 512], P('col')
- grad_neigh: float32 [512, 512], P('col')
Inputs may be any that keep to these rules, and one draw needn't show every extreme that they name: `hub_rows`: the 32 entries of one partition are distinct rows of that partition. `neighbours`: the first 8 slots of a node are always live; every hub row and every received row of the lookup table is named by some live slot in every partition.
All inputs are finite; a program needn't handle non-finite values.
Results may differ from a plain program's by a relative error of at most 0.0053.
Values may be sent and summed in bfloat16 or wider, within the bound.
No kernel may reach another device: no remote copies, remote signals or barrier semaphores. Data moves between devices by JAX's collectives and lax.ppermute only.
A program may use at most 64 MiB of HBM per device.

v0:
```python
import math

import jax
import jax.numpy as jnp
from jax import lax
from jax.sharding import PartitionSpec as P


def activation(value):
    return jax.nn.gelu(value, approximate=True)


def aggregate(lookup, slots, live):
    total = jnp.zeros((slots.shape[0], lookup.shape[1]), jnp.float32)
    for slot in range(slots.shape[1]):
        picked = lookup[slots[:, slot]].astype(jnp.float32)
        total = total + jnp.where((slot < live)[:, None], picked, 0.0)
    return (total / live[:, None].astype(jnp.float32)).astype(jnp.bfloat16)


def shards(features, cotangent, w_self, w_neigh, hub_rows, send_rows, neighbours, counts):
    half_width = features.shape[1]
    hub_block = lax.all_gather(features[hub_rows], "dom", axis=0, tiled=True)
    outgoing = features[send_rows[0]]
    incoming = lax.all_to_all(outgoing, "dom", split_axis=0, concat_axis=0, tiled=True)
    lookup = jnp.concatenate([features, hub_block, incoming.reshape(-1, half_width)], 0)
    neigh_mean = aggregate(lookup, neighbours, counts)
    partial_value = jnp.dot(features, w_self, preferred_element_type=jnp.float32) + jnp.dot(
        neigh_mean, w_neigh, preferred_element_type=jnp.float32
    )
    pre = lax.psum_scatter(partial_value, "col", scatter_dimension=1, tiled=True)
    layer_out = activation(pre).astype(jnp.bfloat16)
    _, pullback = jax.vjp(activation, pre)
    grad_pre = pullback(cotangent.astype(jnp.float32))[0].astype(jnp.bfloat16)
    grad_full = lax.all_gather(grad_pre, "col", axis=1, tiled=True)
    contract = (((0,), (0,)), ((), ()))
    self_term = lax.dot_general(features, grad_full, contract, preferred_element_type=jnp.float32)
    neigh_term = lax.dot_general(
        neigh_mean, grad_full, contract, preferred_element_type=jnp.float32
    )
    self_sum, neigh_sum = lax.psum((self_term, neigh_term), "dom")
    factor = 1.0 / math.sqrt(features.shape[0] * lax.axis_size("dom"))
    return (layer_out, self_sum * factor, neigh_sum * factor)


def solution(mesh):
    placed = (
        P("dom", "col"),
        P("dom", "col"),
        P("col", None),
        P("col", None),
        P("dom"),
        P("dom", None, None),
        P("dom", None),
        P("dom"),
    )
    return jax.shard_map(
        shards,
        mesh=mesh,
        in_specs=placed,
        out_specs=(P("dom", "col"), P("col", None), P("col", None)),
        check_vma=False,
    )
```

profile of v0, /device:TPU:8, one launch (start us, length us, event | category | flops | bytes accessed | tf_op | source)
XLA Modules:
  0.0 517.4 jit_solution(130982961269492205)
XLA Ops:
  7.2 0.0 copy-start
  7.2 0.0 all-gather.6.cloned.1.call-start
  7.2 0.7 compare_select_fusion.13
  7.9 2.4 gather_fusion
  10.4 0.0 all-gather.6.cloned.1.call-update
  10.4 0.7 compare_select_fusion
  11.1 0.1 copy.14
  11.2 0.1 reshape.62
  11.3 17.1 %gather_fusion.1 = bf16[4096,256]{1,0:T(8,128)(2,1)} fusion(bf16[1536,256]{1,0:T(8,128)(2,1)} %param.8, s32[4096]{0:T(1024)S(1)} %broadcast_clamp_fusion), kind=kCustom, calls=%fused_computation.1 | custom fusion | bytes 4210688 | tf_op jit(solution)/shard_map/gather | solution.py:24
  28.4 0.0 copy-start.8
  28.4 0.0 copy-start.7
  28.4 0.0 copy-start.1
  28.4 15.5 %all-to-all-start = ((bf16[128,32,256]{2,1,0:T(8,128)(2,1)}), bf16[128,32,256]{2,1,0:T(8,128)(2,1)S(1)}, u32[]{:S(2)}, u32[]{:S(2)}) async-start(bf16[128,32,256]{2,1,0:T(8,128)(2,1)} %bitcast.17), calls=%async_computation | async-start | bytes 4194304 | tf_op jit(solution)/shard_map/all_to_all | solution.py:25
  43.9 0.0 reduce-scatter.2.cloned.1.call-start
  43.9 0.0 copy-done.8
  43.9 0.0 copy-done.7
  44.0 0.2 fusion.10
  44.3 0.0 copy-done
  44.3 0.0 copy-done.1
  44.3 2.2 fusion.22
  46.5 84.6 %all-gather.6.cloned.1.call-done = bf16[4096,256]{1,0:T(8,128)(2,1)} async-done(((bf16[32,256]{1,0:T(8,128)(2,1)}), bf16[4096,256]{1,0:T(8,128)(2,1)}) %all-gather.6.cloned.1.call-update) | async-done | bytes 2097168 | tf_op jit(solution)/shard_map/all_gather | solution.py:23
  131.2 0.0 all-to-all-done
  131.2 15.6 %pad_maximum_fusion = bf16[9728,256]{1,0:T(8,128)(2,1)} fusion(bf16[4096,256]{1,0:T(8,128)(2,1)S(1)} %bitcast.16, bf16[4096,256]{1,0:T(8,128)(2,1)} %all-gather.6.cloned.1.call-done, bf16[1536,256]{1,0:T(8,128)(2,1)S(1)} %copy-done.1), kind=kLoop, calls=%fused_computation.14 | loop fusion | flops 14942208 | bytes 9961472 | tf_op jit(solution)/shard_map/concatenate | solution.py:26
  146.7 6.7 %gather_fusion.10 = bf16[1536,256]{1,0:T(8,128)(2,1)S(1)} fusion(bf16[9728,256]{1,0:T(8,128)(2,1)} %pad_maximum_fusion, s32[2048]{0:T(1024)S(1)} %get-tuple-element.40), kind=kCustom, calls=%fused_computation.10 | custom fusion | bytes 1579008 | tf_op jit(solution)/shard_map/gather | solution.py:16
  153.4 6.7 %gather_fusion.11 = bf16[1536,256]{1,0:T(8,128)(2,1)S(1)} fusion(bf16[9728,256]{1,0:T(8,128)(2,1)} %pad_maximum_fusion, s32[2048]{0:T(1024)S(1)} %get-tuple-element.39), kind=kCustom, calls=%fused_computation.11 | custom fusion | bytes 1579008 | tf_op jit(solution)/shard_map/gather | solution.py:16
  160.1 7.5 %gather_fusion.12 = bf16[1536,256]{1,0:T(8,128)(2,1)} fusion(bf16[9728,256]{1,0:T(8,128)(2,1)} %pad_maximum_fusion, s32[2048]{0:T(1024)S(1)} %get-tuple-element.38), kind=kCustom, calls=%fused_computation.12 | custom fusion | bytes 1579008 | tf_op jit(solution)/shard_map/gather | solution.py:16
  167.7 7.6 %gather_fusion.13 = bf16[1536,256]{1,0:T(8,128)(2,1)} fusion(bf16[9728,256]{1,0:T(8,128)(2,1)} %pad_maximum_fusion, s32[2048]{0:T(1024)S(1)} %get-tuple-element.37), kind=kCustom, calls=%fused_computation.13 | custom fusion | bytes 1579008 | tf_op jit(solution)/shard_map/gather | solution.py:16
  175.3 7.6 %gather_fusion.2 = bf16[1536,256]{1,0:T(8,128)(2,1)} fusion(bf16[9728,256]{1,0:T(8,128)(2,1)} %pad_maximum_fusion, s32[2048]{0:T(1024)S(1)} %get-tuple-element.48), kind=kCustom, calls=%fused_computation.2 | custom fusion | bytes 1579008 | tf_op jit(solution)/shard_map/gather | solution.py:16
  182.8 7.6 %gather_fusion.3 = bf16[1536,256]{1,0:T(8,128)(2,1)} fusion(bf16[9728,256]{1,0:T(8,128)(2,1)} %pad_maximum_fusion, s32[2048]{0:T(1024)S(1)} %get-tuple-element.47), kind=kCustom, calls=%fused_computation.3 | custom fusion | bytes 1579008 | tf_op jit(solution)/shard_map/gather | solution.py:16
  190.4 7.6 %gather_fusion.4 = bf16[1536,256]{1,0:T(8,128)(2,1)} fusion(bf16[9728,256]{1,0:T(8,128)(2,1)} %pad_maximum_fusion, s32[2048]{0:T(1024)S(1)} %get-tuple-element.46), kind=kCustom, calls=%fused_computation.4 | custom fusion | bytes 1579008 | tf_op jit(solution)/shard_map/gather | solution.py:16
  197.9 7.6 %gather_fusion.5 = bf16[1536,256]{1,0:T(8,128)(2,1)} fusion(bf16[9728,256]{1,0:T(8,128)(2,1)} %pad_maximum_fusion, s32[2048]{0:T(1024)S(1)} %get-tuple-element.45), kind=kCustom, calls=%fused_computation.5 | custom fusion | bytes 1579008 | tf_op jit(solution)/shard_map/gather | solution.py:16
  205.5 7.5 %gather_fusion.6 = bf16[1536,256]{1,0:T(8,128)(2,1)} fusion(bf16[9728,256]{1,0:T(8,128)(2,1)} %pad_maximum_fusion, s32[2048]{0:T(1024)S(1)} %get-tuple-element.44), kind=kCustom, calls=%fused_computation.6 | custom fusion | bytes 1579008 | tf_op jit(solution)/shard_map/gather | solution.py:16
  213.0 7.6 %gather_fusion.7 = bf16[1536,256]{1,0:T(8,128)(2,1)} fusion(bf16[9728,256]{1,0:T(8,128)(2,1)} %pad_maximum_fusion, s32[2048]{0:T(1024)S(1)} %get-tuple-element.43), kind=kCustom, calls=%fused_computation.7 | custom fusion | bytes 1579008 | tf_op jit(solution)/shard_map/gather | solution.py:16
  220.6 7.6 %gather_fusion.8 = bf16[1536,256]{1,0:T(8,128)(2,1)} fusion(bf16[9728,256]{1,0:T(8,128)(2,1)} %pad_maximum_fusion, s32[2048]{0:T(1024)S(1)} %get-tuple-element.42), kind=kCustom, calls=%fused_computation.8 | custom fusion | bytes 1579008 | tf_op jit(solution)/shard_map/gather | solution.py:16
  228.1 7.6 %gather_fusion.9 = bf16[1536,256]{1,0:T(8,128)(2,1)} fusion(bf16[9728,256]{1,0:T(8,128)(2,1)} %pad_maximum_fusion, s32[2048]{0:T(1024)S(1)} %get-tuple-element.41), kind=kCustom, calls=%fused_computation.9 | custom fusion | bytes 1579008 | tf_op jit(solution)/shard_map/gather | solution.py:16
  235.7 0.0 copy-start.2
  235.7 0.0 copy-start.6
  235.7 6.3 %divide_convert_fusion = bf16[1536,256]{1,0:T(8,128)(2,1)S(1)} fusion(bf16[1536,256]{1,0:T(8,128)(2,1)} %gather_fusion.13, bf16[1536,256]{1,0:T(8,128)(2,1)} %gather_fusion.12, bf16[1536,256]{1,0:T(8,128)(2,1)S(1)} %gather_fusion.11, bf16[1536,256]{1,0:T(8,128)(2,1)S(1)} %gather_fusion.10, bf16[1536,256]{1,0:T(8,128)(2,1)} %gather_fusion.9, ...), kind=kLoop, calls=%fused_computation.31 | loop fusion | flops 14548992 | bytes 10248192 | tf_op jit(solution)/shard_map/convert_element_type | solution.py:18
  242.0 0.0 copy-done.2
  242.0 0.0 copy-done.6
  242.0 2.3 convolution_add_fusion
  244.3 0.0 copy-start.4
  244.3 0.0 reduce-scatter.2.cloned.1.call-update
  244.3 0.0 all-gather.4.cloned.1.call-start
  244.4 13.6 %reduce-scatter.2.cloned.1.call-done = f32[1536,256]{1,0:T(8,128)} async-done(((f32[1536,512]{1,0:T(8,128)}), f32[1536,256]{1,0:T(8,128)}) %reduce-scatter.2.cloned.1.call-update) | async-done | bytes 1572880 | tf_op jit(solution)/shard_map/reduce_scatter | solution.py:31
  257.9 0.0 copy-done.4
  257.9 3.8 fusion.2
  261.7 0.0 all-gather.4.cloned.1.call-update
  261.7 0.0 all-reduce.3.cloned.1.call-start
  261.8 16.4 %all-gather.4.cloned.1.call-done = bf16[1536,512]{1,0:T(8,128)(2,1)} async-done(((bf16[1536,256]{1,0:T(8,128)(2,1)}), bf16[1536,512]{1,0:T(8,128)(2,1)}) %all-gather.4.cloned.1.call-update) | async-done | bytes 1572880 | tf_op jit(solution)/shard_map/all_gather | solution.py:35
  278.2 0.0 copy-start.3
  278.2 3.0 fusion.23
  281.2 0.0 copy-done.3
  281.3 1.4 convolution_bitcast_fusion
  282.7 0.0 all-reduce.3.cloned.1.call-update
  282.7 225.0 %all-reduce.3.cloned.1.call-done = (f32[256,512]{0,1:T(8,128)}, f32[256,512]{0,1:T(8,128)}) async-done(((f32[256,512]{0,1:T(8,128)}, f32[256,512]{0,1:T(8,128)}), (f32[256,512]{0,1:T(8,128)}, f32[256,512]{0,1:T(8,128)})) %all-reduce.3.cloned.1.call-update) | async-done | bytes 1048592 | tf_op jit(solution)/shard_map/psum | solution.py:41
  507.7 0.0 copy-start.5
  507.7 1.1 broadcast_multiply_fusion.1
  508.8 1.0 copy.16
  509.8 0.0 copy-done.5
  509.9 1.0 copy.17
  (11 shorter events, 0.1 us)
Async XLA Ops:
  7.2 37.2 %copy-start = (bf16[256,512]{1,0:T(8,128)(2,1)S(1)}, bf16[256,512]{1,0:T(8,128)(2,1)}, u32[]{:S(2)}) copy-start(bf16[256,512]{1,0:T(8,128)(2,1)} %param.10) | copy-start | bytes 786436
  7.2 124.0 %all-gather.6.cloned.1.call-start = ((), (), s32[]{:S(2)}) async-start(), calls=%async_computation.4 | async-start | bytes 2113536 | tf_op jit(solution)/shard_map/all_gather | solution.py:23
  28.4 15.6 %copy-start.8 = (s32[1536]{0:T(1024)S(1)}, s32[1536]{0:T(1024)}, u32[]{:S(2)}) copy-start(s32[1536]{0:T(1024)} %param.15) | copy-start | bytes 18436
  28.4 15.6 %copy-start.7 = (s32[1536,12]{0,1:T(8,128)S(1)}, s32[1536,12]{0,1:T(8,128)}, u32[]{:S(2)}) copy-start(s32[1536,12]{0,1:T(8,128)} %param.14) | copy-start | bytes 221188
  28.4 16.0 %copy-start.1 = (bf16[1536,256]{1,0:T(8,128)(2,1)S(1)}, bf16[1536,256]{1,0:T(8,128)(2,1)}, u32[]{:S(2)}) copy-start(bf16[1536,256]{1,0:T(8,128)(2,1)} %param.8) | copy-start | bytes 2359300
  28.4 102.8 %all-to-all-start = ((bf16[128,32,256]{2,1,0:T(8,128)(2,1)}), bf16[128,32,256]{2,1,0:T(8,128)(2,1)S(1)}, u32[]{:S(2)}, u32[]{:S(2)}) async-start(bf16[128,32,256]{2,1,0:T(8,128)(2,1)} %bitcast.17), calls=%async_computation | async-start | bytes 4194304 | tf_op jit(solution)/shard_map/all_to_all | solution.py:25
  43.9 214.1 %reduce-scatter.2.cloned.1.call-start = ((), (), s32[]{:S(2)}) async-start(), calls=%async_computation.2 | async-start | bytes 4718592 | tf_op jit(solution)/shard_map/reduce_scatter | solution.py:31
  235.7 6.3 %copy-start.2 = (f32[1536,512]{1,0:T(8,128)S(1)}, f32[1536,512]{1,0:T(8,128)}, u32[]{:S(2)}) copy-start(f32[1536,512]{1,0:T(8,128)} %fusion.22) | copy-start | bytes 9437188
  235.7 6.3 %copy-start.6 = (bf16[256,512]{1,0:T(8,128)(2,1)S(1)}, bf16[256,512]{1,0:T(8,128)(2,1)}, u32[]{:S(2)}) copy-start(bf16[256,512]{1,0:T(8,128)(2,1)} %param.11) | copy-start | bytes 786436
  244.3 13.7 %copy-start.4 = (bf16[1536,256]{1,0:T(8,128)(2,1)S(1)}, bf16[1536,256]{1,0:T(8,128)(2,1)}, u32[]{:S(2)}) copy-start(bf16[1536,256]{1,0:T(8,128)(2,1)} %param.9) | copy-start | bytes 2359300
  244.3 33.9 %all-gather.4.cloned.1.call-start = ((), (), s32[]{:S(2)}) async-start(), calls=%async_computation.3 | async-start | bytes 2359296 | tf_op jit(solution)/shard_map/all_gather | solution.py:35
  261.7 245.9 %all-reduce.3.cloned.1.call-start = ((), (), s32[]{:S(2)}) async-start(), calls=%async_computation.5 | async-start | bytes 2097152 | tf_op jit(solution)/shard_map/psum | solution.py:41
  278.2 3.1 copy-start.3
  507.7 2.1 copy-start.5
Sparse Core Ops, SparseCore 0:
  12.3 118.7 all-gather.5
  244.4 13.4 reduce-scatter.1
  261.8 16.3 all-gather.3
  285.0 222.5 all-reduce.2
where the time goes:
time: 518 us; the launch traced here: 517 us
  waiting for transfers between devices  340 us (66%)
  local copies, waits for them, and re-layouts  111 us (21%)
  other arithmetic  28.6 us (6%)
  starting transfers between devices  15.7 us (3%)
  between operations  14 us (3%)
  matrix products  8.9 us (2%)
    psum x1, waiting for transfers between devices, shards(): self_sum, neigh_sum = lax.psum((self_term, neigh_term), 'dom')  225 us
    gather x12, local copies, waits for them, and re-layouts, aggregate(): picked = lookup[slots[:, slot]].astype(jnp.float32)  89 us
    all_gather x1, waiting for transfers between devices, shards(): hub_block = lax.all_gather(features[hub_rows], 'dom', axis=0, tiled=True)  84.6 us
    gather x1, local copies, waits for them, and re-layouts, shards(): outgoing = features[send_rows[0]]  17.1 us
    all_gather x1, waiting for transfers between devices, shards(): grad_full = lax.all_gather(grad_pre, 'col', axis=1, tiled=True)  16.4 us
    concatenate x1, other arithmetic, shards(): jnp.concatenate([features, hub_block, incoming.reshape(-1, half_width)], 0)  15.6 us
    all_to_all x1, starting transfers between devices, shards(): lax.all_to_all(outgoing, 'dom', split_axis=0, concat_axis=0, tiled=True)  15.5 us
    reduce_scatter x1, waiting for transfers between devices, shards(): lax.psum_scatter(partial_value, 'col', scatter_dimension=1, tiled=True)  13.6 us
  transfers between devices with their start and end apart: 5, of which 4 were waited for; matrix products, arithmetic and copies ran while one was open for 4% of the time, Pallas kernels for 0%

commit v1 on v0

v1 whole, which is shorter than its diff:
```python
import math

import jax
import jax.numpy as jnp
from jax import lax
from jax.sharding import PartitionSpec as P

SWAP = [(0, 1), (1, 0)]


def activation(value):
    return jax.nn.gelu(value, approximate=True)


def aggregate(lookup, slots, live):
    total = jnp.zeros((slots.shape[0], lookup.shape[1]), jnp.float32)
    for slot in range(slots.shape[1]):
        picked = lookup[slots[:, slot]].astype(jnp.float32)
        total = total + jnp.where((slot < live)[:, None], picked, 0.0)
    return (total / live[:, None].astype(jnp.float32)).astype(jnp.bfloat16)


def swap(value):
    return lax.ppermute(value, "col", SWAP)


def dot(left, right):
    return jnp.dot(left, right, preferred_element_type=jnp.float32)


def shards(features, cotangent, w_self, w_neigh, hub_rows, send_rows, neighbours, counts):
    parts = lax.axis_size("dom")
    nodes, half = features.shape
    core = lax.axis_index("col")
    weights = jnp.stack([w_self, w_neigh]).reshape(2, half, 2, half)
    w_mine = lax.dynamic_index_in_dim(weights, core, 2, keepdims=False)
    w_other = swap(lax.dynamic_index_in_dim(weights, 1 - core, 2, keepdims=False))
    features_other = swap(features)

    picks = jnp.concatenate(
        [send_rows[0], jnp.broadcast_to(hub_rows[None], (parts, hub_rows.shape[0]))], 1
    ).reshape(-1)
    onehot = (picks[:, None] == jnp.arange(nodes, dtype=jnp.int32)[None, :]).astype(jnp.bfloat16)
    outgoing = dot(onehot, features).astype(jnp.bfloat16).reshape(parts, -1, half)
    incoming = lax.all_to_all(outgoing, "dom", split_axis=0, concat_axis=0, tiled=True)
    blk = send_rows.shape[2]
    own_dot = dot(features, w_mine[0]) + dot(features_other, w_other[0])

    hubs = hub_rows.shape[0]
    width = blk + hubs
    slot = neighbours - nodes
    is_hub = slot < parts * hubs
    local = jnp.where(is_hub, slot, slot - parts * hubs)
    owner = jnp.where(is_hub, local // hubs, local // blk)
    within = jnp.where(is_hub, local % hubs + blk, local % blk)
    place = jnp.where(slot < 0, neighbours, nodes + owner * width + within)
    lookup = jnp.concatenate([features, incoming.reshape(-1, half)], 0)
    neigh_mean = aggregate(lookup, place, counts)
    mean_other = swap(neigh_mean)

    pre = own_dot + dot(neigh_mean, w_mine[1]) + dot(mean_other, w_other[1])
    layer_out = activation(pre).astype(jnp.bfloat16)
    _, pullback = jax.vjp(activation, pre)
    grad_pre = pullback(cotangent.astype(jnp.float32))[0].astype(jnp.bfloat16)

    def weight_grad(rows):
        return lax.dot_general(
            rows, grad_pre, (((0,), (0,)), ((), ())), preferred_element_type=jnp.float32
        ).astype(jnp.bfloat16)

    mine = jnp.stack([weight_grad(features), weight_grad(neigh_mean)])
    other = swap(jnp.stack([weight_grad(features_other), weight_grad(mean_other)]))
    left = jnp.where(core == 0, mine, other)
    right = jnp.where(core == 0, other, mine)
    partial = jnp.concatenate([left, right], 2).reshape(parts, -1, 2 * half)
    pieces = lax.all_to_all(partial, "dom", split_axis=0, concat_axis=0, tiled=True)
    factor = 1.0 / math.sqrt(nodes * parts)
    piece = (pieces.astype(jnp.float32).sum(0) * factor).astype(jnp.bfloat16)
    sums = lax.all_to_all(
        jnp.broadcast_to(piece[None], (parts,) + piece.shape),
        "dom", split_axis=0, concat_axis=0, tiled=True,
    )
    sums = sums.reshape(2, half, 2 * half).astype(jnp.float32)
    return (layer_out, sums[0], sums[1])


def solution(mesh):
    placed = (
        P("dom", "col"),
        P("dom", "col"),
        P("col", None),
        P("col", None),
        P("dom"),
        P("dom", None, None),
        P("dom", None),
        P("dom"),
    )
    return jax.shard_map(
        shards,
        mesh=mesh,
        in_specs=placed,
        out_specs=(P("dom", "col"), P("col", None), P("col", None)),
        check_vma=False,
    )
```

time: 518 us -> 301 us (0.58)
  waiting for transfers between devices: 340 us -> 111 us
  blocking collectives: 0 us -> 27.4 us
  other arithmetic: 28.6 us -> 13.5 us
  between operations: 14 us -> 0.96 us
  local copies, waits for them, and re-layouts: 111 us -> 98.7 us
  matrix products: 8.9 us -> 21.1 us
  starting transfers between devices: 15.7 us -> 26 us
    psum x1 -> x0, waiting for transfers between devices: 225 us -> none  [shards(): self_sum, neigh_sum = lax.psum((self_term, neigh_term), 'dom')]
    all_gather x2 -> x0, waiting for transfers between devices: 101 us -> none  [the longest x1 84.6 us: shards(): hub_block = lax.all_gather(features[hub_rows], 'dom', axis=0, tiled=True)]
    all_to_all x1, waiting for transfers between devices: 0.01 us -> 93.6 us  [shards(): lax.all_to_all(outgoing, 'dom', split_axis=0, concat_axis=0, tiled=True)]
    all_to_all x0 -> x1, blocking collectives: none -> 27.4 us  [shards(): lax.all_to_all(partial, 'dom', split_axis=0, concat_axis=0, tiled=True)]
    gather x2 -> x0, local copies, waits for them, and re-layouts: 19.5 us -> none  [the longest x1 17.1 us: shards(): outgoing = features[send_rows[0]]]
    all_to_all x0 -> x1, waiting for transfers between devices: none -> 16.6 us  [shards(): lax.all_to_all(jnp.broadcast_to(piece[None], (parts,) + piece.shape), 'do...]
    reduce_scatter x1 -> x0, waiting for transfers between devices: 13.6 us -> none  [shards(): lax.psum_scatter(partial_value, 'col', scatter_dimension=1, tiled=True)]
    dot_general x4 -> x9, matrix products: 8.9 us -> 21.1 us  [the longest x5 17.3 us: dot(): return jnp.dot(left, right, preferred_element_type=jnp.float32)]
  transfers between devices with their start and end apart: 5 -> 6, of which waited for: 4 -> 3; matrix products, arithmetic and copies ran while one was open for 4% -> 37% of each run, Pallas kernels for 0% -> 0%
where the time goes in v1:
time: 301 us; the launch traced here: 298 us
  waiting for transfers between devices  111 us (37%)
  local copies, waits for them, and re-layouts  98.7 us (33%)
  blocking collectives  27.4 us (9%)
  starting transfers between devices  26 us (9%)
  matrix products  21.1 us (7%)
  other arithmetic  13.5 us (4%)
    all_to_all x1, waiting for transfers between devices, shards(): lax.all_to_all(outgoing, 'dom', split_axis=0, concat_axis=0, tiled=True)  93.6 us
    gather x12, local copies, waits for them, and re-layouts, aggregate(): picked = lookup[slots[:, slot]].astype(jnp.float32)  89.2 us
    all_to_all x1, blocking collectives, shards(): lax.all_to_all(partial, 'dom', split_axis=0, concat_axis=0, tiled=True)  27.4 us
    dot_general x5, matrix products, dot(): return jnp.dot(left, right, preferred_element_type=jnp.float32)  17.3 us
    all_to_all x1, waiting for transfers between devices, shards(): lax.all_to_all(jnp.broadcast_to(piece[None], (parts,) + piece.shape), 'do...  16.6 us
    all_to_all x1, starting transfers between devices, shards(): lax.all_to_all(outgoing, 'dom', split_axis=0, concat_axis=0, tiled=True)  15.9 us
    all_to_all x1, starting transfers between devices, shards(): lax.all_to_all(jnp.broadcast_to(piece[None], (parts,) + piece.shape), 'do...  8.79 us
    convert_element_type x2, other arithmetic, aggregate(): return (total / live[:, None].astype(jnp.float32)).astype(jnp.bfloat16)  6.08 us
  transfers between devices with their start and end apart: 6, of which 3 were waited for; matrix products, arithmetic and copies ran while one was open for 37% of the time, Pallas kernels for 0%

profile of v1, /device:TPU:8, one launch (start us, length us, event | category | flops | bytes accessed | tf_op | source)
XLA Modules:
  0.0 298.3 jit_solution(2158350216339564973)
XLA Ops:
  0.6 0.7 pad.9.clone
  1.4 0.8 pad_add_fusion
  2.1 0.1 copy.27
  2.2 0.1 eq.22
  2.3 12.3 %fusion.2 = bf16[8192,256]{1,0:T(8,128)(2,1)} fusion(bf16[1536,256]{1,0:T(8,128)(2,1)} %param.8, s32[8192]{0:T(1024)S(1)} %eq.22), kind=kOutput, calls=%fused_computation.15 | convolution fusion | flops 6457131008 | bytes 5013504 | tf_op jit(solution)/shard_map/dot_general | solution.py:28
  14.6 15.9 %all-to-all-start = ((bf16[128,64,256]{2,1,0:T(8,128)(2,1)}), bf16[128,64,256]{2,1,0:T(8,128)(2,1)}, u32[]{:S(2)}, u32[]{:S(2)}) async-start(bf16[128,64,256]{2,1,0:T(8,128)(2,1)} %bitcast.49), calls=%async_computation | async-start | bytes 8388608 | tf_op jit(solution)/shard_map/all_to_all | solution.py:45
  30.5 0.0 copy-done
  30.5 0.0 copy-start.5
  30.6 0.0 copy-start.4
  30.6 0.1 collective-permute-start.1
  30.7 0.0 copy-done.2
  30.7 0.1 copy.23
  30.8 0.0 copy-done.3
  30.8 0.1 copy.24
  31.0 0.1 fusion.18
  31.0 0.8 copy.26
  31.9 0.5 collective-permute-start
  32.4 0.0 copy-done.5
  32.4 0.0 copy-done.4
  32.4 0.1 fusion.24
  32.5 0.2 fusion.29
  32.9 93.6 %all-to-all-done = bf16[128,64,256]{2,1,0:T(8,128)(2,1)} async-done(((bf16[128,64,256]{2,1,0:T(8,128)(2,1)}), bf16[128,64,256]{2,1,0:T(8,128)(2,1)}, u32[]{:S(2)}, u32[]{:S(2)}) %all-to-all-start) | async-done | bytes 4194336 | tf_op jit(solution)/shard_map/all_to_all | solution.py:45
  126.5 5.7 %pad_maximum_fusion = bf16[9728,256]{1,0:T(8,128)(2,1)} fusion(bf16[8192,256]{1,0:T(8,128)(2,1)} %bitcast.8, bf16[1536,256]{1,0:T(8,128)(2,1)S(1)} %copy-done), kind=kLoop, calls=%fused_computation.16 | loop fusion | flops 9961472 | bytes 9961472 | tf_op jit(solution)/shard_map/concatenate | solution.py:57
  132.2 6.7 %gather_fusion = bf16[1536,256]{1,0:T(8,128)(2,1)S(1)} fusion(bf16[9728,256]{1,0:T(8,128)(2,1)} %pad_maximum_fusion, s32[2048]{0:T(1024)S(1)} %get-tuple-element.55), kind=kCustom, calls=%fused_computation | custom fusion | bytes 1579008 | tf_op jit(solution)/shard_map/gather | solution.py:18
  138.9 6.7 %gather_fusion.1 = bf16[1536,256]{1,0:T(8,128)(2,1)S(1)} fusion(bf16[9728,256]{1,0:T(8,128)(2,1)} %pad_maximum_fusion, s32[2048]{0:T(1024)S(1)} %get-tuple-element.54), kind=kCustom, calls=%fused_computation.1 | custom fusion | bytes 1579008 | tf_op jit(solution)/shard_map/gather | solution.py:18
  145.6 7.6 %gather_fusion.10 = bf16[1536,256]{1,0:T(8,128)(2,1)} fusion(bf16[9728,256]{1,0:T(8,128)(2,1)} %pad_maximum_fusion, s32[2048]{0:T(1024)S(1)} %get-tuple-element.45), kind=kCustom, calls=%fused_computation.10 | custom fusion | bytes 1579008 | tf_op jit(solution)/shard_map/gather | solution.py:18
  153.2 7.6 %gather_fusion.11 = bf16[1536,256]{1,0:T(8,128)(2,1)} fusion(bf16[9728,256]{1,0:T(8,128)(2,1)} %pad_maximum_fusion, s32[2048]{0:T(1024)S(1)} %get-tuple-element.44), kind=kCustom, calls=%fused_computation.11 | custom fusion | bytes 1579008 | tf_op jit(solution)/shard_map/gather | solution.py:18
  160.8 7.6 %gather_fusion.2 = bf16[1536,256]{1,0:T(8,128)(2,1)} fusion(bf16[9728,256]{1,0:T(8,128)(2,1)} %pad_maximum_fusion, s32[2048]{0:T(1024)S(1)} %get-tuple-element.53), kind=kCustom, calls=%fused_computation.2 | custom fusion | bytes 1579008 | tf_op jit(solution)/shard_map/gather | solution.py:18
  168.3 7.5 %gather_fusion.3 = bf16[1536,256]{1,0:T(8,128)(2,1)} fusion(bf16[9728,256]{1,0:T(8,128)(2,1)} %pad_maximum_fusion, s32[2048]{0:T(1024)S(1)} %get-tuple-element.52), kind=kCustom, calls=%fused_computation.3 | custom fusion | bytes 1579008 | tf_op jit(solution)/shard_map/gather | solution.py:18
  175.9 7.6 %gather_fusion.4 = bf16[1536,256]{1,0:T(8,128)(2,1)} fusion(bf16[9728,256]{1,0:T(8,128)(2,1)} %pad_maximum_fusion, s32[2048]{0:T(1024)S(1)} %get-tuple-element.51), kind=kCustom, calls=%fused_computation.4 | custom fusion | bytes 1579008 | tf_op jit(solution)/shard_map/gather | solution.py:18
  183.4 7.6 %gather_fusion.5 = bf16[1536,256]{1,0:T(8,128)(2,1)} fusion(bf16[9728,256]{1,0:T(8,128)(2,1)} %pad_maximum_fusion, s32[2048]{0:T(1024)S(1)} %get-tuple-element.50), kind=kCustom, calls=%fused_computation.5 | custom fusion | bytes 1579008 | tf_op jit(solution)/shard_map/gather | solution.py:18
  191.0 7.8 %gather_fusion.6 = bf16[1536,256]{1,0:T(8,128)(2,1)} fusion(bf16[9728,256]{1,0:T(8,128)(2,1)} %pad_maximum_fusion, s32[2048]{0:T(1024)S(1)} %get-tuple-element.49), kind=kCustom, calls=%fused_computation.6 | custom fusion | bytes 1579008 | tf_op jit(solution)/shard_map/gather | solution.py:18
  198.8 7.6 %gather_fusion.7 = bf16[1536,256]{1,0:T(8,128)(2,1)} fusion(bf16[9728,256]{1,0:T(8,128)(2,1)} %pad_maximum_fusion, s32[2048]{0:T(1024)S(1)} %get-tuple-element.48), kind=kCustom, calls=%fused_computation.7 | custom fusion | bytes 1579008 | tf_op jit(solution)/shard_map/gather | solution.py:18
  206.3 7.6 %gather_fusion.8 = bf16[1536,256]{1,0:T(8,128)(2,1)} fusion(bf16[9728,256]{1,0:T(8,128)(2,1)} %pad_maximum_fusion, s32[2048]{0:T(1024)S(1)} %get-tuple-element.47), kind=kCustom, calls=%fused_computation.8 | custom fusion | bytes 1579008 | tf_op jit(solution)/shard_map/gather | solution.py:18
  213.9 7.6 %gather_fusion.9 = bf16[1536,256]{1,0:T(8,128)(2,1)} fusion(bf16[9728,256]{1,0:T(8,128)(2,1)} %pad_maximum_fusion, s32[2048]{0:T(1024)S(1)} %get-tuple-element.46), kind=kCustom, calls=%fused_computation.9 | custom fusion | bytes 1579008 | tf_op jit(solution)/shard_map/gather | solution.py:18
  221.4 6.1 %divide_convert_fusion = bf16[1536,256]{1,0:T(8,128)(2,1)S(1)} fusion(bf16[1536,256]{1,0:T(8,128)(2,1)} %gather_fusion.11, bf16[1536,256]{1,0:T(8,128)(2,1)} %gather_fusion.10, bf16[1536,256]{1,0:T(8,128)(2,1)} %gather_fusion.9, bf16[1536,256]{1,0:T(8,128)(2,1)} %gather_fusion.8, bf16[1536,256]{1,0:T(8,128)(2,1)} %gather_fusion.7, ...), kind=kLoop, calls=%fused_computation.36 | loop fusion | flops 14548992 | bytes 10248192 | tf_op jit(solution)/shard_map/convert_element_type | solution.py:20
  227.5 0.1 collective-permute-start.2
  227.6 0.4 fusion.20
  228.1 2.3 copy.31
  230.3 0.0 collective-permute-done
  230.3 0.0 collective-permute-done.1
  230.3 1.6 fusion.3
  232.0 0.0 copy-start.1
  232.0 0.4 convolution_add_fusion.1
  232.4 0.0 collective-permute-done.2
  232.4 0.7 copy-done.1
  233.1 2.7 fusion.6
  235.8 1.5 fusion.15
  237.3 1.5 fusion.17
  238.8 0.6 collective-permute-start.3
  239.4 0.4 fusion.16
  239.8 0.4 fusion.14
  240.2 0.4 collective-permute-done.3
  240.7 0.2 copy.33
  240.9 0.1 reshape.52
  241.0 27.4 %all_to_all.15 = bf16[128,4,512]{2,1,0:T(4,128)(2,1)S(1)} all-to-all(bf16[128,4,512]{2,1,0:T(4,128)(2,1)S(1)} %reshape.52), channel_id=1, replica_groups=mesh['dom'=128,'col'=2] {'dom'}, dimensions={0} | all-to-all | bytes 1048576 | tf_op jit(solution)/shard_map/all_to_all | solution.py:76
  268.4 0.3 convert_reduce_fusion
  268.7 0.9 broadcast_in_dim.130
  269.6 8.8 %all-to-all-start.2 = ((bf16[128,4,512]{2,1,0:T(4,128)(2,1)}), bf16[128,4,512]{2,1,0:T(4,128)(2,1)S(1)}, u32[]{:S(2)}, u32[]{:S(2)}) async-start(bf16[128,4,512]{2,1,0:T(4,128)(2,1)} %broadcast_in_dim.130), calls=%async_computation.2 | async-start | bytes 1048576 | tf_op jit(solution)/shard_map/all_to_all | solution.py:79
  278.4 1.2 copy.34
  279.6 16.6 %all-to-all-done.2 = bf16[128,4,512]{2,1,0:T(4,128)(2,1)S(1)} async-done(((bf16[128,4,512]{2,1,0:T(4,128)(2,1)}), bf16[128,4,512]{2,1,0:T(4,128)(2,1)S(1)}, u32[]{:S(2)}, u32[]{:S(2)}) %all-to-all-start.2) | async-done | bytes 524320 | tf_op jit(solution)/shard_map/all_to_all | solution.py:79
  296.2 0.1 fusion.41
  296.4 1.0 squeeze.44
  297.3 1.0 squeeze.45
  (15 shorter events, 0.2 us)
Async XLA Ops:
  14.6 16.0 %copy-start = (bf16[1536,256]{1,0:T(8,128)(2,1)S(1)}, bf16[1536,256]{1,0:T(8,128)(2,1)}, u32[]{:S(2)}) copy-start(bf16[1536,256]{1,0:T(8,128)(2,1)} %param.8) | copy-start | bytes 2359300
  14.6 16.1 %copy-start.2 = (bf16[256,512]{1,0:T(8,128)(2,1)S(1)}, bf16[256,512]{1,0:T(8,128)(2,1)}, u32[]{:S(2)}) copy-start(bf16[256,512]{1,0:T(8,128)(2,1)} %param.10) | copy-start | bytes 786436
  14.6 16.2 %copy-start.3 = (bf16[256,512]{1,0:T(8,128)(2,1)S(1)}, bf16[256,512]{1,0:T(8,128)(2,1)}, u32[]{:S(2)}) copy-start(bf16[256,512]{1,0:T(8,128)(2,1)} %param.11) | copy-start | bytes 786436
  14.6 111.9 %all-to-all-start = ((bf16[128,64,256]{2,1,0:T(8,128)(2,1)}), bf16[128,64,256]{2,1,0:T(8,128)(2,1)}, u32[]{:S(2)}, u32[]{:S(2)}) async-start(bf16[128,64,256]{2,1,0:T(8,128)(2,1)} %bitcast.49), calls=%async_computation | async-start | bytes 8388608 | tf_op jit(solution)/shard_map/all_to_all | solution.py:45
  30.5 1.8 copy-start.5
  30.6 1.8 copy-start.4
  30.6 199.8 %collective-permute-start.1 = (bf16[1536,256]{1,0:T(8,128)(2,1)S(1)}, bf16[1536,256]{1,0:T(8,128)(2,1)}, u32[]{:S(2)}, u32[]{:S(2)}) collective-permute-start(bf16[1536,256]{1,0:T(8,128)(2,1)S(1)} %copy-done), channel_id=1, source_target_pairs={{0,1},{1,0},{2,3},{3,2},{4,5},{5,4},{6,7},{7,6},{8,9},{9,8},{10,11... | collective-permute-start | bytes 2359304 | tf_op jit(solution)/shard_map/ppermute | solution.py:24
  31.9 198.5 %collective-permute-start = (bf16[2,256,256]{2,1,0:T(8,128)(2,1)}, bf16[2,256,256]{2,1,0:T(8,128)(2,1)}, u32[]{:S(2)}, u32[]{:S(2)}) collective-permute-start(bf16[2,256,256]{2,1,0:T(8,128)(2,1)} %bitcast.3), channel_id=1, source_target_pairs={{0,1},{1,0},{2,3},{3,2},{4,5},{5,4},{6,7},{7,6},{8,9},{9,8},{10,11... | collective-permute-start | bytes 786440 | tf_op jit(solution)/shard_map/ppermute | solution.py:24
  227.5 4.9 %collective-permute-start.2 = (bf16[1536,256]{1,0:T(8,128)(2,1)S(1)}, bf16[1536,256]{1,0:T(8,128)(2,1)}, u32[]{:S(2)}, u32[]{:S(2)}) collective-permute-start(bf16[1536,256]{1,0:T(8,128)(2,1)S(1)} %divide_convert_fusion), channel_id=1, source_target_pairs={{0,1},{1,0},{2,3},{3,2},{4,5},{5,4},{6,7},{7,6},{8,9},{9,8},{10,11... | collective-permute-start | bytes 2359304 | tf_op jit(solution)/shard_map/ppermute | solution.py:24
  232.0 1.1 copy-start.1
  238.8 1.7 collective-permute-start.3
  269.6 26.6 %all-to-all-start.2 = ((bf16[128,4,512]{2,1,0:T(4,128)(2,1)}), bf16[128,4,512]{2,1,0:T(4,128)(2,1)S(1)}, u32[]{:S(2)}, u32[]{:S(2)}) async-start(bf16[128,4,512]{2,1,0:T(4,128)(2,1)} %broadcast_in_dim.130), calls=%async_computation.2 | async-start | bytes 1048576 | tf_op jit(solution)/shard_map/all_to_all | solution.py:79

commit v2 on v1

--- a/solution.py
+++ b/solution.py
@@ -1,8 +1,11 @@
+import functools
 import math
 
 import jax
 import jax.numpy as jnp
 from jax import lax
+from jax.experimental import pallas as pl
+from jax.experimental.pallas import tpu as pltpu
 from jax.sharding import PartitionSpec as P
 
 SWAP = [(0, 1), (1, 0)]
@@ -12,12 +15,83 @@
     return jax.nn.gelu(value, approximate=True)
 
 
-def aggregate(lookup, slots, live):
-    total = jnp.zeros((slots.shape[0], lookup.shape[1]), jnp.float32)
-    for slot in range(slots.shape[1]):
-        picked = lookup[slots[:, slot]].astype(jnp.float32)
-        total = total + jnp.where((slot < live)[:, None], picked, 0.0)
-    return (total / live[:, None].astype(jnp.float32)).astype(jnp.bfloat16)
+def incidence_kernel(widths, slots_ref, counts_ref, *rest):
+    outs, (col_ref, mult_ref) = rest[:len(widths)], rest[len(widths):]
+    deg, rows = slots_ref.shape
+    live = lax.broadcasted_iota(jnp.int32, (deg, rows), 0) < counts_ref[...]
+    slots = jnp.where(live, slots_ref[...], -1)
+    mult = jnp.zeros((deg, rows), jnp.float32)
+    for k in range(deg):
+        mult = mult + jnp.where(slots == slots[k:k + 1, :], 1.0, 0.0)
+    col_ref[...] = slots.astype(jnp.float32).T
+    mult_ref[...] = mult.T
+
+    def tile(r, _):
+        r16 = pl.multiple_of(r * 16, 16)
+        cols = col_ref[pl.ds(r16, 16), :]
+        mults = mult_ref[pl.ds(r16, 16), :]
+        want = [jnp.broadcast_to(cols[:, k:k + 1], (16, 128)).astype(jnp.int32).astype(jnp.int16) for k in range(deg)]
+        vals = [jnp.broadcast_to(mults[:, k:k + 1], (16, 128)).astype(jnp.bfloat16) for k in range(deg)]
+        lane = lax.broadcasted_iota(jnp.int32, (16, 128), 1).astype(jnp.int16)
+        base = 0
+        for out, width in zip(outs, widths):
+            for t in range(width // 128):
+                here = lane + jnp.int16(base + t * 128)
+                acc = jnp.zeros((16, 128), jnp.bfloat16)
+                for k in range(deg):
+                    acc = jnp.where(want[k] == here, vals[k], acc)
+                out[pl.ds(r16, 16), t * 128:(t + 1) * 128] = acc
+            base += width
+        return 0
+    lax.fori_loop(0, rows // 16, tile, 0)
+
+def incidence(slots_t, counts, widths, block=128):
+    deg, nodes = slots_t.shape
+    total = sum(widths)
+    return pl.pallas_call(
+        functools.partial(incidence_kernel, widths),
+        grid=(nodes // block,),
+        in_specs=[pl.BlockSpec((deg, block), lambda i: (0, i)), pl.BlockSpec((1, block), lambda i: (0, i))],
+        out_specs=[pl.BlockSpec((block, w), lambda i: (i, 0)) for w in widths],
+        out_shape=[jax.ShapeDtypeStruct((nodes, w), jnp.bfloat16) for w in widths],
+        scratch_shapes=[pltpu.VMEM((block, deg), jnp.float32)] * 2,
+        cost_estimate=pl.CostEstimate(flops=2 * nodes * total * deg, bytes_accessed=2 * nodes * total, transcendentals=0),
+        compiler_params=pltpu.CompilerParams(vmem_limit_bytes=40 << 20),
+        name="incidence",
+    )(slots_t, counts.reshape(1, nodes))
+
+
+def mean_kernel(table_ref, weight_ref, start_ref, counts_ref, out_ref):
+    rows = out_ref.shape[0]
+    live = jnp.broadcast_to(counts_ref[...].astype(jnp.float32), (8, rows)).T[:, :1]
+    total = start_ref[...] + jnp.dot(
+        weight_ref[...], table_ref[...], preferred_element_type=jnp.float32
+    )
+    out_ref[...] = (total / live).astype(jnp.bfloat16)
+
+
+def finish_mean(table, weight, start, counts, block=256):
+    nodes, depth = weight.shape
+    width = table.shape[1]
+    return pl.pallas_call(
+        mean_kernel,
+        grid=(nodes // block,),
+        in_specs=[
+            pl.BlockSpec((depth, width), lambda i: (0, 0), pipeline_mode=pl.Buffered(1)),
+            pl.BlockSpec((block, depth), lambda i: (i, 0)),
+            pl.BlockSpec((block, width), lambda i: (i, 0)),
+            pl.BlockSpec((1, block), lambda i: (0, i)),
+        ],
+        out_specs=pl.BlockSpec((block, width), lambda i: (i, 0)),
+        out_shape=jax.ShapeDtypeStruct((nodes, width), jnp.bfloat16),
+        cost_estimate=pl.CostEstimate(
+            flops=2 * nodes * depth * width,
+            bytes_accessed=2 * (nodes * depth + depth * width + 3 * nodes * width),
+            transcendentals=0,
+        ),
+        compiler_params=pltpu.CompilerParams(vmem_limit_bytes=32 << 20),
+        name="finish_mean",
+    )(table, weight, start, counts.reshape(1, nodes))
 
 
 def swap(value):
@@ -48,14 +122,16 @@
 
     hubs = hub_rows.shape[0]
     width = blk + hubs
-    slot = neighbours - nodes
+    named = neighbours.T
+    slot = named - nodes
     is_hub = slot < parts * hubs
-    local = jnp.where(is_hub, slot, slot - parts * hubs)
-    owner = jnp.where(is_hub, local // hubs, local // blk)
-    within = jnp.where(is_hub, local % hubs + blk, local % blk)
-    place = jnp.where(slot < 0, neighbours, nodes + owner * width + within)
-    lookup = jnp.concatenate([features, incoming.reshape(-1, half)], 0)
-    neigh_mean = aggregate(lookup, place, counts)
+    far = jnp.where(is_hub, slot, slot - parts * hubs)
+    owner = jnp.where(is_hub, far // hubs, far // blk)
+    within = jnp.where(is_hub, far % hubs + blk, far % blk)
+    place = jnp.where(slot < 0, named, nodes + owner * width + within)
+    near_weight, far_weight = incidence(place, counts, (nodes, parts * width))
+    near_sum = dot(near_weight, features)
+    neigh_mean = finish_mean(incoming.reshape(-1, half), far_weight, near_sum, counts)
     mean_other = swap(neigh_mean)
 
     pre = own_dot + dot(neigh_mean, w_mine[1]) + dot(mean_other, w_other[1])

time: 301 us -> 213 us (0.71)
  local copies, waits for them, and re-layouts: 98.7 us -> 9.55 us
  Pallas kernels: 0 us -> 59.7 us
  waiting for transfers between devices: 111 us -> 63.2 us
  other arithmetic: 13.5 us -> 1.35 us
    gather x12 -> x0, local copies, waits for them, and re-layouts: 89.2 us -> none  [aggregate(): picked = lookup[slots[:, slot]].astype(jnp.float32)]
    pallas_call x0 -> x2, Pallas kernels: none -> 59.7 us  [the longest x1 46.3 us: incidence(): pl.pallas_call(functools.partial(incidence_kernel, widths), grid=(nodes /...]
    all_to_all x1, waiting for transfers between devices: 93.6 us -> 46.2 us  [shards(): lax.all_to_all(outgoing, 'dom', split_axis=0, concat_axis=0, tiled=True)]
    convert_element_type x2 -> x0, other arithmetic: 6.08 us -> none  [aggregate(): return (total / live[:, None].astype(jnp.float32)).astype(jnp.bfloat16)]
    concatenate x1 -> x0, other arithmetic: 5.75 us -> none  [shards(): lookup = jnp.concatenate([features, incoming.reshape(-1, half)], 0)]
    dot_general x5 -> x6, matrix products: 17.3 us -> 18.8 us  [dot(): return jnp.dot(left, right, preferred_element_type=jnp.float32)]
  transfers between devices with their start and end apart: 6 -> 6, of which waited for: 3 -> 3; matrix products, arithmetic and copies ran while one was open for 37% -> 4% of each run, Pallas kernels for 0% -> 28%
where the time goes in v2:
time: 213 us; the launch traced here: 211 us
  waiting for transfers between devices  63.2 us (30%)
  Pallas kernels  59.7 us (28%)
  blocking collectives  27.4 us (13%)
  starting transfers between devices  26.2 us (12%)
  matrix products  22.5 us (11%)
  local copies, waits for them, and re-layouts  9.55 us (4%)
    pallas_call x1, Pallas kernels, incidence(): pl.pallas_call(functools.partial(incidence_kernel, widths), grid=(nodes /...  46.3 us
    all_to_all x1, waiting for transfers between devices, shards(): lax.all_to_all(outgoing, 'dom', split_axis=0, concat_axis=0, tiled=True)  46.2 us
    all_to_all x1, blocking collectives, shards(): lax.all_to_all(partial, 'dom', split_axis=0, concat_axis=0, tiled=True)  27.4 us
    dot_general x6, matrix products, dot(): return jnp.dot(left, right, preferred_element_type=jnp.float32)  18.8 us
    all_to_all x1, waiting for transfers between devices, shards(): lax.all_to_all(jnp.broadcast_to(piece[None], (parts,) + piece.shape), 'do...  16.6 us
    all_to_all x1, starting transfers between devices, shards(): lax.all_to_all(outgoing, 'dom', split_axis=0, concat_axis=0, tiled=True)  15.9 us
    pallas_call x1, Pallas kernels, finish_mean(): pl.pallas_call(mean_kernel, grid=(nodes // block,), in_specs=[pl.BlockSpe...  13.3 us
    all_to_all x1, starting transfers between devices, shards(): lax.all_to_all(jnp.broadcast_to(piece[None], (parts,) + piece.shape), 'do...  8.79 us
  transfers between devices with their start and end apart: 6, of which 3 were waited for; matrix products, arithmetic and copies ran while one was open for 4% of the time, Pallas kernels for 28%

profile of v2, /device:TPU:8, one launch (start us, length us, event | category | flops | bytes accessed | tf_op | source)
XLA Modules:
  0.0 210.8 jit_solution(10241655713647446810)
XLA Ops:
  0.6 0.7 pad.7.clone
  1.4 0.8 pad_add_fusion
  2.1 0.1 copy.27
  2.2 0.1 eq.22
  2.3 12.3 %fusion.2 = bf16[8192,256]{1,0:T(8,128)(2,1)} fusion(bf16[1536,256]{1,0:T(8,128)(2,1)} %param.8, s32[8192]{0:T(1024)S(1)} %eq.22), kind=kOutput, calls=%fused_computation.3 | convolution fusion | flops 6457131008 | bytes 5013504 | tf_op jit(solution)/shard_map/dot_general | solution.py:102
  14.6 0.0 copy-start
  14.6 0.0 copy-start.2
  14.6 0.0 copy-start.3
  14.6 15.9 %all-to-all-start = ((bf16[128,64,256]{2,1,0:T(8,128)(2,1)}), bf16[128,64,256]{2,1,0:T(8,128)(2,1)}, u32[]{:S(2)}, u32[]{:S(2)}) async-start(bf16[128,64,256]{2,1,0:T(8,128)(2,1)} %bitcast.67), calls=%async_computation | async-start | bytes 8388608 | tf_op jit(solution)/shard_map/all_to_all | solution.py:119
  30.5 0.0 copy-done
  30.6 0.0 copy-start.5
  30.6 0.0 copy-start.4
  30.6 0.1 collective-permute-start.1
  30.7 0.0 copy-done.2
  30.7 0.1 copy.23
  30.8 0.0 copy-done.3
  30.8 0.1 copy.24
  31.0 0.1 fusion.18
  31.1 0.8 copy.26
  31.9 0.5 collective-permute-start
  32.4 0.0 copy-done.5
  32.4 0.0 copy-done.4
  32.4 0.1 fusion.24.slots_ref
  32.5 46.3 %incidence.1 = (bf16[1536,1536]{1,0:T(8,128)(2,1)S(1)}, bf16[1536,8192]{1,0:T(8,128)(2,1)}) custom-call(s32[12,1536]{1,0:T(8,128)S(1)} %fusion.24.slots_ref, s32[1,1536]{1,0:T(1,128)S(1)} %reshape.42.counts_ref), custom_call_target="tpu_custom_call" | custom-call | flops 358612992 | bytes 29884416 | tf_op jit(solution)/shard_map/incidence/pallas_call | solution.py:51
  78.9 1.4 fusion.31.start_ref
  80.3 46.2 %all-to-all-done = bf16[128,64,256]{2,1,0:T(8,128)(2,1)} async-done(((bf16[128,64,256]{2,1,0:T(8,128)(2,1)}), bf16[128,64,256]{2,1,0:T(8,128)(2,1)}, u32[]{:S(2)}, u32[]{:S(2)}) %all-to-all-start) | async-done | bytes 4194336 | tf_op jit(solution)/shard_map/all_to_all | solution.py:119
  126.5 13.3 %finish_mean.1 = bf16[1536,256]{1,0:T(8,128)(2,1)S(1)} custom-call(bf16[8192,256]{1,0:T(8,128)(2,1)} %bitcast.8.table_ref, bf16[1536,8192]{1,0:T(8,128)(2,1)} %get-tuple-element.5.weight_ref, f32[1536,256]{1,0:T(8,128)S(1)} %fusion.31.start_ref, s32[1,1536]{1,0:T(1,128)S(1)} %reshape.42.counts_ref), custom_call_target="tpu_custom_call" | custom-call | flops 6442450944 | bytes 31719424 | tf_op jit(solution)/shard_map/finish_mean/pallas_call | solution.py:76
  139.8 0.3 collective-permute-start.2
  140.1 0.4 fusion.20
  140.5 2.3 %copy.31 = bf16[1536,256]{0,1:T(8,128)(2,1)} copy(bf16[1536,256]{1,0:T(8,128)(2,1)} %param.9) | data formatting | bytes 1572864 | tf_op args[1]
  142.8 0.0 collective-permute-done
  142.8 0.0 collective-permute-done.1
  142.8 1.6 fusion.3
  144.4 0.0 copy-start.1
  144.4 0.4 convolution_add_fusion.1
  144.8 0.0 collective-permute-done.2
  144.9 0.7 copy-done.1
  145.6 2.7 %fusion.6 = (bf16[1536,256]{0,1:T(8,128)(2,1)S(1)}, bf16[1536,256]{0,1:T(8,128)(2,1)S(1)}) fusion(bf16[1536,256]{0,1:T(8,128)(2,1)S(1)} %copy-done.1, f32[1536,256]{0,1:T(8,128)S(1)} %convolution_add_fusion.1, bf16[1536,256]{1,0:T(8,128)(2,1)} %collective-permute-done.2, bf16[2,256,256]{2,1,0:T(8,128)(2,1)} %collective-permute-done), kind=kOutput, calls=%fused_computation.14 | convolution fusion | flops 210763776 | bytes 4849664 | tf_op jit(solution)/shard_map/dot_general | solution.py:102
  148.2 1.5 fusion.15
  149.7 1.5 fusion.17
  151.3 0.6 collective-permute-start.3
  151.8 0.4 fusion.16
  152.2 0.4 fusion.14
  152.6 0.4 collective-permute-done.3
  153.1 0.2 copy.33
  153.3 0.1 reshape.43
  153.4 27.4 %all_to_all.15 = bf16[128,4,512]{2,1,0:T(4,128)(2,1)S(1)} all-to-all(bf16[128,4,512]{2,1,0:T(4,128)(2,1)S(1)} %reshape.43), channel_id=1, replica_groups=mesh['dom'=128,'col'=2] {'dom'}, dimensions={0} | all-to-all | bytes 1048576 | tf_op jit(solution)/shard_map/all_to_all | solution.py:152
  180.8 0.3 convert_reduce_fusion
  181.1 0.9 broadcast_in_dim.5
  182.1 8.8 %all-to-all-start.2 = ((bf16[128,4,512]{2,1,0:T(4,128)(2,1)}), bf16[128,4,512]{2,1,0:T(4,128)(2,1)S(1)}, u32[]{:S(2)}, u32[]{:S(2)}) async-start(bf16[128,4,512]{2,1,0:T(4,128)(2,1)} %broadcast_in_dim.5), calls=%async_computation.2 | async-start | bytes 1048576 | tf_op jit(solution)/shard_map/all_to_all | solution.py:155
  190.9 1.2 copy.34
  192.0 16.6 %all-to-all-done.2 = bf16[128,4,512]{2,1,0:T(4,128)(2,1)S(1)} async-done(((bf16[128,4,512]{2,1,0:T(4,128)(2,1)}), bf16[128,4,512]{2,1,0:T(4,128)(2,1)S(1)}, u32[]{:S(2)}, u32[]{:S(2)}) %all-to-all-start.2) | async-done | bytes 524320 | tf_op jit(solution)/shard_map/all_to_all | solution.py:155
  208.6 0.1 fusion.30
  208.8 1.0 squeeze.32
  209.8 1.0 squeeze.33
  (5 shorter events, 0.1 us)
Async XLA Ops:
  14.6 16.0 %copy-start = (bf16[1536,256]{1,0:T(8,128)(2,1)S(1)}, bf16[1536,256]{1,0:T(8,128)(2,1)}, u32[]{:S(2)}) copy-start(bf16[1536,256]{1,0:T(8,128)(2,1)} %param.8) | copy-start | bytes 2359300
  14.6 16.1 %copy-start.2 = (bf16[256,512]{1,0:T(8,128)(2,1)S(1)}, bf16[256,512]{1,0:T(8,128)(2,1)}, u32[]{:S(2)}) copy-start(bf16[256,512]{1,0:T(8,128)(2,1)} %param.10) | copy-start | bytes 786436
  14.6 16.2 %copy-start.3 = (bf16[256,512]{1,0:T(8,128)(2,1)S(1)}, bf16[256,512]{1,0:T(8,128)(2,1)}, u32[]{:S(2)}) copy-start(bf16[256,512]{1,0:T(8,128)(2,1)} %param.11) | copy-start | bytes 786436
  14.6 111.9 %all-to-all-start = ((bf16[128,64,256]{2,1,0:T(8,128)(2,1)}), bf16[128,64,256]{2,1,0:T(8,128)(2,1)}, u32[]{:S(2)}, u32[]{:S(2)}) async-start(bf16[128,64,256]{2,1,0:T(8,128)(2,1)} %bitcast.67), calls=%async_computation | async-start | bytes 8388608 | tf_op jit(solution)/shard_map/all_to_all | solution.py:119
  30.6 1.8 copy-start.5
  30.6 1.8 copy-start.4
  30.6 112.2 %collective-permute-start.1 = (bf16[1536,256]{1,0:T(8,128)(2,1)S(1)}, bf16[1536,256]{1,0:T(8,128)(2,1)}, u32[]{:S(2)}, u32[]{:S(2)}) collective-permute-start(bf16[1536,256]{1,0:T(8,128)(2,1)S(1)} %copy-done), channel_id=1, source_target_pairs={{0,1},{1,0},{2,3},{3,2},{4,5},{5,4},{6,7},{7,6},{8,9},{9,8},{10,11... | collective-permute-start | bytes 2359304 | tf_op jit(solution)/shard_map/ppermute | solution.py:98
  31.9 110.9 %collective-permute-start = (bf16[2,256,256]{2,1,0:T(8,128)(2,1)}, bf16[2,256,256]{2,1,0:T(8,128)(2,1)}, u32[]{:S(2)}, u32[]{:S(2)}) collective-permute-start(bf16[2,256,256]{2,1,0:T(8,128)(2,1)} %bitcast.3), channel_id=1, source_target_pairs={{0,1},{1,0},{2,3},{3,2},{4,5},{5,4},{6,7},{7,6},{8,9},{9,8},{10,11... | collective-permute-start | bytes 786440 | tf_op jit(solution)/shard_map/ppermute | solution.py:98
  139.8 5.0 %collective-permute-start.2 = (bf16[1536,256]{1,0:T(8,128)(2,1)S(1)}, bf16[1536,256]{1,0:T(8,128)(2,1)}, u32[]{:S(2)}, u32[]{:S(2)}) collective-permute-start(bf16[1536,256]{1,0:T(8,128)(2,1)S(1)} %finish_mean.1), channel_id=1, source_target_pairs={{0,1},{1,0},{2,3},{3,2},{4,5},{5,4},{6,7},{7,6},{8,9},{9,8},{10,11... | collective-permute-start | bytes 2359304 | tf_op jit(solution)/shard_map/ppermute | solution.py:98
  144.4 1.1 copy-start.1
  151.3 1.7 collective-permute-start.3
  182.1 26.6 %all-to-all-start.2 = ((bf16[128,4,512]{2,1,0:T(4,128)(2,1)}), bf16[128,4,512]{2,1,0:T(4,128)(2,1)S(1)}, u32[]{:S(2)}, u32[]{:S(2)}) async-start(bf16[128,4,512]{2,1,0:T(4,128)(2,1)} %broadcast_in_dim.5), calls=%async_computation.2 | async-start | bytes 1048576 | tf_op jit(solution)/shard_map/all_to_all | solution.py:155

commit v3 on v2

--- a/solution.py
+++ b/solution.py
@@ -9,56 +9,56 @@
 from jax.sharding import PartitionSpec as P
 
 SWAP = [(0, 1), (1, 0)]
+LINES = {"x": (32, 4), "y": (8, 4), "z": (1, 8)}
+GROUP = 16
+SPAN = 256
 
 
 def activation(value):
     return jax.nn.gelu(value, approximate=True)
 
 
-def incidence_kernel(widths, slots_ref, counts_ref, *rest):
-    outs, (col_ref, mult_ref) = rest[:len(widths)], rest[len(widths):]
-    deg, rows = slots_ref.shape
-    live = lax.broadcasted_iota(jnp.int32, (deg, rows), 0) < counts_ref[...]
-    slots = jnp.where(live, slots_ref[...], -1)
-    mult = jnp.zeros((deg, rows), jnp.float32)
-    for k in range(deg):
-        mult = mult + jnp.where(slots == slots[k:k + 1, :], 1.0, 0.0)
-    col_ref[...] = slots.astype(jnp.float32).T
-    mult_ref[...] = mult.T
-
-    def tile(r, _):
-        r16 = pl.multiple_of(r * 16, 16)
-        cols = col_ref[pl.ds(r16, 16), :]
-        mults = mult_ref[pl.ds(r16, 16), :]
-        want = [jnp.broadcast_to(cols[:, k:k + 1], (16, 128)).astype(jnp.int32).astype(jnp.int16) for k in range(deg)]
-        vals = [jnp.broadcast_to(mults[:, k:k + 1], (16, 128)).astype(jnp.bfloat16) for k in range(deg)]
-        lane = lax.broadcasted_iota(jnp.int32, (16, 128), 1).astype(jnp.int16)
-        base = 0
-        for out, width in zip(outs, widths):
-            for t in range(width // 128):
-                here = lane + jnp.int16(base + t * 128)
-                acc = jnp.zeros((16, 128), jnp.bfloat16)
-                for k in range(deg):
-                    acc = jnp.where(want[k] == here, vals[k], acc)
-                out[pl.ds(r16, 16), t * 128:(t + 1) * 128] = acc
-            base += width
-        return 0
-    lax.fori_loop(0, rows // 16, tile, 0)
-
-def incidence(slots_t, counts, widths, block=128):
+def incidence_kernel(slots_ref, *outs):
+    slots = slots_ref[...]
+    low = (slots & (SPAN - 1)).astype(jnp.float32).T
+    high = slots >> 8
+    lane = lax.broadcasted_iota(jnp.int32, (SPAN, SPAN), 1).astype(jnp.float32)
+    owner = lax.broadcasted_iota(jnp.int32, (GROUP, SPAN), 1) & (GROUP - 1)
+    own = owner == lax.broadcasted_iota(jnp.int32, (GROUP, SPAN), 0)
+    one = jnp.ones((GROUP, SPAN), jnp.bfloat16)
+    zero = jnp.zeros((GROUP, SPAN), jnp.bfloat16)
+    for g in range(slots.shape[0]):
+        right = jnp.where(low[:, g:g + 1] == lane, 1.0, 0.0).astype(jnp.bfloat16)
+        mine = jnp.where(own, jnp.broadcast_to(high[g:g + 1, :], (GROUP, SPAN)), -1).astype(jnp.int16)
+        first = 0
+        for out in outs:
+            tiles = out.shape[1] // SPAN
+            left = jnp.concatenate([jnp.where(mine == jnp.int16(first + t), one, zero) for t in range(tiles)], 0)
+            made = jnp.dot(left, right, preferred_element_type=jnp.float32).astype(jnp.bfloat16)
+            for t in range(tiles):
+                out[g * GROUP:(g + 1) * GROUP, t * SPAN:(t + 1) * SPAN] = made[t * GROUP:(t + 1) * GROUP]
+            first += tiles
+
+def incidence(slots_t, counts, widths, batch=8):
     deg, nodes = slots_t.shape
+    groups = nodes // GROUP
+    depth = SPAN // GROUP
+    step = lax.broadcasted_iota(jnp.int32, (depth, nodes), 0)
+    slots = jnp.pad(slots_t, ((0, depth - deg), (0, 0)), constant_values=-1)
+    slots = jnp.where(step < counts[None, :], slots, -1)
+    slots = slots.reshape(depth, groups, GROUP).transpose(1, 0, 2).reshape(groups, SPAN)
     total = sum(widths)
+    block = batch * GROUP
     return pl.pallas_call(
-        functools.partial(incidence_kernel, widths),
-        grid=(nodes // block,),
-        in_specs=[pl.BlockSpec((deg, block), lambda i: (0, i)), pl.BlockSpec((1, block), lambda i: (0, i))],
+        incidence_kernel,
+        grid=(groups // batch,),
+        in_specs=[pl.BlockSpec((batch, SPAN), lambda i: (i, 0))],
         out_specs=[pl.BlockSpec((block, w), lambda i: (i, 0)) for w in widths],
         out_shape=[jax.ShapeDtypeStruct((nodes, w), jnp.bfloat16) for w in widths],
-        scratch_shapes=[pltpu.VMEM((block, deg), jnp.float32)] * 2,
-        cost_estimate=pl.CostEstimate(flops=2 * nodes * total * deg, bytes_accessed=2 * nodes * total, transcendentals=0),
-        compiler_params=pltpu.CompilerParams(vmem_limit_bytes=40 << 20),
+        cost_estimate=pl.CostEstimate(flops=2 * nodes * total * SPAN, bytes_accessed=2 * nodes * total, transcendentals=0),
+        compiler_params=pltpu.CompilerParams(vmem_limit_bytes=24 << 20),
         name="incidence",
-    )(slots_t, counts.reshape(1, nodes))
+    )(slots)
 
 
 def mean_kernel(table_ref, weight_ref, start_ref, counts_ref, out_ref):
@@ -98,6 +98,38 @@
     return lax.ppermute(value, "col", SWAP)
 
 
+def shift(value, axis, offset):
+    stride, size = LINES[axis]
+    pairs = []
+    for source in range(128):
+        here = source // stride % size
+        pairs.append((source, source + ((here + offset) % size - here) * stride))
+    return lax.ppermute(value, "dom", pairs)
+
+
+def gather_hubs(block, slots, nodes):
+    stride, size = LINES["z"]
+    lines = [list(range(first, first + size)) for first in range(0, 128, size)]
+    copies = jnp.broadcast_to(block[None], (size,) + block.shape)
+    line = lax.all_to_all(
+        copies, "dom", split_axis=0, concat_axis=0, tiled=True, axis_index_groups=lines
+    ).reshape(-1, block.shape[1])
+    plane = jnp.concatenate([line] + [shift(line, "y", -ahead) for ahead in (1, 2, 3)], 0)
+    middle = plane.shape[0] // 2
+    after, before = shift(plane, "x", -1), shift(plane, "x", 1)
+    table = jnp.concatenate(
+        [plane, after, shift(after[:middle], "x", -1), shift(before[middle:], "x", 1), before], 0
+    )
+    here = lax.axis_index("dom")
+    hub = slots - nodes
+    owner = hub >> 5
+    ahead_x = ((owner >> 5) - (here >> 5)) & 3
+    ahead_y = ((owner >> 3) - (here >> 3)) & 3
+    moved = nodes + (ahead_x * 4 + ahead_y) * line.shape[0] + (hub & (line.shape[0] - 1))
+    is_hub = (hub >= 0) & (hub < table.shape[0])
+    return table, jnp.where(is_hub, moved, slots)
+
+
 def dot(left, right):
     return jnp.dot(left, right, preferred_element_type=jnp.float32)
 
@@ -111,26 +143,21 @@
     w_other = swap(lax.dynamic_index_in_dim(weights, 1 - core, 2, keepdims=False))
     features_other = swap(features)
 
-    picks = jnp.concatenate(
-        [send_rows[0], jnp.broadcast_to(hub_rows[None], (parts, hub_rows.shape[0]))], 1
-    ).reshape(-1)
-    onehot = (picks[:, None] == jnp.arange(nodes, dtype=jnp.int32)[None, :]).astype(jnp.bfloat16)
-    outgoing = dot(onehot, features).astype(jnp.bfloat16).reshape(parts, -1, half)
+    lanes = jnp.arange(nodes, dtype=jnp.int32)[None, :]
+
+    def pick(rows):
+        onehot = (rows[:, None] == lanes).astype(jnp.bfloat16)
+        return dot(onehot, features).astype(jnp.bfloat16)
+
+    hub_block, named = gather_hubs(pick(hub_rows), neighbours.T, nodes)
+    outgoing = pick(send_rows.reshape(-1)).reshape(parts, -1, half)
     incoming = lax.all_to_all(outgoing, "dom", split_axis=0, concat_axis=0, tiled=True)
-    blk = send_rows.shape[2]
     own_dot = dot(features, w_mine[0]) + dot(features_other, w_other[0])
 
-    hubs = hub_rows.shape[0]
-    width = blk + hubs
-    named = neighbours.T
-    slot = named - nodes
-    is_hub = slot < parts * hubs
-    far = jnp.where(is_hub, slot, slot - parts * hubs)
-    owner = jnp.where(is_hub, far // hubs, far // blk)
-    within = jnp.where(is_hub, far % hubs + blk, far % blk)
-    place = jnp.where(slot < 0, named, nodes + owner * width + within)
-    near_weight, far_weight = incidence(place, counts, (nodes, parts * width))
-    near_sum = dot(near_weight, features)
+    own_weight, hub_weight, far_weight = incidence(
+        named, counts, (nodes, hub_block.shape[0], incoming.shape[0] * incoming.shape[1])
+    )
+    near_sum = dot(own_weight, features) + dot(hub_weight, hub_block)
     neigh_mean = finish_mean(incoming.reshape(-1, half), far_weight, near_sum, counts)
     mean_other = swap(neigh_mean)
 

time: 213 us -> 183 us (0.86)
  Pallas kernels: 59.7 us -> 17.4 us
  waiting for transfers between devices: 63.2 us -> 41.2 us
  local copies, waits for them, and re-layouts: 9.55 us -> 27.7 us
  starting transfers between devices: 26.2 us -> 42.4 us
    all_to_all x1, waiting for transfers between devices: 46.2 us -> 0.01 us  [shards(): lax.all_to_all(outgoing, 'dom', split_axis=0, concat_axis=0, tiled=True)]
    pallas_call x1, Pallas kernels: 46.3 us -> 13.1 us  [incidence(): pl.pallas_call(incidence_kernel, grid=(groups // batch,), in_specs=[pl.Bl...]
    ppermute x0 -> x7, waiting for transfers between devices: none -> 23.2 us  [shift(): return lax.ppermute(value, 'dom', pairs)]
    unnamed x16 -> x40, local copies, waits for them, and re-layouts: 4.44 us -> 20.1 us
    ppermute x0 -> x7, starting transfers between devices: none -> 11.9 us  [shift(): return lax.ppermute(value, 'dom', pairs)]
    pallas_call x1, Pallas kernels: 13.3 us -> 4.29 us  [finish_mean(): pl.pallas_call(mean_kernel, grid=(nodes // block,), in_specs=[pl.BlockSpe...]
    all_to_all x0 -> x1, starting transfers between devices: none -> 8.6 us  [gather_hubs(): lax.all_to_all(copies, 'dom', split_axis=0, concat_axis=0, tiled=True, ax...]
    all_to_all x1, starting transfers between devices: 15.9 us -> 12.9 us  [shards(): lax.all_to_all(outgoing, 'dom', split_axis=0, concat_axis=0, tiled=True)]
  transfers between devices with their start and end apart: 6 -> 14, of which waited for: 3 -> 6; matrix products, arithmetic and copies ran while one was open for 4% -> 14% of each run, Pallas kernels for 28% -> 10%
where the time goes in v3:
time: 183 us; the launch traced here: 181 us
  starting transfers between devices  42.4 us (23%)
  waiting for transfers between devices  41.2 us (23%)
  blocking collectives  28.1 us (15%)
  local copies, waits for them, and re-layouts  27.7 us (15%)
  matrix products  22.5 us (12%)
  Pallas kernels  17.4 us (10%)
    all_to_all x1, blocking collectives, shards(): lax.all_to_all(partial, 'dom', split_axis=0, concat_axis=0, tiled=True)  28.1 us
    ppermute x7, waiting for transfers between devices, shift(): return lax.ppermute(value, 'dom', pairs)  23.2 us
    unnamed x40, local copies, waits for them, and re-layouts  20.1 us
    dot_general x8, matrix products, dot(): return jnp.dot(left, right, preferred_element_type=jnp.float32)  18.7 us
    all_to_all x1, waiting for transfers between devices, shards(): lax.all_to_all(jnp.broadcast_to(piece[None], (parts,) + piece.shape), 'do...  16.1 us
    pallas_call x1, Pallas kernels, incidence(): pl.pallas_call(incidence_kernel, grid=(groups // batch,), in_specs=[pl.Bl...  13.1 us
    all_to_all x1, starting transfers between devices, shards(): lax.all_to_all(outgoing, 'dom', split_axis=0, concat_axis=0, tiled=True)  12.9 us
    ppermute x7, starting transfers between devices, shift(): return lax.ppermute(value, 'dom', pairs)  11.9 us
  transfers between devices with their start and end apart: 14, of which 6 were waited for; matrix products, arithmetic and copies ran while one was open for 14% of the time, Pallas kernels for 10%

profile of v3, /device:TPU:8, one launch (start us, length us, event | category | flops | bytes accessed | tf_op | source)
XLA Modules:
  0.0 180.9 jit_solution(16153103109079096262)
XLA Ops:
  0.6 0.1 collective-permute-start.1
  0.7 1.4 convolution_convert_fusion.4
  2.2 0.0 copy-start.13
  2.2 0.7 broadcast_in_dim.11
  2.9 8.6 %all-to-all-start.1 = ((bf16[8,32,256]{2,1,0:T(8,128)(2,1)}), bf16[8,32,256]{2,1,0:T(8,128)(2,1)S(1)}, u32[]{:S(2)}, u32[]{:S(2)}) async-start(bf16[8,32,256]{2,1,0:T(8,128)(2,1)} %broadcast_in_dim.11), calls=%async_computation.1 | async-start | bytes 262144 | tf_op jit(solution)/shard_map/all_to_all | solution.py:114
  11.5 1.1 copy.26
  12.6 0.1 copy.27
  12.7 0.1 fusion.18
  12.8 0.8 copy.29
  13.6 0.2 collective-permute-start
  13.8 0.1 copy.30
  13.9 0.1 eq.32
  14.0 0.0 copy-done.5
  14.0 6.0 %fusion.2 = bf16[4096,256]{1,0:T(8,128)(2,1)} fusion(bf16[1536,256]{1,0:T(8,128)(2,1)S(1)} %copy-done.5, s32[4096]{0:T(1024)S(1)} %eq.32), kind=kOutput, calls=%fused_computation.3 | convolution fusion | flops 3228565504 | bytes 2899968 | tf_op jit(solution)/shard_map/dot_general | solution.py:134
  20.0 1.1 all-to-all-done.1
  21.2 12.9 %all-to-all-start = ((bf16[128,32,256]{2,1,0:T(8,128)(2,1)}), bf16[128,32,256]{2,1,0:T(8,128)(2,1)S(1)}, u32[]{:S(2)}, u32[]{:S(2)}) async-start(bf16[128,32,256]{2,1,0:T(8,128)(2,1)} %bitcast.73), calls=%async_computation | async-start | bytes 4194304 | tf_op jit(solution)/shard_map/all_to_all | solution.py:154
  34.1 0.1 bitcast_select_fusion
  34.2 1.2 reshape.50
  35.3 1.4 copy.31
  36.7 0.1 copy.32.slots_ref
  36.8 1.0 collective-permute-start.2
  37.8 2.0 %collective-permute-start.3 = (bf16[256,256]{1,0:T(8,128)(2,1)S(1)}, bf16[256,256]{1,0:T(8,128)(2,1)S(1)}, u32[]{:S(2)}, u32[]{:S(2)}) collective-permute-start(bf16[256,256]{1,0:T(8,128)(2,1)S(1)} %bitcast.75), channel_id=1, source_target_pairs={{0,32},{2,34},{4,36},{6,38},{8,40},{10,42},{12,44},{14,46},{16,48}... | collective-permute-start | bytes 393224 | tf_op jit(solution)/shard_map/ppermute | solution.py:107
  39.8 1.8 %collective-permute-start.4 = (bf16[256,256]{1,0:T(8,128)(2,1)S(1)}, bf16[256,256]{1,0:T(8,128)(2,1)S(1)}, u32[]{:S(2)}, u32[]{:S(2)}) collective-permute-start(bf16[256,256]{1,0:T(8,128)(2,1)S(1)} %bitcast.76), channel_id=1, source_target_pairs={{0,16},{2,18},{4,20},{6,22},{8,24},{10,26},{12,28},{14,30},{16,32}... | collective-permute-start | bytes 393224 | tf_op jit(solution)/shard_map/ppermute | solution.py:107
  41.6 13.1 %incidence.1 = (bf16[1536,1536]{1,0:T(8,128)(2,1)S(1)}, bf16[1536,4096]{1,0:T(8,128)(2,1)S(1)}, bf16[1536,4096]{1,0:T(8,128)(2,1)S(1)}) custom-call(s32[96,256]{1,0:T(8,128)S(1)} %copy.32.slots_ref), custom_call_target="tpu_custom_call" | custom-call | flops 7650410496 | bytes 29884416 | tf_op jit(solution)/shard_map/incidence/pallas_call | solution.py:52
  54.7 4.5 %copy-done = bf16[1536,4096]{1,0:T(8,128)(2,1)} copy-done((bf16[1536,4096]{1,0:T(8,128)(2,1)}, bf16[1536,4096]{1,0:T(8,128)(2,1)S(1)}, u32[]{:S(2)}) %copy-start) | copy-done | bytes 12582936
  59.2 4.5 %copy-done.3 = bf16[1536,4096]{1,0:T(8,128)(2,1)} copy-done((bf16[1536,4096]{1,0:T(8,128)(2,1)}, bf16[1536,4096]{1,0:T(8,128)(2,1)S(1)}, u32[]{:S(2)}) %copy-start.3) | copy-done | bytes 12582936
  63.8 3.4 %collective-permute-start.5 = (bf16[1024,256]{1,0:T(8,128)(2,1)S(1)}, bf16[1024,256]{1,0:T(8,128)(2,1)S(1)}, u32[]{:S(2)}, u32[]{:S(2)}) collective-permute-start(bf16[1024,256]{1,0:T(8,128)(2,1)S(1)} %pad_maximum_fusion), channel_id=1, source_target_pairs={{0,192},{2,194},{4,196},{6,198},{8,200},{10,202},{12,204},{14,206}... | collective-permute-start | bytes 1572872 | tf_op jit(solution)/shard_map/ppermute | solution.py:107
  67.2 1.4 fusion.26
  68.7 15.2 %collective-permute-done.5 = bf16[1024,256]{1,0:T(8,128)(2,1)S(1)} collective-permute-done((bf16[1024,256]{1,0:T(8,128)(2,1)S(1)}, bf16[1024,256]{1,0:T(8,128)(2,1)S(1)}, u32[]{:S(2)}, u32[]{:S(2)}) %collective-permute-start.5) | collective-permute-done | bytes 524320 | tf_op jit(solution)/shard_map/ppermute | solution.py:107
  83.9 3.6 %collective-permute-start.6 = (bf16[512,256]{1,0:T(8,128)(2,1)S(1)}, bf16[512,256]{1,0:T(8,128)(2,1)S(1)}, u32[]{:S(2)}, u32[]{:S(2)}) collective-permute-start(bf16[512,256]{1,0:T(8,128)(2,1)S(1)} %slice.38), channel_id=1, source_target_pairs={{0,192},{2,194},{4,196},{6,198},{8,200},{10,202},{12,204},{14,206}... | collective-permute-start | bytes 786440 | tf_op jit(solution)/shard_map/ppermute | solution.py:107
  87.5 0.1 collective-permute-start.8
  87.7 4.4 %collective-permute-done.6 = bf16[512,256]{1,0:T(8,128)(2,1)S(1)} collective-permute-done((bf16[512,256]{1,0:T(8,128)(2,1)S(1)}, bf16[512,256]{1,0:T(8,128)(2,1)S(1)}, u32[]{:S(2)}, u32[]{:S(2)}) %collective-permute-start.6) | collective-permute-done | bytes 262176 | tf_op jit(solution)/shard_map/ppermute | solution.py:107
  92.1 3.7 %collective-permute-done.8 = bf16[512,256]{1,0:T(8,128)(2,1)S(1)} collective-permute-done((bf16[512,256]{1,0:T(8,128)(2,1)S(1)}, bf16[512,256]{1,0:T(8,128)(2,1)S(1)}, u32[]{:S(2)}, u32[]{:S(2)}) %collective-permute-start.8) | collective-permute-done | bytes 262176 | tf_op jit(solution)/shard_map/ppermute | solution.py:107
  95.8 4.8 %convolution_add_fusion.3.start_ref = f32[1536,256]{1,0:T(8,128)} fusion(f32[1536,256]{1,0:T(8,128)S(1)} %fusion.26, bf16[1536,4096]{1,0:T(8,128)(2,1)S(1)} %copy-done.4, bf16[4096,256]{1,0:T(8,128)(2,1)S(1)} %constant_dynamic-update-slice_fusion), kind=kOutput, calls=%fused_computation.8 | convolution fusion | flops 3221618688 | bytes 17825792 | tf_op jit(solution)/shard_map/dot_general | solution.py:134
  100.7 4.6 %copy-done.1 = bf16[1536,4096]{1,0:T(8,128)(2,1)S(1)} copy-done((bf16[1536,4096]{1,0:T(8,128)(2,1)S(1)}, bf16[1536,4096]{1,0:T(8,128)(2,1)}, u32[]{:S(2)}) %copy-start.1) | copy-done | bytes 12582936
  105.2 1.4 copy-done.2
  106.6 4.3 %finish_mean.1 = bf16[1536,256]{1,0:T(8,128)(2,1)S(1)} custom-call(bf16[4096,256]{1,0:T(8,128)(2,1)S(1)} %bitcast.71, bf16[1536,4096]{1,0:T(8,128)(2,1)S(1)} %copy-done.1, f32[1536,256]{1,0:T(8,128)S(1)} %copy-done.2, s32[1,1536]{1,0:T(1,128)S(1)} %broadcast_in_dim.12.counts_ref), custom_call_target="tpu_custom_call" | custom-call | flops 3221225472 | bytes 17039360 | tf_op jit(solution)/shard_map/finish_mean/pallas_call | solution.py:76
  110.9 0.0 copy-start.8
  110.9 0.1 collective-permute-start.9
  111.1 0.4 fusion.20
  111.5 0.6 copy-done.8
  112.1 1.2 copy.36
  113.2 1.6 fusion.3
  114.9 0.0 copy-start.9
  114.9 0.4 convolution_add_fusion.1
  115.3 0.7 copy-done.9
  116.0 2.6 %fusion.6 = (bf16[1536,256]{0,1:T(8,128)(2,1)S(1)}, bf16[1536,256]{0,1:T(8,128)(2,1)S(1)}) fusion(bf16[1536,256]{0,1:T(8,128)(2,1)S(1)} %copy-done.9, f32[1536,256]{0,1:T(8,128)S(1)} %convolution_add_fusion.1, bf16[1536,256]{1,0:T(8,128)(2,1)} %collective-permute-done.9, bf16[2,256,256]{2,1,0:T(8,128)(2,1)} %collective-permute-done), kind=kOutput, calls=%fused_computation.15 | convolution fusion | flops 210763776 | bytes 4849664 | tf_op jit(solution)/shard_map/dot_general | solution.py:134
  118.7 1.5 fusion.15
  120.2 1.6 fusion.17
  121.8 0.1 collective-permute-start.10
  121.9 0.4 fusion.16
  122.3 0.4 fusion.14
  122.7 0.8 collective-permute-done.10
  123.5 0.2 copy.38
  123.7 0.1 reshape.53
  123.9 28.1 %all_to_all.20 = bf16[128,4,512]{2,1,0:T(4,128)(2,1)S(1)} all-to-all(bf16[128,4,512]{2,1,0:T(4,128)(2,1)S(1)} %reshape.53), channel_id=1, replica_groups=mesh['dom'=128,'col'=2] {'dom'}, dimensions={0} | all-to-all | bytes 1048576 | tf_op jit(solution)/shard_map/all_to_all | solution.py:179
  151.9 0.3 convert_reduce_fusion
  152.2 0.9 broadcast_in_dim.24
  153.1 8.5 %all-to-all-start.3 = ((bf16[128,4,512]{2,1,0:T(4,128)(2,1)}), bf16[128,4,512]{2,1,0:T(4,128)(2,1)S(1)}, u32[]{:S(2)}, u32[]{:S(2)}) async-start(bf16[128,4,512]{2,1,0:T(4,128)(2,1)} %broadcast_in_dim.24), calls=%async_computation.3 | async-start | bytes 1048576 | tf_op jit(solution)/shard_map/all_to_all | solution.py:182
  161.6 1.2 copy.39
  162.8 16.1 %all-to-all-done.3 = bf16[128,4,512]{2,1,0:T(4,128)(2,1)S(1)} async-done(((bf16[128,4,512]{2,1,0:T(4,128)(2,1)}), bf16[128,4,512]{2,1,0:T(4,128)(2,1)S(1)}, u32[]{:S(2)}, u32[]{:S(2)}) %all-to-all-start.3) | async-done | bytes 524320 | tf_op jit(solution)/shard_map/all_to_all | solution.py:182
  178.8 0.1 fusion.25
  179.0 1.0 squeeze.28
  179.9 1.0 squeeze.29
  (44 shorter events, 0.4 us)
Async XLA Ops:
  0.6 11.9 %copy-start.10 = (bf16[256,512]{1,0:T(8,128)(2,1)S(1)}, bf16[256,512]{1,0:T(8,128)(2,1)}, u32[]{:S(2)}) copy-start(bf16[256,512]{1,0:T(8,128)(2,1)} %param.11) | copy-start | bytes 786436
  0.6 112.6 %collective-permute-start.1 = (bf16[1536,256]{1,0:T(8,128)(2,1)}, bf16[1536,256]{1,0:T(8,128)(2,1)}, u32[]{:S(2)}, u32[]{:S(2)}) collective-permute-start(bf16[1536,256]{1,0:T(8,128)(2,1)} %param.8), channel_id=1, source_target_pairs={{0,1},{1,0},{2,3},{3,2},{4,5},{5,4},{6,7},{7,6},{8,9},{9,8},{10,11... | collective-permute-start | bytes 2359304 | tf_op jit(solution)/shard_map/ppermute | solution.py:98
  2.2 11.6 %copy-start.13 = (s32[1,128,32]{1,2,0:T(8,128)S(1)}, s32[1,128,32]{1,2,0:T(8,128)}, u32[]{:S(2)}) copy-start(s32[1,128,32]{1,2,0:T(8,128)} %param.13) | copy-start | bytes 49156
  2.9 11.1 %copy-start.5 = (bf16[1536,256]{1,0:T(8,128)(2,1)S(1)}, bf16[1536,256]{1,0:T(8,128)(2,1)}, u32[]{:S(2)}) copy-start(bf16[1536,256]{1,0:T(8,128)(2,1)} %param.8) | copy-start | bytes 2359300
  2.9 18.3 %all-to-all-start.1 = ((bf16[8,32,256]{2,1,0:T(8,128)(2,1)}), bf16[8,32,256]{2,1,0:T(8,128)(2,1)S(1)}, u32[]{:S(2)}, u32[]{:S(2)}) async-start(bf16[8,32,256]{2,1,0:T(8,128)(2,1)} %broadcast_in_dim.11), calls=%async_computation.1 | async-start | bytes 262144 | tf_op jit(solution)/shard_map/all_to_all | solution.py:114
  13.6 99.6 %collective-permute-start = (bf16[2,256,256]{2,1,0:T(8,128)(2,1)}, bf16[2,256,256]{2,1,0:T(8,128)(2,1)}, u32[]{:S(2)}, u32[]{:S(2)}) collective-permute-start(bf16[2,256,256]{2,1,0:T(8,128)(2,1)} %bitcast.3), channel_id=1, source_target_pairs={{0,1},{1,0},{2,3},{3,2},{4,5},{5,4},{6,7},{7,6},{8,9},{9,8},{10,11... | collective-permute-start | bytes 786440 | tf_op jit(solution)/shard_map/ppermute | solution.py:98
  21.2 12.9 %copy-start.11 = (s32[1536,12]{0,1:T(8,128)S(1)}, s32[1536,12]{0,1:T(8,128)}, u32[]{:S(2)}) copy-start(s32[1536,12]{0,1:T(8,128)} %param.14) | copy-start | bytes 221188
  21.2 13.0 %copy-start.12 = (s32[1536]{0:T(1024)S(1)}, s32[1536]{0:T(1024)}, u32[]{:S(2)}) copy-start(s32[1536]{0:T(1024)} %param.15) | copy-start | bytes 18436
  21.2 79.5 %all-to-all-start = ((bf16[128,32,256]{2,1,0:T(8,128)(2,1)}), bf16[128,32,256]{2,1,0:T(8,128)(2,1)S(1)}, u32[]{:S(2)}, u32[]{:S(2)}) async-start(bf16[128,32,256]{2,1,0:T(8,128)(2,1)} %bitcast.73), calls=%async_computation | async-start | bytes 4194304 | tf_op jit(solution)/shard_map/all_to_all | solution.py:154
  36.8 26.9 %collective-permute-start.2 = (bf16[256,256]{1,0:T(8,128)(2,1)S(1)}, bf16[256,256]{1,0:T(8,128)(2,1)S(1)}, u32[]{:S(2)}, u32[]{:S(2)}) collective-permute-start(bf16[256,256]{1,0:T(8,128)(2,1)S(1)} %bitcast.74), channel_id=1, source_target_pairs={{0,48},{2,50},{4,52},{6,54},{8,56},{10,58},{12,60},{14,62},{16,0},... | collective-permute-start | bytes 393224 | tf_op jit(solution)/shard_map/ppermute | solution.py:107
  37.8 26.0 %collective-permute-start.3 = (bf16[256,256]{1,0:T(8,128)(2,1)S(1)}, bf16[256,256]{1,0:T(8,128)(2,1)S(1)}, u32[]{:S(2)}, u32[]{:S(2)}) collective-permute-start(bf16[256,256]{1,0:T(8,128)(2,1)S(1)} %bitcast.75), channel_id=1, source_target_pairs={{0,32},{2,34},{4,36},{6,38},{8,40},{10,42},{12,44},{14,46},{16,48}... | collective-permute-start | bytes 393224 | tf_op jit(solution)/shard_map/ppermute | solution.py:107
  39.8 23.9 %collective-permute-start.4 = (bf16[256,256]{1,0:T(8,128)(2,1)S(1)}, bf16[256,256]{1,0:T(8,128)(2,1)S(1)}, u32[]{:S(2)}, u32[]{:S(2)}) collective-permute-start(bf16[256,256]{1,0:T(8,128)(2,1)S(1)} %bitcast.76), channel_id=1, source_target_pairs={{0,16},{2,18},{4,20},{6,22},{8,24},{10,26},{12,28},{14,30},{16,32}... | collective-permute-start | bytes 393224 | tf_op jit(solution)/shard_map/ppermute | solution.py:107
  54.7 4.5 %copy-start = (bf16[1536,4096]{1,0:T(8,128)(2,1)}, bf16[1536,4096]{1,0:T(8,128)(2,1)S(1)}, u32[]{:S(2)}) copy-start(bf16[1536,4096]{1,0:T(8,128)(2,1)S(1)} %get-tuple-element.6.weight_ref) | copy-start | bytes 37748740
  59.2 4.5 %copy-start.3 = (bf16[1536,4096]{1,0:T(8,128)(2,1)}, bf16[1536,4096]{1,0:T(8,128)(2,1)S(1)}, u32[]{:S(2)}) copy-start(bf16[1536,4096]{1,0:T(8,128)(2,1)S(1)} %get-tuple-element.8) | copy-start | bytes 37748740
  63.8 20.0 %collective-permute-start.5 = (bf16[1024,256]{1,0:T(8,128)(2,1)S(1)}, bf16[1024,256]{1,0:T(8,128)(2,1)S(1)}, u32[]{:S(2)}, u32[]{:S(2)}) collective-permute-start(bf16[1024,256]{1,0:T(8,128)(2,1)S(1)} %pad_maximum_fusion), channel_id=1, source_target_pairs={{0,192},{2,194},{4,196},{6,198},{8,200},{10,202},{12,204},{14,206}... | collective-permute-start | bytes 1572872 | tf_op jit(solution)/shard_map/ppermute | solution.py:107
  67.2 20.3 %collective-permute-start.7 = (bf16[1024,256]{1,0:T(8,128)(2,1)S(1)}, bf16[1024,256]{1,0:T(8,128)(2,1)S(1)}, u32[]{:S(2)}, u32[]{:S(2)}) collective-permute-start(bf16[1024,256]{1,0:T(8,128)(2,1)S(1)} %pad_maximum_fusion), channel_id=1, source_target_pairs={{0,64},{2,66},{4,68},{6,70},{8,72},{10,74},{12,76},{14,78},{16,80}... | collective-permute-start | bytes 1572872 | tf_op jit(solution)/shard_map/ppermute | solution.py:107
  67.2 28.6 %copy-start.4 = (bf16[1536,4096]{1,0:T(8,128)(2,1)S(1)}, bf16[1536,4096]{1,0:T(8,128)(2,1)}, u32[]{:S(2)}) copy-start(bf16[1536,4096]{1,0:T(8,128)(2,1)} %copy-done.3) | copy-start | bytes 37748740
  83.9 8.2 %collective-permute-start.6 = (bf16[512,256]{1,0:T(8,128)(2,1)S(1)}, bf16[512,256]{1,0:T(8,128)(2,1)S(1)}, u32[]{:S(2)}, u32[]{:S(2)}) collective-permute-start(bf16[512,256]{1,0:T(8,128)(2,1)S(1)} %slice.38), channel_id=1, source_target_pairs={{0,192},{2,194},{4,196},{6,198},{8,200},{10,202},{12,204},{14,206}... | collective-permute-start | bytes 786440 | tf_op jit(solution)/shard_map/ppermute | solution.py:107
  87.5 8.2 %collective-permute-start.8 = (bf16[512,256]{1,0:T(8,128)(2,1)S(1)}, bf16[512,256]{1,0:T(8,128)(2,1)S(1)}, u32[]{:S(2)}, u32[]{:S(2)}) collective-permute-start(bf16[512,256]{1,0:T(8,128)(2,1)S(1)} %slice.39), channel_id=1, source_target_pairs={{0,64},{2,66},{4,68},{6,70},{8,72},{10,74},{12,76},{14,78},{16,80}... | collective-permute-start | bytes 786440 | tf_op jit(solution)/shard_map/ppermute | solution.py:107
  100.6 4.6 %copy-start.1 = (bf16[1536,4096]{1,0:T(8,128)(2,1)S(1)}, bf16[1536,4096]{1,0:T(8,128)(2,1)}, u32[]{:S(2)}) copy-start(bf16[1536,4096]{1,0:T(8,128)(2,1)} %copy-done) | copy-start | bytes 37748740
  105.2 1.4 copy-start.2
  106.6 4.4 %copy-start.6 = (bf16[1536,256]{1,0:T(8,128)(2,1)S(1)}, bf16[1536,256]{1,0:T(8,128)(2,1)}, u32[]{:S(2)}) copy-start(bf16[1536,256]{1,0:T(8,128)(2,1)} %param.8) | copy-start | bytes 2359300
  110.9 1.1 copy-start.8
  110.9 4.4 %collective-permute-start.9 = (bf16[1536,256]{1,0:T(8,128)(2,1)S(1)}, bf16[1536,256]{1,0:T(8,128)(2,1)}, u32[]{:S(2)}, u32[]{:S(2)}) collective-permute-start(bf16[1536,256]{1,0:T(8,128)(2,1)S(1)} %finish_mean.1), channel_id=1, source_target_pairs={{0,1},{1,0},{2,3},{3,2},{4,5},{5,4},{6,7},{7,6},{8,9},{9,8},{10,11... | collective-permute-start | bytes 2359304 | tf_op jit(solution)/shard_map/ppermute | solution.py:98
  114.9 1.1 copy-start.9
  120.2 2.1 %copy-start.7 = (bf16[1536,256]{1,0:T(8,128)(2,1)S(1)}, bf16[1536,256]{1,0:T(8,128)(2,1)}, u32[]{:S(2)}) copy-start(bf16[1536,256]{1,0:T(8,128)(2,1)} %param.8) | copy-start | bytes 2359300
  121.8 1.6 collective-permute-start.10
  153.1 25.7 %all-to-all-start.3 = ((bf16[128,4,512]{2,1,0:T(4,128)(2,1)}), bf16[128,4,512]{2,1,0:T(4,128)(2,1)S(1)}, u32[]{:S(2)}, u32[]{:S(2)}) async-start(bf16[128,4,512]{2,1,0:T(4,128)(2,1)} %broadcast_in_dim.24), calls=%async_computation.3 | async-start | bytes 1048576 | tf_op jit(solution)/shard_map/all_to_all | solution.py:182

commit v4 on v3

v4 whole, which is shorter than its diff:
```python
import functools
import math

import jax
import jax.numpy as jnp
from jax import lax
from jax.experimental import pallas as pl
from jax.experimental.pallas import tpu as pltpu
from jax.sharding import PartitionSpec as P

SWAP = [(0, 1), (1, 0)]
LINES = {"x": (32, 4), "y": (8, 4), "z": (1, 8)}
GROUP = 16
SPAN = 256


def incidence_kernel(waits, offset, slots_ref, *refs):
    slots = slots_ref[...]
    low = (slots & (SPAN - 1)).astype(jnp.float32).T
    high = slots >> 8
    lane = lax.broadcasted_iota(jnp.int32, (SPAN, SPAN), 1).astype(jnp.float32)
    owner = lax.broadcasted_iota(jnp.int32, (GROUP, SPAN), 1) & (GROUP - 1)
    own = owner == lax.broadcasted_iota(jnp.int32, (GROUP, SPAN), 0)
    one = jnp.ones((GROUP, SPAN), jnp.bfloat16)
    zero = jnp.zeros((GROUP, SPAN), jnp.bfloat16)
    for g in range(slots.shape[0]):
        right = jnp.where(low[:, g:g + 1] == lane, 1.0, 0.0).astype(jnp.bfloat16)
        mine = jnp.where(own, jnp.broadcast_to(high[g:g + 1, :], (GROUP, SPAN)), -1).astype(jnp.int16)
        first = offset // SPAN
        for out in refs[waits:]:
            tiles = out.shape[1] // SPAN
            left = jnp.concatenate([jnp.where(mine == jnp.int16(first + t), one, zero) for t in range(tiles)], 0)
            made = jnp.dot(left, right, preferred_element_type=jnp.float32).astype(jnp.bfloat16)
            for t in range(tiles):
                out[g * GROUP:(g + 1) * GROUP, t * SPAN:(t + 1) * SPAN] = made[t * GROUP:(t + 1) * GROUP]
            first += tiles

def pack_slots(slots_t, counts):
    deg, nodes = slots_t.shape
    groups = nodes // GROUP
    depth = SPAN // GROUP
    step = lax.broadcasted_iota(jnp.int32, (depth, nodes), 0)
    slots = jnp.pad(slots_t, ((0, depth - deg), (0, 0)), constant_values=-1)
    slots = jnp.where(step < counts[None, :], slots, -1)
    return slots.reshape(depth, groups, GROUP).transpose(1, 0, 2).reshape(groups, SPAN)


def incidence(slots, offset, widths, after, batch=8):
    groups = slots.shape[0]
    nodes = groups * GROUP
    total = sum(widths)
    block = batch * GROUP
    return pl.pallas_call(
        functools.partial(incidence_kernel, len(after), offset),
        grid=(groups // batch,),
        in_specs=[pl.BlockSpec((batch, SPAN), lambda i: (i, 0))]
        + [pl.BlockSpec(memory_space=pl.ANY)] * len(after),
        out_specs=[pl.BlockSpec((block, w), lambda i: (i, 0)) for w in widths],
        out_shape=[jax.ShapeDtypeStruct((nodes, w), jnp.bfloat16) for w in widths],
        cost_estimate=pl.CostEstimate(flops=2 * nodes * total * 64, bytes_accessed=nodes, transcendentals=0),
        compiler_params=pltpu.CompilerParams(vmem_limit_bytes=56 << 20),
        name="incidence",
    )(slots, *after)


def mean_kernel(table_ref, weight_ref, start_ref, counts_ref, out_ref):
    rows = out_ref.shape[0]
    live = jnp.broadcast_to(counts_ref[...].astype(jnp.float32), (8, rows)).T[:, :1]
    total = start_ref[...] + jnp.dot(
        weight_ref[...], table_ref[...], preferred_element_type=jnp.float32
    )
    out_ref[...] = (total / live).astype(jnp.bfloat16)


def finish_mean(table, weight, start, counts, block=256):
    nodes, depth = weight.shape
    width = table.shape[1]
    return pl.pallas_call(
        mean_kernel,
        grid=(nodes // block,),
        in_specs=[
            pl.BlockSpec((depth, width), lambda i: (0, 0), pipeline_mode=pl.Buffered(1)),
            pl.BlockSpec((block, depth), lambda i: (i, 0)),
            pl.BlockSpec((block, width), lambda i: (i, 0)),
            pl.BlockSpec((1, block), lambda i: (0, i)),
        ],
        out_specs=pl.BlockSpec((block, width), lambda i: (i, 0)),
        out_shape=jax.ShapeDtypeStruct((nodes, width), jnp.bfloat16),
        cost_estimate=pl.CostEstimate(
            flops=2 * nodes * depth * width,
            bytes_accessed=2 * (nodes * depth + depth * width + 3 * nodes * width),
            transcendentals=0,
        ),
        compiler_params=pltpu.CompilerParams(vmem_limit_bytes=56 << 20),
        name="finish_mean",
    )(table, weight, start, counts.reshape(1, nodes))


def layer_kernel(core_ref, own, own_far, mean, mean_far, w_self, w_self_far, w_neigh, w_neigh_far,
                 cotangent_ref, out_ref, mine_ref, other_ref, total_ref):
    step = pl.program_id(0)

    def product(rows, weight):
        return jnp.dot(rows[...], weight[...], preferred_element_type=jnp.float32)

    pre = (product(own, w_self) + product(own_far, w_self_far)) + (
        product(mean, w_neigh) + product(mean_far, w_neigh_far)
    )
    scale = math.sqrt(2 / math.pi)
    square = pre * pre
    tanh = jnp.tanh(scale * (pre + 0.044715 * (square * pre)))
    half_up = 0.5 * (1.0 + tanh)
    out_ref[...] = (pre * half_up).astype(jnp.bfloat16)
    slope = half_up + 0.5 * pre * (1.0 - tanh * tanh) * (scale * (1.0 + 3 * 0.044715 * square))
    grad = (cotangent_ref[...].astype(jnp.float32) * slope).astype(jnp.bfloat16)
    part = jnp.concatenate(
        [
            lax.dot_general(
                grad, rows[...], (((0,), (0,)), ((), ())), preferred_element_type=jnp.float32
            )
            for rows in (own, mean, own_far, mean_far)
        ],
        1,
    )

    @pl.when(step == 0)
    def _():
        total_ref[...] = part

    @pl.when(step > 0)
    def _():
        total_ref[...] += part

    @pl.when(step == pl.num_programs(0) - 1)
    def _():
        total = total_ref[...].T.astype(jnp.bfloat16)
        mine_ref[...] = total[:mine_ref.shape[0]]
        other_ref[...] = total[mine_ref.shape[0]:]


def layer(core, own, own_far, mean, mean_far, w_self, w_self_far, w_neigh, w_neigh_far, cotangent, block=256):
    nodes, half = own.shape
    rows = pl.BlockSpec((block, half), lambda i, c: (i, 0))
    weight = pl.BlockSpec((half, half), lambda i, c: (0, c[0]), pipeline_mode=pl.Buffered(1))
    whole = pl.BlockSpec((2 * half, half), lambda i, c: (0, 0))
    return pl.pallas_call(
        layer_kernel,
        grid_spec=pltpu.PrefetchScalarGridSpec(
            num_scalar_prefetch=1,
            grid=(nodes // block,),
            in_specs=[rows] * 4 + [weight] * 4 + [rows],
            out_specs=[rows, whole, whole],
            scratch_shapes=[pltpu.VMEM((half, 4 * half), jnp.float32)],
        ),
        out_shape=[
            jax.ShapeDtypeStruct((nodes, half), jnp.bfloat16),
            jax.ShapeDtypeStruct((2 * half, half), jnp.bfloat16),
            jax.ShapeDtypeStruct((2 * half, half), jnp.bfloat16),
        ],
        cost_estimate=pl.CostEstimate(
            flops=16 * nodes * half * half, bytes_accessed=12 * nodes * half, transcendentals=nodes * half
        ),
        compiler_params=pltpu.CompilerParams(vmem_limit_bytes=24 << 20),
        name="layer",
    )(core, own, own_far, mean, mean_far, w_self, w_self_far, w_neigh, w_neigh_far, cotangent)


def swap(value):
    return lax.ppermute(value, "col", SWAP)


def shift(value, axis, offset):
    stride, size = LINES[axis]
    pairs = []
    for source in range(128):
        here = source // stride % size
        pairs.append((source, source + ((here + offset) % size - here) * stride))
    return lax.ppermute(value, "dom", pairs)


def gather_hubs(block, slots, nodes):
    size = LINES["z"][1]
    line = jnp.concatenate([block] + [shift(block, "z", -ahead) for ahead in range(1, size)], 0)
    plane = jnp.concatenate([line] + [shift(line, "y", -ahead) for ahead in (1, 2, 3)], 0)
    middle = plane.shape[0] // 2
    after, before = shift(plane, "x", -1), shift(plane, "x", 1)
    table = jnp.concatenate(
        [plane, after, shift(after[:middle], "x", -1), shift(before[middle:], "x", 1), before], 0
    )
    here = lax.axis_index("dom")
    hub = slots - nodes
    owner = hub >> 5
    ahead_x = ((owner >> 5) - (here >> 5)) & 3
    ahead_y = ((owner >> 3) - (here >> 3)) & 3
    ahead_z = (owner - here) & 7
    moved = nodes + (((ahead_x * 4 + ahead_y) * 8 + ahead_z) << 5) + (hub & 31)
    is_hub = (hub >= 0) & (hub < table.shape[0])
    return table, plane, jnp.where(is_hub, moved, slots)


def dot(left, right):
    return jnp.dot(left, right, preferred_element_type=jnp.float32)


def shards(features, cotangent, w_self, w_neigh, hub_rows, send_rows, neighbours, counts):
    parts = lax.axis_size("dom")
    nodes, half = features.shape
    core = lax.axis_index("col")
    features_far, w_self_far, w_neigh_far = swap(features), swap(w_self), swap(w_neigh)
    lanes = jnp.arange(nodes, dtype=jnp.int32)[None, :]

    def pick(rows):
        onehot = (rows[:, None] == lanes).astype(jnp.bfloat16)
        return dot(onehot, features).astype(jnp.bfloat16)

    outgoing = pick(send_rows.reshape(-1))
    started = jnp.minimum(jnp.abs(outgoing[0, 0]), 0).astype(jnp.int32)
    outgoing = outgoing.reshape(parts, -1, half)
    hub_block, plane, named = gather_hubs(pick(hub_rows + started), neighbours.T, nodes)
    incoming = lax.all_to_all(outgoing, "dom", split_axis=0, concat_axis=0, tiled=True)

    slots = pack_slots(named, counts)
    near = nodes + hub_block.shape[0]
    far = incoming.shape[0] * incoming.shape[1]
    (far_weight,) = incidence(slots, near, (far,), (plane, features_far, w_self_far, w_neigh_far))
    own_weight, hub_weight = incidence(slots, 0, (nodes, hub_block.shape[0]), (plane,))
    near_sum = dot(own_weight, features) + dot(hub_weight, hub_block)
    neigh_mean = finish_mean(incoming.reshape(-1, half), far_weight, near_sum, counts)
    mean_far = swap(neigh_mean)
    layer_out, mine, other = layer(
        core.astype(jnp.int32).reshape(1), features, features_far, neigh_mean, mean_far,
        w_self, w_self_far, w_neigh, w_neigh_far, cotangent,
    )
    partial = jnp.concatenate([mine, swap(other)], 0).reshape(parts, -1, half)
    pieces = lax.all_to_all(partial, "dom", split_axis=0, concat_axis=0, tiled=True)
    factor = 1.0 / math.sqrt(nodes * parts)
    piece = (pieces.astype(jnp.float32).sum(0) * factor).astype(jnp.bfloat16)
    sums = lax.all_to_all(
        jnp.broadcast_to(piece[None], (parts,) + piece.shape),
        "dom", split_axis=0, concat_axis=0, tiled=True,
    )
    sums = sums.reshape(2, 2, half, half).astype(jnp.float32)
    low = jnp.where(core == 0, sums[0], sums[1])
    high = jnp.where(core == 0, sums[1], sums[0])
    return (
        layer_out,
        jnp.concatenate([low[0], high[0]], 1),
        jnp.concatenate([low[1], high[1]], 1),
    )


def solution(mesh):
    placed = (
        P("dom", "col"),
        P("dom", "col"),
        P("col", None),
        P("col", None),
        P("dom"),
        P("dom", None, None),
        P("dom", None),
        P("dom"),
    )
    return jax.shard_map(
        shards,
        mesh=mesh,
        in_specs=placed,
        out_specs=(P("dom", "col"), P("col", None), P("col", None)),
        check_vma=False,
    )
```

time: 183 us -> 239 us (1.31)
  waiting for transfers between devices: 41.2 us -> 71.8 us
  Pallas kernels: 17.4 us -> 44.2 us
  local copies, waits for them, and re-layouts: 27.7 us -> 18.4 us
  starting transfers between devices: 42.4 us -> 51.5 us
  matrix products: 22.5 us -> 17.3 us
    ppermute x7 -> x14, waiting for transfers between devices: 23.2 us -> 50.5 us  [shift(): return lax.ppermute(value, 'dom', pairs)]
    pallas_call x1 -> x3, Pallas kernels: 13.1 us -> 34.3 us  [the longest x2 26 us: incidence(): pl.pallas_call(functools.partial(incidence_kernel, len(after), offset), g...]
    ppermute x7 -> x14, starting transfers between devices: 11.9 us -> 28.4 us  [shift(): return lax.ppermute(value, 'dom', pairs)]
    unnamed x40 -> x48, local copies, waits for them, and re-layouts: 20.1 us -> 11.2 us
    all_to_all x1 -> x0, starting transfers between devices: 8.6 us -> none  [gather_hubs(): lax.all_to_all(copies, 'dom', split_axis=0, concat_axis=0, tiled=True, ax...]
    pallas_call x1, Pallas kernels: 4.29 us -> 9.89 us  [finish_mean(): pl.pallas_call(mean_kernel, grid=(nodes // block,), in_specs=[pl.BlockSpe...]
    dot_general x4 -> x0, matrix products: 3.81 us -> none  [weight_grad(): lax.dot_general(rows, grad_pre, (((0,), (0,)), ((), ())), preferred_eleme...]
    ppermute x4 -> x5, waiting for transfers between devices: 0.77 us -> 4.04 us  [swap(): return lax.ppermute(value, 'col', SWAP)]
  transfers between devices with their start and end apart: 14 -> 21, of which waited for: 6 -> 8; matrix products, arithmetic and copies ran while one was open for 14% -> 9% of each run, Pallas kernels for 10% -> 11%
where the time goes in v4:
time: 239 us; the launch traced here: 237 us
  waiting for transfers between devices  71.8 us (30%)
  starting transfers between devices  51.5 us (22%)
  Pallas kernels  44.2 us (18%)
  blocking collectives  30.1 us (13%)
  local copies, waits for them, and re-layouts  18.4 us (8%)
  matrix products  17.3 us (7%)
    ppermute x14, waiting for transfers between devices, shift(): return lax.ppermute(value, 'dom', pairs)  50.5 us
    all_to_all x1, blocking collectives, shards(): lax.all_to_all(partial, 'dom', split_axis=0, concat_axis=0, tiled=True)  30.1 us
    ppermute x14, starting transfers between devices, shift(): return lax.ppermute(value, 'dom', pairs)  28.4 us
    pallas_call x2, Pallas kernels, incidence(): pl.pallas_call(functools.partial(incidence_kernel, len(after), offset), g...  26 us
    dot_general x4, matrix products, dot(): return jnp.dot(left, right, preferred_element_type=jnp.float32)  17.3 us
    all_to_all x1, waiting for transfers between devices, shards(): lax.all_to_all(jnp.broadcast_to(piece[None], (parts,) + piece.shape), 'do...  17.2 us
    all_to_all x1, starting transfers between devices, shards(): lax.all_to_all(outgoing, 'dom', split_axis=0, concat_axis=0, tiled=True)  13.8 us
    unnamed x48, local copies, waits for them, and re-layouts  11.2 us
  transfers between devices with their start and end apart: 21, of which 8 were waited for; matrix products, arithmetic and copies ran while one was open for 9% of the time, Pallas kernels for 11%

profile of v4, /device:TPU:8, one launch (start us, length us, event | category | flops | bytes accessed | tf_op | source)
XLA Modules:
  0.0 236.5 jit_solution(3997470282670976243)
XLA Ops:
  0.6 0.8 copy.12
  1.4 0.1 eq.32
  1.5 7.2 %fusion.2 = bf16[4096,256]{1,0:T(8,128)(2,1)} fusion(bf16[1536,256]{1,0:T(8,128)(2,1)} %own.1, s32[4096]{0:T(1024)S(1)} %eq.32), kind=kOutput, calls=%fused_computation.3 | convolution fusion | flops 3228565504 | bytes 2899968 | tf_op jit(solution)/shard_map/dot_general | solution.py:202
  8.8 1.2 slice.44
  10.7 0.9 constant_dynamic-update-slice_fusion.33
  11.6 5.9 %collective-permute-start.1 = (bf16[32,256]{1,0:T(8,128)(2,1)S(1)}, bf16[32,256]{1,0:T(8,128)(2,1)S(1)}, u32[]{:S(2)}, u32[]{:S(2)}) collective-permute-start(bf16[32,256]{1,0:T(8,128)(2,1)S(1)} %get-tuple-element.49), channel_id=1, source_target_pairs={{0,14},{2,0},{4,2},{6,4},{8,6},{10,8},{12,10},{14,12},{16,30},{18,... | collective-permute-start | bytes 49160 | tf_op jit(solution)/shard_map/ppermute | solution.py:178
  17.4 1.4 collective-permute-start.2
  18.9 0.4 collective-permute-start.3
  19.3 5.0 %collective-permute-start.4 = (bf16[32,256]{1,0:T(8,128)(2,1)S(1)}, bf16[32,256]{1,0:T(8,128)(2,1)S(1)}, u32[]{:S(2)}, u32[]{:S(2)}) collective-permute-start(bf16[32,256]{1,0:T(8,128)(2,1)S(1)} %get-tuple-element.49), channel_id=1, source_target_pairs={{0,8},{2,10},{4,12},{6,14},{8,0},{10,2},{12,4},{14,6},{16,24},{18,... | collective-permute-start | bytes 49160 | tf_op jit(solution)/shard_map/ppermute | solution.py:178
  24.4 13.8 %all-to-all-start = ((bf16[128,32,256]{2,1,0:T(8,128)(2,1)}), bf16[128,32,256]{2,1,0:T(8,128)(2,1)}, u32[]{:S(2)}, u32[]{:S(2)}) async-start(bf16[128,32,256]{2,1,0:T(8,128)(2,1)} %bitcast.1), calls=%async_computation | async-start | bytes 4194304 | tf_op jit(solution)/shard_map/all_to_all | solution.py:220
  38.2 2.4 %collective-permute-start.6 = (bf16[32,256]{1,0:T(8,128)(2,1)S(1)}, bf16[32,256]{1,0:T(8,128)(2,1)S(1)}, u32[]{:S(2)}, u32[]{:S(2)}) collective-permute-start(bf16[32,256]{1,0:T(8,128)(2,1)S(1)} %get-tuple-element.49), channel_id=1, source_target_pairs={{0,4},{2,6},{4,8},{6,10},{8,12},{10,14},{12,0},{14,2},{16,20},{18,... | collective-permute-start | bytes 49160 | tf_op jit(solution)/shard_map/ppermute | solution.py:178
  40.6 0.6 constant_dynamic-update-slice_fusion.32
  41.2 1.5 collective-permute-start.7
  42.7 0.6 constant_dynamic-update-slice_fusion.31
  43.3 0.6 constant_dynamic-update-slice_fusion.30
  43.9 0.6 constant_dynamic-update-slice_fusion.29
  44.6 0.6 constant_dynamic-update-slice_fusion.28
  45.2 39.3 %collective-permute-done.6 = bf16[32,256]{1,0:T(8,128)(2,1)S(1)} collective-permute-done((bf16[32,256]{1,0:T(8,128)(2,1)S(1)}, bf16[32,256]{1,0:T(8,128)(2,1)S(1)}, u32[]{:S(2)}, u32[]{:S(2)}) %collective-permute-start.6) | collective-permute-done | bytes 16416 | tf_op jit(solution)/shard_map/ppermute | solution.py:178
  84.5 0.6 constant_dynamic-update-slice_fusion.27
  85.1 0.6 constant_dynamic-update-slice_fusion.26
  85.7 0.9 collective-permute-start.8
  86.6 2.1 collective-permute-start.9
  88.7 0.5 collective-permute-start.11
  89.2 0.3 collective-permute-start.12
  89.5 1.2 collective-permute-done.8
  90.7 1.5 collective-permute-start.10
  92.2 0.7 constant_dynamic-update-slice_fusion.25
  92.9 0.2 collective-permute-done.9
  93.1 0.7 constant_dynamic-update-slice_fusion.24
  93.8 2.1 collective-permute-done.10
  95.9 0.7 constant_dynamic-update-slice_fusion.23
  96.6 3.3 %collective-permute-start.13 = (bf16[1024,256]{1,0:T(8,128)(2,1)}, bf16[1024,256]{1,0:T(8,128)(2,1)}, u32[]{:S(2)}, u32[]{:S(2)}) collective-permute-start(bf16[1024,256]{1,0:T(8,128)(2,1)} %get-tuple-element.20.refs_0_), channel_id=1, source_target_pairs={{0,192},{2,194},{4,196},{6,198},{8,200},{10,202},{12,204},{14,206}... | collective-permute-start | bytes 1572872 | tf_op jit(solution)/shard_map/ppermute | solution.py:178
  100.0 0.1 bitcast_select_fusion
  100.0 0.1 collective-permute-start.15
  100.2 0.6 broadcast_in_dim.16.counts_ref
  100.8 0.3 reshape.60
  101.0 0.2 copy.13
  101.3 0.7 copy.14.slots_ref
  102.0 7.6 %collective-permute-done.13 = bf16[1024,256]{1,0:T(8,128)(2,1)} collective-permute-done((bf16[1024,256]{1,0:T(8,128)(2,1)}, bf16[1024,256]{1,0:T(8,128)(2,1)}, u32[]{:S(2)}, u32[]{:S(2)}) %collective-permute-start.13) | collective-permute-done | bytes 524320 | tf_op jit(solution)/shard_map/ppermute | solution.py:178
  109.7 1.0 slice.45
  110.7 3.8 %collective-permute-start.14 = (bf16[512,256]{1,0:T(8,128)(2,1)S(1)}, bf16[512,256]{1,0:T(8,128)(2,1)S(1)}, u32[]{:S(2)}, u32[]{:S(2)}) collective-permute-start(bf16[512,256]{1,0:T(8,128)(2,1)S(1)} %slice.45), channel_id=1, source_target_pairs={{0,192},{2,194},{4,196},{6,198},{8,200},{10,202},{12,204},{14,206}... | collective-permute-start | bytes 786440 | tf_op jit(solution)/shard_map/ppermute | solution.py:178
  114.4 13.2 %incidence.3 = (bf16[1536,1536]{1,0:T(8,128)(2,1)}, bf16[1536,4096]{1,0:T(8,128)(2,1)}) custom-call(s32[96,256]{1,0:T(8,128)} %copy.14.slots_ref, bf16[1024,256]{1,0:T(8,128)(2,1)} %get-tuple-element.20.refs_0_), custom_call_target="tpu_custom_call" | custom-call | flops 1107296256 | bytes 1536 | tf_op jit(solution)/shard_map/incidence/pallas_call | solution.py:53
  127.6 1.0 slice.46
  128.6 0.1 collective-permute-start.16
  128.7 1.1 constant_dynamic-update-slice_fusion.22
  129.8 0.7 copy-done.4
  130.5 0.1 copy-done.6
  130.6 0.9 copy-done
  131.4 12.8 %incidence.2.weight_ref = bf16[1536,4096]{1,0:T(8,128)(2,1)} custom-call(s32[96,256]{1,0:T(8,128)} %copy.14.slots_ref, bf16[1024,256]{1,0:T(8,128)(2,1)} %get-tuple-element.20.refs_0_, bf16[1536,256]{1,0:T(8,128)(2,1)} %copy-done, bf16[256,512]{1,0:T(8,128)(2,1)} %copy-done.4, bf16[256,512]{1,0:T(8,128)(2,1)} %copy-done.6), custom_call_target="tpu_custom_call" | custom-call | flops 805306368 | bytes 1536 | tf_op jit(solution)/shard_map/incidence/pallas_call | solution.py:53
  144.4 1.2 constant_dynamic-update-slice_fusion.19
  145.6 6.6 %fusion.10 = f32[1536,256]{1,0:T(8,128)S(1)} fusion(bf16[1536,4096]{1,0:T(8,128)(2,1)} %get-tuple-element.9, bf16[4096,256]{1,0:T(8,128)(2,1)S(1)} %constant_dynamic-update-slice_fusion.19), kind=kOutput, calls=%fused_computation.65 | convolution fusion | flops 3221225472 | bytes 16252928 | tf_op jit(solution)/shard_map/dot_general | solution.py:202
  152.2 2.6 %convolution_add_fusion.start_ref = f32[1536,256]{1,0:T(8,128)} fusion(f32[1536,256]{1,0:T(8,128)S(1)} %fusion.10, bf16[1536,1536]{1,0:T(8,128)(2,1)S(1)} %bitcast.45, bf16[1536,256]{1,0:T(8,128)(2,1)S(1)} %copy-done.3), kind=kOutput, calls=%fused_computation.4 | convolution fusion | flops 1208352768 | bytes 8650752 | tf_op jit(solution)/shard_map/dot_general | solution.py:202
  154.9 9.9 %finish_mean.1.mean = bf16[1536,256]{1,0:T(8,128)(2,1)} custom-call(bf16[4096,256]{1,0:T(8,128)(2,1)} %bitcast.2.table_ref, bf16[1536,4096]{1,0:T(8,128)(2,1)} %incidence.2.weight_ref, f32[1536,256]{1,0:T(8,128)} %convolution_add_fusion.start_ref, s32[1,1536]{1,0:T(1,128)} %broadcast_in_dim.16.counts_ref), custom_call_target="tpu_custom_call" | custom-call | flops 3221225472 | bytes 17039360 | tf_op jit(solution)/shard_map/finish_mean/pallas_call | solution.py:78
  164.8 2.6 %collective-permute-done.17.mean_far = bf16[1536,256]{1,0:T(8,128)(2,1)} collective-permute-done((bf16[1536,256]{1,0:T(8,128)(2,1)}, bf16[1536,256]{1,0:T(8,128)(2,1)}, u32[]{:S(2)}, u32[]{:S(2)}) %collective-permute-start.17) | collective-permute-done | bytes 786464 | tf_op jit(solution)/shard_map/ppermute | solution.py:169
  167.4 1.1 copy-done.2
  168.5 8.3 %layer.1 = (bf16[1536,256]{1,0:T(8,128)(2,1)}, bf16[512,256]{1,0:T(8,128)(2,1)S(1)}, bf16[512,256]{1,0:T(8,128)(2,1)S(1)}) custom-call(s32[1]{0:T(128)} %bitcast.core_ref, bf16[1536,256]{1,0:T(8,128)(2,1)S(1)} %copy-done.3, bf16[1536,256]{1,0:T(8,128)(2,1)S(1)} %copy-done.1, bf16[1536,256]{1,0:T(8,128)(2,1)S(1)} %copy-done.2, ...), custom_call_target="tpu_custom_call" | custom-call | flops 1610612736 | bytes 4718592 | tf_op jit(solution)/shard_map/layer/pallas_call | solution.py:146
  176.8 0.1 collective-permute-start.18
  176.9 1.4 collective-permute-done.18
  178.4 30.1 %all_to_all.15 = bf16[128,8,256]{2,1,0:T(8,128)(2,1)S(1)} all-to-all(bf16[128,8,256]{2,1,0:T(8,128)(2,1)S(1)} %maximum_bitcast_fusion), channel_id=1, replica_groups=mesh['dom'=128,'col'=2] {'dom'}, dimensions={0} | all-to-all | bytes 1048576 | tf_op jit(solution)/shard_map/all_to_all | solution.py:235
  208.5 0.1 convert_reduce_fusion
  208.6 0.8 broadcast_in_dim.17
  209.4 8.5 %all-to-all-start.2 = ((bf16[128,8,256]{2,1,0:T(8,128)(2,1)}), bf16[128,8,256]{2,1,0:T(8,128)(2,1)S(1)}, u32[]{:S(2)}, u32[]{:S(2)}) async-start(bf16[128,8,256]{2,1,0:T(8,128)(2,1)} %broadcast_in_dim.17), calls=%async_computation.2 | async-start | bytes 1048576 | tf_op jit(solution)/shard_map/all_to_all | solution.py:238
  217.9 17.2 %all-to-all-done.2 = bf16[128,8,256]{2,1,0:T(8,128)(2,1)S(1)} async-done(((bf16[128,8,256]{2,1,0:T(8,128)(2,1)}), bf16[128,8,256]{2,1,0:T(8,128)(2,1)S(1)}, u32[]{:S(2)}, u32[]{:S(2)}) %all-to-all-start.2) | async-done | bytes 524320 | tf_op jit(solution)/shard_map/all_to_all | solution.py:238
  235.4 1.1 pad_maximum_fusion
  (57 shorter events, 0.4 us)
Async XLA Ops:
  1.5 9.1 %copy-start.14 = (s32[32]{0:T(128)S(1)}, s32[32]{0:T(128)}, u32[]{:S(2)}) copy-start(s32[32]{0:T(128)} %param.12) | copy-start | bytes 388
  1.5 9.1 %copy-start.3 = (bf16[1536,256]{1,0:T(8,128)(2,1)S(1)}, bf16[1536,256]{1,0:T(8,128)(2,1)}, u32[]{:S(2)}) copy-start(bf16[1536,256]{1,0:T(8,128)(2,1)} %own.1) | copy-start | bytes 2359300
  11.6 26.6 %collective-permute-start.1 = (bf16[32,256]{1,0:T(8,128)(2,1)S(1)}, bf16[32,256]{1,0:T(8,128)(2,1)S(1)}, u32[]{:S(2)}, u32[]{:S(2)}) collective-permute-start(bf16[32,256]{1,0:T(8,128)(2,1)S(1)} %get-tuple-element.49), channel_id=1, source_target_pairs={{0,14},{2,0},{4,2},{6,4},{8,6},{10,8},{12,10},{14,12},{16,30},{18,... | collective-permute-start | bytes 49160 | tf_op jit(solution)/shard_map/ppermute | solution.py:178
  17.4 23.8 %collective-permute-start.2 = (bf16[32,256]{1,0:T(8,128)(2,1)S(1)}, bf16[32,256]{1,0:T(8,128)(2,1)S(1)}, u32[]{:S(2)}, u32[]{:S(2)}) collective-permute-start(bf16[32,256]{1,0:T(8,128)(2,1)S(1)} %get-tuple-element.49), channel_id=1, source_target_pairs={{0,12},{2,14},{4,0},{6,2},{8,4},{10,6},{12,8},{14,10},{16,28},{18,... | collective-permute-start | bytes 49160 | tf_op jit(solution)/shard_map/ppermute | solution.py:178
  18.9 24.5 %collective-permute-start.3 = (bf16[32,256]{1,0:T(8,128)(2,1)S(1)}, bf16[32,256]{1,0:T(8,128)(2,1)S(1)}, u32[]{:S(2)}, u32[]{:S(2)}) collective-permute-start(bf16[32,256]{1,0:T(8,128)(2,1)S(1)} %get-tuple-element.49), channel_id=1, source_target_pairs={{0,10},{2,12},{4,14},{6,0},{8,2},{10,4},{12,6},{14,8},{16,26},{18,... | collective-permute-start | bytes 49160 | tf_op jit(solution)/shard_map/ppermute | solution.py:178
  19.3 24.6 %collective-permute-start.4 = (bf16[32,256]{1,0:T(8,128)(2,1)S(1)}, bf16[32,256]{1,0:T(8,128)(2,1)S(1)}, u32[]{:S(2)}, u32[]{:S(2)}) collective-permute-start(bf16[32,256]{1,0:T(8,128)(2,1)S(1)} %get-tuple-element.49), channel_id=1, source_target_pairs={{0,8},{2,10},{4,12},{6,14},{8,0},{10,2},{12,4},{14,6},{16,24},{18,... | collective-permute-start | bytes 49160 | tf_op jit(solution)/shard_map/ppermute | solution.py:178
  24.4 20.2 %collective-permute-start.5 = (bf16[32,256]{1,0:T(8,128)(2,1)S(1)}, bf16[32,256]{1,0:T(8,128)(2,1)S(1)}, u32[]{:S(2)}, u32[]{:S(2)}) collective-permute-start(bf16[32,256]{1,0:T(8,128)(2,1)S(1)} %get-tuple-element.49), channel_id=1, source_target_pairs={{0,6},{2,8},{4,10},{6,12},{8,14},{10,0},{12,2},{14,4},{16,22},{18,... | collective-permute-start | bytes 49160 | tf_op jit(solution)/shard_map/ppermute | solution.py:178
  24.4 64.3 %copy-start.9 = (bf16[256,512]{1,0:T(8,128)(2,1)S(1)}, bf16[256,512]{1,0:T(8,128)(2,1)}, u32[]{:S(2)}) copy-start(bf16[256,512]{1,0:T(8,128)(2,1)} %w_self.1) | copy-start | bytes 786436
  24.4 64.8 %copy-start.10 = (bf16[256,512]{1,0:T(8,128)(2,1)S(1)}, bf16[256,512]{1,0:T(8,128)(2,1)}, u32[]{:S(2)}) copy-start(bf16[256,512]{1,0:T(8,128)(2,1)} %w_neigh.1) | copy-start | bytes 786436
  24.4 75.6 %copy-start.11 = (s32[1536,12]{0,1:T(8,128)S(1)}, s32[1536,12]{0,1:T(8,128)}, u32[]{:S(2)}) copy-start(s32[1536,12]{0,1:T(8,128)} %param.14) | copy-start | bytes 221188
  24.4 75.8 %copy-start.12 = (s32[1536]{0:T(1024)S(1)}, s32[1536]{0:T(1024)}, u32[]{:S(2)}) copy-start(s32[1536]{0:T(1024)} %param.15) | copy-start | bytes 18436
  24.4 130.5 %all-to-all-start = ((bf16[128,32,256]{2,1,0:T(8,128)(2,1)}), bf16[128,32,256]{2,1,0:T(8,128)(2,1)}, u32[]{:S(2)}, u32[]{:S(2)}) async-start(bf16[128,32,256]{2,1,0:T(8,128)(2,1)} %bitcast.1), calls=%async_computation | async-start | bytes 4194304 | tf_op jit(solution)/shard_map/all_to_all | solution.py:220
  38.2 46.3 %collective-permute-start.6 = (bf16[32,256]{1,0:T(8,128)(2,1)S(1)}, bf16[32,256]{1,0:T(8,128)(2,1)S(1)}, u32[]{:S(2)}, u32[]{:S(2)}) collective-permute-start(bf16[32,256]{1,0:T(8,128)(2,1)S(1)} %get-tuple-element.49), channel_id=1, source_target_pairs={{0,4},{2,6},{4,8},{6,10},{8,12},{10,14},{12,0},{14,2},{16,20},{18,... | collective-permute-start | bytes 49160 | tf_op jit(solution)/shard_map/ppermute | solution.py:178
  41.2 43.9 %collective-permute-start.7 = (bf16[32,256]{1,0:T(8,128)(2,1)S(1)}, bf16[32,256]{1,0:T(8,128)(2,1)S(1)}, u32[]{:S(2)}, u32[]{:S(2)}) collective-permute-start(bf16[32,256]{1,0:T(8,128)(2,1)S(1)} %get-tuple-element.49), channel_id=1, source_target_pairs={{0,2},{2,4},{4,6},{6,8},{8,10},{10,12},{12,14},{14,0},{16,18},{18,... | collective-permute-start | bytes 49160 | tf_op jit(solution)/shard_map/ppermute | solution.py:178
  85.7 5.0 %collective-permute-start.8 = (bf16[256,256]{1,0:T(8,128)(2,1)S(1)}, bf16[256,256]{1,0:T(8,128)(2,1)S(1)}, u32[]{:S(2)}, u32[]{:S(2)}) collective-permute-start(bf16[256,256]{1,0:T(8,128)(2,1)S(1)} %get-tuple-element.27), channel_id=1, source_target_pairs={{0,48},{2,50},{4,52},{6,54},{8,56},{10,58},{12,60},{14,62},{16,0},... | collective-permute-start | bytes 393224 | tf_op jit(solution)/shard_map/ppermute | solution.py:178
  86.6 6.5 %collective-permute-start.9 = (bf16[256,256]{1,0:T(8,128)(2,1)S(1)}, bf16[256,256]{1,0:T(8,128)(2,1)S(1)}, u32[]{:S(2)}, u32[]{:S(2)}) collective-permute-start(bf16[256,256]{1,0:T(8,128)(2,1)S(1)} %get-tuple-element.27), channel_id=1, source_target_pairs={{0,32},{2,34},{4,36},{6,38},{8,40},{10,42},{12,44},{14,46},{16,48}... | collective-permute-start | bytes 393224 | tf_op jit(solution)/shard_map/ppermute | solution.py:178
  88.7 41.1 %collective-permute-start = (bf16[1536,256]{1,0:T(8,128)(2,1)S(1)}, bf16[1536,256]{1,0:T(8,128)(2,1)S(1)}, u32[]{:S(2)}, u32[]{:S(2)}) collective-permute-start(bf16[1536,256]{1,0:T(8,128)(2,1)S(1)} %copy-done.3), channel_id=1, source_target_pairs={{0,1},{1,0},{2,3},{3,2},{4,5},{5,4},{6,7},{7,6},{8,9},{9,8},{10,11... | collective-permute-start | bytes 2359304 | tf_op jit(solution)/shard_map/ppermute | solution.py:169
  88.7 41.1 %collective-permute-start.11 = (bf16[256,512]{1,0:T(8,128)(2,1)S(1)}, bf16[256,512]{1,0:T(8,128)(2,1)S(1)}, u32[]{:S(2)}, u32[]{:S(2)}) collective-permute-start(bf16[256,512]{1,0:T(8,128)(2,1)S(1)} %copy-done.9), channel_id=1, source_target_pairs={{0,1},{1,0},{2,3},{3,2},{4,5},{5,4},{6,7},{7,6},{8,9},{9,8},{10,11... | collective-permute-start | bytes 786440 | tf_op jit(solution)/shard_map/ppermute | solution.py:169
  89.2 40.6 %collective-permute-start.12 = (bf16[256,512]{1,0:T(8,128)(2,1)S(1)}, bf16[256,512]{1,0:T(8,128)(2,1)S(1)}, u32[]{:S(2)}, u32[]{:S(2)}) collective-permute-start(bf16[256,512]{1,0:T(8,128)(2,1)S(1)} %copy-done.10), channel_id=1, source_target_pairs={{0,1},{1,0},{2,3},{3,2},{4,5},{5,4},{6,7},{7,6},{8,9},{9,8},{10,11... | collective-permute-start | bytes 786440 | tf_op jit(solution)/shard_map/ppermute | solution.py:169
  90.7 5.2 %collective-permute-start.10 = (bf16[256,256]{1,0:T(8,128)(2,1)S(1)}, bf16[256,256]{1,0:T(8,128)(2,1)S(1)}, u32[]{:S(2)}, u32[]{:S(2)}) collective-permute-start(bf16[256,256]{1,0:T(8,128)(2,1)S(1)} %get-tuple-element.27), channel_id=1, source_target_pairs={{0,16},{2,18},{4,20},{6,22},{8,24},{10,26},{12,28},{14,30},{16,32}... | collective-permute-start | bytes 393224 | tf_op jit(solution)/shard_map/ppermute | solution.py:178
  96.6 13.0 %collective-permute-start.13 = (bf16[1024,256]{1,0:T(8,128)(2,1)}, bf16[1024,256]{1,0:T(8,128)(2,1)}, u32[]{:S(2)}, u32[]{:S(2)}) collective-permute-start(bf16[1024,256]{1,0:T(8,128)(2,1)} %get-tuple-element.20.refs_0_), channel_id=1, source_target_pairs={{0,192},{2,194},{4,196},{6,198},{8,200},{10,202},{12,204},{14,206}... | collective-permute-start | bytes 1572872 | tf_op jit(solution)/shard_map/ppermute | solution.py:178
  100.0 27.6 %collective-permute-start.15 = (bf16[1024,256]{1,0:T(8,128)(2,1)}, bf16[1024,256]{1,0:T(8,128)(2,1)}, u32[]{:S(2)}, u32[]{:S(2)}) collective-permute-start(bf16[1024,256]{1,0:T(8,128)(2,1)} %get-tuple-element.20.refs_0_), channel_id=1, source_target_pairs={{0,64},{2,66},{4,68},{6,70},{8,72},{10,74},{12,76},{14,78},{16,80}... | collective-permute-start | bytes 1572872 | tf_op jit(solution)/shard_map/ppermute | solution.py:178
  110.6 18.0 %copy-start.13 = (bf16[4096,256]{1,0:T(8,128)(2,1)S(1)}, bf16[4096,256]{1,0:T(8,128)(2,1)}, u32[]{:S(2)}) copy-start(bf16[4096,256]{1,0:T(8,128)(2,1)} %get-tuple-element.19) | copy-start | bytes 6291460
  110.7 33.6 %collective-permute-start.14 = (bf16[512,256]{1,0:T(8,128)(2,1)S(1)}, bf16[512,256]{1,0:T(8,128)(2,1)S(1)}, u32[]{:S(2)}, u32[]{:S(2)}) collective-permute-start(bf16[512,256]{1,0:T(8,128)(2,1)S(1)} %slice.45), channel_id=1, source_target_pairs={{0,192},{2,194},{4,196},{6,198},{8,200},{10,202},{12,204},{14,206}... | collective-permute-start | bytes 786440 | tf_op jit(solution)/shard_map/ppermute | solution.py:178
  128.6 15.7 %collective-permute-start.16 = (bf16[512,256]{1,0:T(8,128)(2,1)S(1)}, bf16[512,256]{1,0:T(8,128)(2,1)S(1)}, u32[]{:S(2)}, u32[]{:S(2)}) collective-permute-start(bf16[512,256]{1,0:T(8,128)(2,1)S(1)} %slice.46), channel_id=1, source_target_pairs={{0,64},{2,66},{4,68},{6,70},{8,72},{10,74},{12,76},{14,78},{16,80}... | collective-permute-start | bytes 786440 | tf_op jit(solution)/shard_map/ppermute | solution.py:178
  129.8 0.7 copy-start.4
  129.8 0.8 copy-start.6
  130.6 0.9 copy-start
  144.3 7.9 %slice-start = ((s8[4718592]{0:T(1024)(128)(4,1)}), s8[4194304]{0:T(1024)(128)(4,1)S(1)}, s32[]{:S(2)}) async-start(s8[4718592]{0:T(1024)(128)(4,1)} %bitcast.44), calls=%async_computation.3 | async-start | bytes 8388608
  145.6 6.6 %slice-start.1 = ((s8[4718592]{0:T(1024)(128)(4,1)}), s8[524288]{0:T(1024)(128)(4,1)S(1)}, s32[]{:S(2)}) async-start(s8[4718592]{0:T(1024)(128)(4,1)} %bitcast.44), calls=%async_computation.4 | async-start | bytes 1048576
  154.8 12.5 %copy-start.1 = (bf16[1536,256]{1,0:T(8,128)(2,1)S(1)}, bf16[1536,256]{1,0:T(8,128)(2,1)}, u32[]{:S(2)}) copy-start(bf16[1536,256]{1,0:T(8,128)(2,1)} %copy-done) | copy-start | bytes 2359300
  154.8 12.5 %copy-start.5 = (bf16[256,512]{1,0:T(8,128)(2,1)S(1)}, bf16[256,512]{1,0:T(8,128)(2,1)}, u32[]{:S(2)}) copy-start(bf16[256,512]{1,0:T(8,128)(2,1)} %copy-done.4) | copy-start | bytes 786436
  154.8 12.5 %copy-start.7 = (bf16[256,512]{1,0:T(8,128)(2,1)S(1)}, bf16[256,512]{1,0:T(8,128)(2,1)}, u32[]{:S(2)}) copy-start(bf16[256,512]{1,0:T(8,128)(2,1)} %copy-done.6) | copy-start | bytes 786436
  154.9 12.5 %copy-start.8 = (bf16[1536,256]{1,0:T(8,128)(2,1)S(1)}, bf16[1536,256]{1,0:T(8,128)(2,1)}, u32[]{:S(2)}) copy-start(bf16[1536,256]{1,0:T(8,128)(2,1)} %cotangent_ref.1) | copy-start | bytes 2359300
  164.8 2.6 %collective-permute-start.17 = (bf16[1536,256]{1,0:T(8,128)(2,1)}, bf16[1536,256]{1,0:T(8,128)(2,1)}, u32[]{:S(2)}, u32[]{:S(2)}) collective-permute-start(bf16[1536,256]{1,0:T(8,128)(2,1)} %finish_mean.1.mean), channel_id=1, source_target_pairs={{0,1},{1,0},{2,3},{3,2},{4,5},{5,4},{6,7},{7,6},{8,9},{9,8},{10,11... | collective-permute-start | bytes 2359304 | tf_op jit(solution)/shard_map/ppermute | solution.py:169
  167.4 1.1 copy-start.2
  176.8 1.5 collective-permute-start.18
  209.4 25.7 %all-to-all-start.2 = ((bf16[128,8,256]{2,1,0:T(8,128)(2,1)}), bf16[128,8,256]{2,1,0:T(8,128)(2,1)S(1)}, u32[]{:S(2)}, u32[]{:S(2)}) async-start(bf16[128,8,256]{2,1,0:T(8,128)(2,1)} %broadcast_in_dim.17), calls=%async_computation.2 | async-start | bytes 1048576 | tf_op jit(solution)/shard_map/all_to_all | solution.py:238

commit v5 on v4

--- a/solution.py
+++ b/solution.py
@@ -14,7 +14,7 @@
 SPAN = 256
 
 
-def incidence_kernel(waits, offset, slots_ref, *refs):
+def incidence_kernel(waits, slots_ref, *refs):
     slots = slots_ref[...]
     low = (slots & (SPAN - 1)).astype(jnp.float32).T
     high = slots >> 8
@@ -26,7 +26,7 @@
     for g in range(slots.shape[0]):
         right = jnp.where(low[:, g:g + 1] == lane, 1.0, 0.0).astype(jnp.bfloat16)
         mine = jnp.where(own, jnp.broadcast_to(high[g:g + 1, :], (GROUP, SPAN)), -1).astype(jnp.int16)
-        first = offset // SPAN
+        first = 0
         for out in refs[waits:]:
             tiles = out.shape[1] // SPAN
             left = jnp.concatenate([jnp.where(mine == jnp.int16(first + t), one, zero) for t in range(tiles)], 0)
@@ -45,19 +45,19 @@
     return slots.reshape(depth, groups, GROUP).transpose(1, 0, 2).reshape(groups, SPAN)
 
 
-def incidence(slots, offset, widths, after, batch=8):
+def incidence(slots, widths, after, batch=8):
     groups = slots.shape[0]
     nodes = groups * GROUP
     total = sum(widths)
     block = batch * GROUP
     return pl.pallas_call(
-        functools.partial(incidence_kernel, len(after), offset),
+        functools.partial(incidence_kernel, len(after)),
         grid=(groups // batch,),
         in_specs=[pl.BlockSpec((batch, SPAN), lambda i: (i, 0))]
         + [pl.BlockSpec(memory_space=pl.ANY)] * len(after),
         out_specs=[pl.BlockSpec((block, w), lambda i: (i, 0)) for w in widths],
         out_shape=[jax.ShapeDtypeStruct((nodes, w), jnp.bfloat16) for w in widths],
-        cost_estimate=pl.CostEstimate(flops=2 * nodes * total * 64, bytes_accessed=nodes, transcendentals=0),
+        cost_estimate=pl.CostEstimate(flops=nodes, bytes_accessed=nodes, transcendentals=0),
         compiler_params=pltpu.CompilerParams(vmem_limit_bytes=56 << 20),
         name="incidence",
     )(slots, *after)
@@ -178,15 +178,36 @@
     return lax.ppermute(value, "dom", pairs)
 
 
-def gather_hubs(block, slots, nodes):
-    size = LINES["z"][1]
-    line = jnp.concatenate([block] + [shift(block, "z", -ahead) for ahead in range(1, size)], 0)
-    plane = jnp.concatenate([line] + [shift(line, "y", -ahead) for ahead in (1, 2, 3)], 0)
+def nothing(value):
+    return jnp.minimum(jnp.abs(value[0, 0]), 0)
+
+
+def spread_z(block, picked):
+    near = jnp.concatenate([block] + [shift(block, "z", -ahead) for ahead in (1, 2, 3)], 0)
+    near = near + nothing(picked)
+    return jnp.concatenate([near, shift(near, "z", -4)], 0)
+
+
+def spread_y(line):
+    return jnp.concatenate([line] + [shift(line, "y", -ahead) for ahead in (1, 2, 3)], 0)
+
+
+def spread_x(plane, after, before, weight):
     middle = plane.shape[0] // 2
-    after, before = shift(plane, "x", -1), shift(plane, "x", 1)
-    table = jnp.concatenate(
-        [plane, after, shift(after[:middle], "x", -1), shift(before[middle:], "x", 1), before], 0
-    )
+    zero = nothing(weight)
+    return jnp.concatenate(
+        [
+            plane,
+            after,
+            shift(after[:middle] + zero, "x", -1),
+            shift(before[middle:] + zero, "x", 1),
+            before,
+        ],
+        0,
+    )
+
+
+def table_order(slots, nodes, hubs):
     here = lax.axis_index("dom")
     hub = slots - nodes
     owner = hub >> 5
@@ -194,8 +215,7 @@
     ahead_y = ((owner >> 3) - (here >> 3)) & 3
     ahead_z = (owner - here) & 7
     moved = nodes + (((ahead_x * 4 + ahead_y) * 8 + ahead_z) << 5) + (hub & 31)
-    is_hub = (hub >= 0) & (hub < table.shape[0])
-    return table, plane, jnp.where(is_hub, moved, slots)
+    return jnp.where((hub >= 0) & (hub < hubs), moved, slots)
 
 
 def dot(left, right):
@@ -214,18 +234,19 @@
         return dot(onehot, features).astype(jnp.bfloat16)
 
     outgoing = pick(send_rows.reshape(-1))
-    started = jnp.minimum(jnp.abs(outgoing[0, 0]), 0).astype(jnp.int32)
-    outgoing = outgoing.reshape(parts, -1, half)
-    hub_block, plane, named = gather_hubs(pick(hub_rows + started), neighbours.T, nodes)
-    incoming = lax.all_to_all(outgoing, "dom", split_axis=0, concat_axis=0, tiled=True)
-
-    slots = pack_slots(named, counts)
-    near = nodes + hub_block.shape[0]
-    far = incoming.shape[0] * incoming.shape[1]
-    (far_weight,) = incidence(slots, near, (far,), (plane, features_far, w_self_far, w_neigh_far))
-    own_weight, hub_weight = incidence(slots, 0, (nodes, hub_block.shape[0]), (plane,))
-    near_sum = dot(own_weight, features) + dot(hub_weight, hub_block)
-    neigh_mean = finish_mean(incoming.reshape(-1, half), far_weight, near_sum, counts)
+    plane = spread_y(spread_z(pick(hub_rows), outgoing))
+    incoming = lax.all_to_all(
+        outgoing.reshape(parts, -1, half), "dom", split_axis=0, concat_axis=0, tiled=True
+    ).reshape(-1, half)
+    hubs = parts * hub_rows.shape[0]
+    slots = pack_slots(table_order(neighbours.T, nodes, hubs), counts)
+    after, before = shift(plane, "x", -1), shift(plane, "x", 1)
+    own_weight, hub_weight, far_weight = incidence(
+        slots, (nodes, hubs, incoming.shape[0]), (plane, features_far, w_self_far, w_neigh_far)
+    )
+    table = spread_x(plane, after, before, own_weight)
+    near_sum = dot(own_weight, features) + dot(hub_weight, table)
+    neigh_mean = finish_mean(incoming, far_weight, near_sum, counts)
     mean_far = swap(neigh_mean)
     layer_out, mine, other = layer(
         core.astype(jnp.int32).reshape(1), features, features_far, neigh_mean, mean_far,

time: 239 us -> 186 us (0.78)
  waiting for transfers between devices: 71.8 us -> 36.6 us
  Pallas kernels: 44.2 us -> 34.9 us
  starting transfers between devices: 51.5 us -> 45.4 us
  local copies, waits for them, and re-layouts: 18.4 us -> 14 us
  other arithmetic: 1.54 us -> 4.14 us
    ppermute x14 -> x11, waiting for transfers between devices: 50.5 us -> 15.4 us  [shift(): return lax.ppermute(value, 'dom', pairs)]
    pallas_call x2 -> x1, Pallas kernels: 26 us -> 16.8 us  [incidence(): pl.pallas_call(functools.partial(incidence_kernel, len(after)), grid=(gro...]
    all_to_all x1, starting transfers between devices: 13.8 us -> 10.2 us  [shards(): lax.all_to_all(outgoing.reshape(parts, -1, half), 'dom', split_axis=0, co...]
    unnamed x48 -> x43, local copies, waits for them, and re-layouts: 11.2 us -> 8.19 us
    ppermute x14 -> x11, starting transfers between devices: 28.4 us -> 26 us  [shift(): return lax.ppermute(value, 'dom', pairs)]
  transfers between devices with their start and end apart: 21 -> 18, of which waited for: 8 -> 8; matrix products, arithmetic and copies ran while one was open for 9% -> 15% of each run, Pallas kernels for 11% -> 9%
where the time goes in v5:
time: 186 us; the launch traced here: 184 us
  starting transfers between devices  45.4 us (24%)
  waiting for transfers between devices  36.6 us (20%)
  Pallas kernels  34.9 us (19%)
  blocking collectives  30.2 us (16%)
  matrix products  16.6 us (9%)
  local copies, waits for them, and re-layouts  14 us (8%)
  other arithmetic  4.14 us (2%)
  between operations  2.37 us (1%)
    all_to_all x1, blocking collectives, shards(): lax.all_to_all(partial, 'dom', split_axis=0, concat_axis=0, tiled=True)  30.2 us
    ppermute x11, starting transfers between devices, shift(): return lax.ppermute(value, 'dom', pairs)  26 us
    all_to_all x1, waiting for transfers between devices, shards(): lax.all_to_all(jnp.broadcast_to(piece[None], (parts,) + piece.shape), 'do...  17.2 us
    pallas_call x1, Pallas kernels, incidence(): pl.pallas_call(functools.partial(incidence_kernel, len(after)), grid=(gro...  16.8 us
    dot_general x4, matrix products, dot(): return jnp.dot(left, right, preferred_element_type=jnp.float32)  16.6 us
    ppermute x11, waiting for transfers between devices, shift(): return lax.ppermute(value, 'dom', pairs)  15.4 us
    all_to_all x1, starting transfers between devices, shards(): lax.all_to_all(outgoing.reshape(parts, -1, half), 'dom', split_axis=0, co...  10.2 us
    pallas_call x1, Pallas kernels, finish_mean(): pl.pallas_call(mean_kernel, grid=(nodes // block,), in_specs=[pl.BlockSpe...  9.91 us
  transfers between devices with their start and end apart: 18, of which 8 were waited for; matrix products, arithmetic and copies ran while one was open for 15% of the time, Pallas kernels for 9%

profile of v5, /device:TPU:8, one launch (start us, length us, event | category | flops | bytes accessed | tf_op | source)
XLA Modules:
  0.0 184.2 jit_solution(6741298317247229150)
XLA Ops:
  0.6 1.4 convolution_convert_fusion
  2.1 6.8 %collective-permute-start.3 = (bf16[32,256]{1,0:T(8,128)(2,1)S(1)}, bf16[32,256]{1,0:T(8,128)(2,1)S(1)}, u32[]{:S(2)}, u32[]{:S(2)}) collective-permute-start(bf16[32,256]{1,0:T(8,128)(2,1)S(1)} %convolution_convert_fusion), channel_id=1, source_target_pairs={{0,10},{2,12},{4,14},{6,0},{8,2},{10,4},{12,6},{14,8},{16,26},{18,... | collective-permute-start | bytes 49160 | tf_op jit(solution)/shard_map/ppermute | solution.py:178
  8.9 0.6 collective-permute-start.2
  9.4 0.5 collective-permute-start.1
  9.9 0.8 copy.12
  10.7 0.1 eq.32
  10.8 0.0 copy-start.1
  10.8 5.9 %fusion.2 = bf16[4096,256]{1,0:T(8,128)(2,1)S(1)} fusion(bf16[1536,256]{1,0:T(8,128)(2,1)} %own.1, s32[4096]{0:T(1024)S(1)} %eq.32), kind=kOutput, calls=%fused_computation.3 | convolution fusion | flops 3228565504 | bytes 2899968 | tf_op jit(solution)/shard_map/dot_general | solution.py:222
  16.8 0.5 slice.48
  18.0 0.6 constant_dynamic-update-slice_fusion.13
  18.7 5.0 %collective-permute-start.4 = (bf16[128,256]{1,0:T(8,128)(2,1)S(1)}, bf16[128,256]{1,0:T(8,128)(2,1)S(1)}, u32[]{:S(2)}, u32[]{:S(2)}) collective-permute-start(bf16[128,256]{1,0:T(8,128)(2,1)S(1)} %get-tuple-element.16), channel_id=1, source_target_pairs={{0,8},{2,10},{4,12},{6,14},{8,0},{10,2},{12,4},{14,6},{16,24},{18,... | collective-permute-start | bytes 196616 | tf_op jit(solution)/shard_map/ppermute | solution.py:178
  23.7 0.0 copy-start.9
  23.8 0.0 copy-start.12
  23.8 0.0 copy-start.13
  23.8 10.2 %all-to-all-start = ((bf16[128,32,256]{2,1,0:T(8,128)(2,1)}), bf16[128,32,256]{2,1,0:T(8,128)(2,1)}, u32[]{:S(2)}, u32[]{:S(2)}) async-start(bf16[128,32,256]{2,1,0:T(8,128)(2,1)} %bitcast.43), calls=%async_computation | async-start | bytes 4194304 | tf_op jit(solution)/shard_map/all_to_all | solution.py:238
  34.0 0.1 collective-permute-start.8
  34.1 0.5 collective-permute-start.9
  34.6 1.0 collective-permute-start.5
  35.7 0.6 constant_dynamic-update-slice_fusion.4
  36.3 2.0 %collective-permute-start.6 = (bf16[256,256]{1,0:T(8,128)(2,1)S(1)}, bf16[256,256]{1,0:T(8,128)(2,1)S(1)}, u32[]{:S(2)}, u32[]{:S(2)}) collective-permute-start(bf16[256,256]{1,0:T(8,128)(2,1)S(1)} %pad_maximum_fusion.2), channel_id=1, source_target_pairs={{0,32},{2,34},{4,36},{6,38},{8,40},{10,42},{12,44},{14,46},{16,48}... | collective-permute-start | bytes 393224 | tf_op jit(solution)/shard_map/ppermute | solution.py:178
  38.3 0.7 constant_dynamic-update-slice_fusion.12
  38.9 5.6 %collective-permute-done.5 = bf16[256,256]{1,0:T(8,128)(2,1)S(1)} collective-permute-done((bf16[256,256]{1,0:T(8,128)(2,1)S(1)}, bf16[256,256]{1,0:T(8,128)(2,1)S(1)}, u32[]{:S(2)}, u32[]{:S(2)}) %collective-permute-start.5) | collective-permute-done | bytes 131104 | tf_op jit(solution)/shard_map/ppermute | solution.py:178
  44.5 2.7 %collective-permute-start.7 = (bf16[256,256]{1,0:T(8,128)(2,1)S(1)}, bf16[256,256]{1,0:T(8,128)(2,1)S(1)}, u32[]{:S(2)}, u32[]{:S(2)}) collective-permute-start(bf16[256,256]{1,0:T(8,128)(2,1)S(1)} %pad_maximum_fusion.2), channel_id=1, source_target_pairs={{0,16},{2,18},{4,20},{6,22},{8,24},{10,26},{12,28},{14,30},{16,32}... | collective-permute-start | bytes 393224 | tf_op jit(solution)/shard_map/ppermute | solution.py:178
  47.2 0.7 constant_dynamic-update-slice_fusion.11
  48.0 3.3 %collective-permute-done.6 = bf16[256,256]{1,0:T(8,128)(2,1)S(1)} collective-permute-done((bf16[256,256]{1,0:T(8,128)(2,1)S(1)}, bf16[256,256]{1,0:T(8,128)(2,1)S(1)}, u32[]{:S(2)}, u32[]{:S(2)}) %collective-permute-start.6) | collective-permute-done | bytes 131104 | tf_op jit(solution)/shard_map/ppermute | solution.py:178
  51.2 0.7 constant_dynamic-update-slice_fusion.10
  52.0 0.1 collective-permute-done.7
  52.1 0.7 constant_dynamic-update-slice_fusion.9
  52.8 3.7 %collective-permute-start.10 = (bf16[1024,256]{1,0:T(8,128)(2,1)}, bf16[1024,256]{1,0:T(8,128)(2,1)}, u32[]{:S(2)}, u32[]{:S(2)}) collective-permute-start(bf16[1024,256]{1,0:T(8,128)(2,1)} %get-tuple-element.24.refs_0_), channel_id=1, source_target_pairs={{0,192},{2,194},{4,196},{6,198},{8,200},{10,202},{12,204},{14,206}... | collective-permute-start | bytes 1572872 | tf_op jit(solution)/shard_map/ppermute | solution.py:178
  56.5 0.1 bitcast_select_fusion
  56.6 0.3 collective-permute-start.12
  56.9 0.3 reshape.61
  57.2 0.2 copy.13
  57.4 0.7 copy.14.slots_ref
  58.2 0.7 copy-done.4
  58.9 0.1 copy-done.6
  59.0 0.9 copy-done.2
  59.8 16.8 %incidence.1 = (bf16[1536,1536]{1,0:T(8,128)(2,1)}, bf16[1536,4096]{1,0:T(8,128)(2,1)}, bf16[1536,4096]{1,0:T(8,128)(2,1)}) custom-call(s32[96,256]{1,0:T(8,128)} %copy.14.slots_ref, bf16[1024,256]{1,0:T(8,128)(2,1)} %get-tuple-element.24.refs_0_, bf16[1536,256]{1,0:T(8,128)(2,1)} %copy-done.2, bf16[256,512]{1,0:T(8,128)(2,1)} %copy-done.4, ...), custom_call_target="tpu_custom_call" | custom-call | flops 1536 | bytes 1536 | tf_op jit(solution)/shard_map/incidence/pallas_call | solution.py:53
  76.6 1.2 slice.40
  78.4 1.0 slice_add_fusion.1
  79.4 3.3 %collective-permute-start.11 = (bf16[512,256]{1,0:T(8,128)(2,1)S(1)}, bf16[512,256]{1,0:T(8,128)(2,1)S(1)}, u32[]{:S(2)}, u32[]{:S(2)}) collective-permute-start(bf16[512,256]{1,0:T(8,128)(2,1)S(1)} %slice_add_fusion.1), channel_id=1, source_target_pairs={{0,192},{2,194},{4,196},{6,198},{8,200},{10,202},{12,204},{14,206}... | collective-permute-start | bytes 786440 | tf_op jit(solution)/shard_map/ppermute | solution.py:178
  82.7 1.0 slice_add_fusion
  83.7 0.1 collective-permute-start.13
  83.8 0.6 broadcast_in_dim.16.counts_ref
  84.4 1.1 constant_dynamic-update-slice_fusion.8
  85.5 1.9 %collective-permute-done.11 = bf16[512,256]{1,0:T(8,128)(2,1)S(1)} collective-permute-done((bf16[512,256]{1,0:T(8,128)(2,1)S(1)}, bf16[512,256]{1,0:T(8,128)(2,1)S(1)}, u32[]{:S(2)}, u32[]{:S(2)}) %collective-permute-start.11) | collective-permute-done | bytes 262176 | tf_op jit(solution)/shard_map/ppermute | solution.py:178
  87.4 4.4 %collective-permute-done.13 = bf16[512,256]{1,0:T(8,128)(2,1)S(1)} collective-permute-done((bf16[512,256]{1,0:T(8,128)(2,1)S(1)}, bf16[512,256]{1,0:T(8,128)(2,1)S(1)}, u32[]{:S(2)}, u32[]{:S(2)}) %collective-permute-start.13) | collective-permute-done | bytes 262176 | tf_op jit(solution)/shard_map/ppermute | solution.py:178
  91.9 1.2 constant_dynamic-update-slice_fusion.5
  93.1 6.6 %fusion.10 = f32[1536,256]{1,0:T(8,128)S(1)} fusion(bf16[1536,4096]{1,0:T(8,128)(2,1)} %get-tuple-element.11, bf16[4096,256]{1,0:T(8,128)(2,1)S(1)} %constant_dynamic-update-slice_fusion.5), kind=kOutput, calls=%fused_computation.48 | convolution fusion | flops 3221225472 | bytes 16252928 | tf_op jit(solution)/shard_map/dot_general | solution.py:222
  99.8 2.6 %convolution_add_fusion.start_ref = f32[1536,256]{1,0:T(8,128)} fusion(f32[1536,256]{1,0:T(8,128)S(1)} %fusion.10, bf16[1536,1536]{1,0:T(8,128)(2,1)S(1)} %bitcast.46, bf16[1536,256]{1,0:T(8,128)(2,1)S(1)} %copy-done.1), kind=kOutput, calls=%fused_computation.4 | convolution fusion | flops 1208352768 | bytes 8650752 | tf_op jit(solution)/shard_map/dot_general | solution.py:222
  102.4 9.9 %finish_mean.1.mean = bf16[1536,256]{1,0:T(8,128)(2,1)} custom-call(bf16[4096,256]{1,0:T(8,128)(2,1)} %bitcast.2.table_ref, bf16[1536,4096]{1,0:T(8,128)(2,1)} %get-tuple-element.9.weight_ref, f32[1536,256]{1,0:T(8,128)} %convolution_add_fusion.start_ref, s32[1,1536]{1,0:T(1,128)} %broadcast_in_dim.16.counts_ref), custom_call_target="tpu_custom_call" | custom-call | flops 3221225472 | bytes 17039360 | tf_op jit(solution)/shard_map/finish_mean/pallas_call | solution.py:78
  112.3 2.6 %collective-permute-done.14.mean_far = bf16[1536,256]{1,0:T(8,128)(2,1)} collective-permute-done((bf16[1536,256]{1,0:T(8,128)(2,1)}, bf16[1536,256]{1,0:T(8,128)(2,1)}, u32[]{:S(2)}, u32[]{:S(2)}) %collective-permute-start.14) | collective-permute-done | bytes 786464 | tf_op jit(solution)/shard_map/ppermute | solution.py:169
  115.0 1.1 copy-done
  116.1 8.3 %layer.1 = (bf16[1536,256]{1,0:T(8,128)(2,1)}, bf16[512,256]{1,0:T(8,128)(2,1)S(1)}, bf16[512,256]{1,0:T(8,128)(2,1)S(1)}) custom-call(s32[1]{0:T(128)} %bitcast.core_ref, bf16[1536,256]{1,0:T(8,128)(2,1)S(1)} %copy-done.1, bf16[1536,256]{1,0:T(8,128)(2,1)S(1)} %copy-done.3, bf16[1536,256]{1,0:T(8,128)(2,1)S(1)} %copy-done, ...), custom_call_target="tpu_custom_call" | custom-call | flops 1610612736 | bytes 4718592 | tf_op jit(solution)/shard_map/layer/pallas_call | solution.py:146
  124.4 0.1 collective-permute-start.15
  124.5 1.4 collective-permute-done.15
  126.0 30.2 %all_to_all.15 = bf16[128,8,256]{2,1,0:T(8,128)(2,1)S(1)} all-to-all(bf16[128,8,256]{2,1,0:T(8,128)(2,1)S(1)} %maximum_bitcast_fusion), channel_id=1, replica_groups=mesh['dom'=128,'col'=2] {'dom'}, dimensions={0} | all-to-all | bytes 1048576 | tf_op jit(solution)/shard_map/all_to_all | solution.py:256
  156.1 0.1 convert_reduce_fusion
  156.3 0.8 broadcast_in_dim.17
  157.1 8.5 %all-to-all-start.2 = ((bf16[128,8,256]{2,1,0:T(8,128)(2,1)}), bf16[128,8,256]{2,1,0:T(8,128)(2,1)S(1)}, u32[]{:S(2)}, u32[]{:S(2)}) async-start(bf16[128,8,256]{2,1,0:T(8,128)(2,1)} %broadcast_in_dim.17), calls=%async_computation.2 | async-start | bytes 1048576 | tf_op jit(solution)/shard_map/all_to_all | solution.py:259
  165.6 17.2 %all-to-all-done.2 = bf16[128,8,256]{2,1,0:T(8,128)(2,1)S(1)} async-done(((bf16[128,8,256]{2,1,0:T(8,128)(2,1)}), bf16[128,8,256]{2,1,0:T(8,128)(2,1)S(1)}, u32[]{:S(2)}, u32[]{:S(2)}) %all-to-all-start.2) | async-done | bytes 524320 | tf_op jit(solution)/shard_map/all_to_all | solution.py:259
  182.8 0.1 convert_element_type.26
  182.9 0.1 slice_select_fusion.1
  183.0 1.1 pad_maximum_fusion
  (47 shorter events, 0.3 us)
Async XLA Ops:
  2.1 15.9 %collective-permute-start.3 = (bf16[32,256]{1,0:T(8,128)(2,1)S(1)}, bf16[32,256]{1,0:T(8,128)(2,1)S(1)}, u32[]{:S(2)}, u32[]{:S(2)}) collective-permute-start(bf16[32,256]{1,0:T(8,128)(2,1)S(1)} %convolution_convert_fusion), channel_id=1, source_target_pairs={{0,10},{2,12},{4,14},{6,0},{8,2},{10,4},{12,6},{14,8},{16,26},{18,... | collective-permute-start | bytes 49160 | tf_op jit(solution)/shard_map/ppermute | solution.py:178
  8.9 9.1 %collective-permute-start.2 = (bf16[32,256]{1,0:T(8,128)(2,1)S(1)}, bf16[32,256]{1,0:T(8,128)(2,1)S(1)}, u32[]{:S(2)}, u32[]{:S(2)}) collective-permute-start(bf16[32,256]{1,0:T(8,128)(2,1)S(1)} %convolution_convert_fusion), channel_id=1, source_target_pairs={{0,12},{2,14},{4,0},{6,2},{8,4},{10,6},{12,8},{14,10},{16,28},{18,... | collective-permute-start | bytes 49160 | tf_op jit(solution)/shard_map/ppermute | solution.py:178
  9.4 8.6 %collective-permute-start.1 = (bf16[32,256]{1,0:T(8,128)(2,1)S(1)}, bf16[32,256]{1,0:T(8,128)(2,1)S(1)}, u32[]{:S(2)}, u32[]{:S(2)}) collective-permute-start(bf16[32,256]{1,0:T(8,128)(2,1)S(1)} %convolution_convert_fusion), channel_id=1, source_target_pairs={{0,14},{2,0},{4,2},{6,4},{8,6},{10,8},{12,10},{14,12},{16,30},{18,... | collective-permute-start | bytes 49160 | tf_op jit(solution)/shard_map/ppermute | solution.py:178
  10.8 12.9 %copy-start.1 = (bf16[1536,256]{1,0:T(8,128)(2,1)S(1)}, bf16[1536,256]{1,0:T(8,128)(2,1)}, u32[]{:S(2)}) copy-start(bf16[1536,256]{1,0:T(8,128)(2,1)} %own.1) | copy-start | bytes 2359300
  16.7 7.0 %copy-start.11 = (bf16[4096,256]{1,0:T(8,128)(2,1)}, bf16[4096,256]{1,0:T(8,128)(2,1)S(1)}, u32[]{:S(2)}) copy-start(bf16[4096,256]{1,0:T(8,128)(2,1)S(1)} %fusion.2) | copy-start | bytes 6291460
  18.7 15.9 %collective-permute-start.4 = (bf16[128,256]{1,0:T(8,128)(2,1)S(1)}, bf16[128,256]{1,0:T(8,128)(2,1)S(1)}, u32[]{:S(2)}, u32[]{:S(2)}) collective-permute-start(bf16[128,256]{1,0:T(8,128)(2,1)S(1)} %get-tuple-element.16), channel_id=1, source_target_pairs={{0,8},{2,10},{4,12},{6,14},{8,0},{10,2},{12,4},{14,6},{16,24},{18,... | collective-permute-start | bytes 196616 | tf_op jit(solution)/shard_map/ppermute | solution.py:178
  23.7 34.5 %collective-permute-start = (bf16[1536,256]{1,0:T(8,128)(2,1)S(1)}, bf16[1536,256]{1,0:T(8,128)(2,1)S(1)}, u32[]{:S(2)}, u32[]{:S(2)}) collective-permute-start(bf16[1536,256]{1,0:T(8,128)(2,1)S(1)} %copy-done.1), channel_id=1, source_target_pairs={{0,1},{1,0},{2,3},{3,2},{4,5},{5,4},{6,7},{7,6},{8,9},{9,8},{10,11... | collective-permute-start | bytes 2359304 | tf_op jit(solution)/shard_map/ppermute | solution.py:169
  23.7 10.3 %copy-start.9 = (bf16[256,512]{1,0:T(8,128)(2,1)S(1)}, bf16[256,512]{1,0:T(8,128)(2,1)}, u32[]{:S(2)}) copy-start(bf16[256,512]{1,0:T(8,128)(2,1)} %w_self.1) | copy-start | bytes 786436
  23.8 10.4 %copy-start.10 = (bf16[256,512]{1,0:T(8,128)(2,1)S(1)}, bf16[256,512]{1,0:T(8,128)(2,1)}, u32[]{:S(2)}) copy-start(bf16[256,512]{1,0:T(8,128)(2,1)} %w_neigh.1) | copy-start | bytes 786436
  23.8 32.8 %copy-start.12 = (s32[1536,12]{0,1:T(8,128)S(1)}, s32[1536,12]{0,1:T(8,128)}, u32[]{:S(2)}) copy-start(s32[1536,12]{0,1:T(8,128)} %param.14) | copy-start | bytes 221188
  23.8 33.1 %copy-start.13 = (s32[1536]{0:T(1024)S(1)}, s32[1536]{0:T(1024)}, u32[]{:S(2)}) copy-start(s32[1536]{0:T(1024)} %param.15) | copy-start | bytes 18436
  23.8 78.6 %all-to-all-start = ((bf16[128,32,256]{2,1,0:T(8,128)(2,1)}), bf16[128,32,256]{2,1,0:T(8,128)(2,1)}, u32[]{:S(2)}, u32[]{:S(2)}) async-start(bf16[128,32,256]{2,1,0:T(8,128)(2,1)} %bitcast.43), calls=%async_computation | async-start | bytes 4194304 | tf_op jit(solution)/shard_map/all_to_all | solution.py:238
  34.0 24.2 %collective-permute-start.8 = (bf16[256,512]{1,0:T(8,128)(2,1)S(1)}, bf16[256,512]{1,0:T(8,128)(2,1)S(1)}, u32[]{:S(2)}, u32[]{:S(2)}) collective-permute-start(bf16[256,512]{1,0:T(8,128)(2,1)S(1)} %copy-done.9), channel_id=1, source_target_pairs={{0,1},{1,0},{2,3},{3,2},{4,5},{5,4},{6,7},{7,6},{8,9},{9,8},{10,11... | collective-permute-start | bytes 786440 | tf_op jit(solution)/shard_map/ppermute | solution.py:169
  34.1 24.1 %collective-permute-start.9 = (bf16[256,512]{1,0:T(8,128)(2,1)S(1)}, bf16[256,512]{1,0:T(8,128)(2,1)S(1)}, u32[]{:S(2)}, u32[]{:S(2)}) collective-permute-start(bf16[256,512]{1,0:T(8,128)(2,1)S(1)} %copy-done.10), channel_id=1, source_target_pairs={{0,1},{1,0},{2,3},{3,2},{4,5},{5,4},{6,7},{7,6},{8,9},{9,8},{10,11... | collective-permute-start | bytes 786440 | tf_op jit(solution)/shard_map/ppermute | solution.py:169
  34.6 9.9 %collective-permute-start.5 = (bf16[256,256]{1,0:T(8,128)(2,1)S(1)}, bf16[256,256]{1,0:T(8,128)(2,1)S(1)}, u32[]{:S(2)}, u32[]{:S(2)}) collective-permute-start(bf16[256,256]{1,0:T(8,128)(2,1)S(1)} %pad_maximum_fusion.2), channel_id=1, source_target_pairs={{0,48},{2,50},{4,52},{6,54},{8,56},{10,58},{12,60},{14,62},{16,0},... | collective-permute-start | bytes 393224 | tf_op jit(solution)/shard_map/ppermute | solution.py:178
  36.3 14.9 %collective-permute-start.6 = (bf16[256,256]{1,0:T(8,128)(2,1)S(1)}, bf16[256,256]{1,0:T(8,128)(2,1)S(1)}, u32[]{:S(2)}, u32[]{:S(2)}) collective-permute-start(bf16[256,256]{1,0:T(8,128)(2,1)S(1)} %pad_maximum_fusion.2), channel_id=1, source_target_pairs={{0,32},{2,34},{4,36},{6,38},{8,40},{10,42},{12,44},{14,46},{16,48}... | collective-permute-start | bytes 393224 | tf_op jit(solution)/shard_map/ppermute | solution.py:178
  44.5 7.6 %collective-permute-start.7 = (bf16[256,256]{1,0:T(8,128)(2,1)S(1)}, bf16[256,256]{1,0:T(8,128)(2,1)S(1)}, u32[]{:S(2)}, u32[]{:S(2)}) collective-permute-start(bf16[256,256]{1,0:T(8,128)(2,1)S(1)} %pad_maximum_fusion.2), channel_id=1, source_target_pairs={{0,16},{2,18},{4,20},{6,22},{8,24},{10,26},{12,28},{14,30},{16,32}... | collective-permute-start | bytes 393224 | tf_op jit(solution)/shard_map/ppermute | solution.py:178
  52.8 25.6 %collective-permute-start.10 = (bf16[1024,256]{1,0:T(8,128)(2,1)}, bf16[1024,256]{1,0:T(8,128)(2,1)}, u32[]{:S(2)}, u32[]{:S(2)}) collective-permute-start(bf16[1024,256]{1,0:T(8,128)(2,1)} %get-tuple-element.24.refs_0_), channel_id=1, source_target_pairs={{0,192},{2,194},{4,196},{6,198},{8,200},{10,202},{12,204},{14,206}... | collective-permute-start | bytes 1572872 | tf_op jit(solution)/shard_map/ppermute | solution.py:178
  56.6 26.1 %collective-permute-start.12 = (bf16[1024,256]{1,0:T(8,128)(2,1)}, bf16[1024,256]{1,0:T(8,128)(2,1)}, u32[]{:S(2)}, u32[]{:S(2)}) collective-permute-start(bf16[1024,256]{1,0:T(8,128)(2,1)} %get-tuple-element.24.refs_0_), channel_id=1, source_target_pairs={{0,64},{2,66},{4,68},{6,70},{8,72},{10,74},{12,76},{14,78},{16,80}... | collective-permute-start | bytes 1572872 | tf_op jit(solution)/shard_map/ppermute | solution.py:178
  58.2 26.2 %copy-start.14 = (bf16[4096,256]{1,0:T(8,128)(2,1)S(1)}, bf16[4096,256]{1,0:T(8,128)(2,1)}, u32[]{:S(2)}) copy-start(bf16[4096,256]{1,0:T(8,128)(2,1)} %get-tuple-element.23) | copy-start | bytes 6291460
  58.2 0.7 copy-start.4
  58.2 0.8 copy-start.6
  59.0 0.9 copy-start.2
  79.4 8.0 %collective-permute-start.11 = (bf16[512,256]{1,0:T(8,128)(2,1)S(1)}, bf16[512,256]{1,0:T(8,128)(2,1)S(1)}, u32[]{:S(2)}, u32[]{:S(2)}) collective-permute-start(bf16[512,256]{1,0:T(8,128)(2,1)S(1)} %slice_add_fusion.1), channel_id=1, source_target_pairs={{0,192},{2,194},{4,196},{6,198},{8,200},{10,202},{12,204},{14,206}... | collective-permute-start | bytes 786440 | tf_op jit(solution)/shard_map/ppermute | solution.py:178
  83.7 8.2 %collective-permute-start.13 = (bf16[512,256]{1,0:T(8,128)(2,1)S(1)}, bf16[512,256]{1,0:T(8,128)(2,1)S(1)}, u32[]{:S(2)}, u32[]{:S(2)}) collective-permute-start(bf16[512,256]{1,0:T(8,128)(2,1)S(1)} %slice_add_fusion), channel_id=1, source_target_pairs={{0,64},{2,66},{4,68},{6,70},{8,72},{10,74},{12,76},{14,78},{16,80}... | collective-permute-start | bytes 786440 | tf_op jit(solution)/shard_map/ppermute | solution.py:178
  91.9 7.9 %slice-start = ((s8[4718592]{0:T(1024)(128)(4,1)}), s8[4194304]{0:T(1024)(128)(4,1)S(1)}, s32[]{:S(2)}) async-start(s8[4718592]{0:T(1024)(128)(4,1)} %bitcast.45), calls=%async_computation.3 | async-start | bytes 8388608
  93.1 6.6 %slice-start.1 = ((s8[4718592]{0:T(1024)(128)(4,1)}), s8[524288]{0:T(1024)(128)(4,1)S(1)}, s32[]{:S(2)}) async-start(s8[4718592]{0:T(1024)(128)(4,1)} %bitcast.45), calls=%async_computation.4 | async-start | bytes 1048576
  102.4 12.6 %copy-start.3 = (bf16[1536,256]{1,0:T(8,128)(2,1)S(1)}, bf16[1536,256]{1,0:T(8,128)(2,1)}, u32[]{:S(2)}) copy-start(bf16[1536,256]{1,0:T(8,128)(2,1)} %copy-done.2) | copy-start | bytes 2359300
  102.4 12.6 %copy-start.5 = (bf16[256,512]{1,0:T(8,128)(2,1)S(1)}, bf16[256,512]{1,0:T(8,128)(2,1)}, u32[]{:S(2)}) copy-start(bf16[256,512]{1,0:T(8,128)(2,1)} %copy-done.4) | copy-start | bytes 786436
  102.4 12.6 %copy-start.7 = (bf16[256,512]{1,0:T(8,128)(2,1)S(1)}, bf16[256,512]{1,0:T(8,128)(2,1)}, u32[]{:S(2)}) copy-start(bf16[256,512]{1,0:T(8,128)(2,1)} %copy-done.6) | copy-start | bytes 786436
  102.4 12.6 %copy-start.8 = (bf16[1536,256]{1,0:T(8,128)(2,1)S(1)}, bf16[1536,256]{1,0:T(8,128)(2,1)}, u32[]{:S(2)}) copy-start(bf16[1536,256]{1,0:T(8,128)(2,1)} %cotangent_ref.1) | copy-start | bytes 2359300
  112.3 2.6 %collective-permute-start.14 = (bf16[1536,256]{1,0:T(8,128)(2,1)}, bf16[1536,256]{1,0:T(8,128)(2,1)}, u32[]{:S(2)}, u32[]{:S(2)}) collective-permute-start(bf16[1536,256]{1,0:T(8,128)(2,1)} %finish_mean.1.mean), channel_id=1, source_target_pairs={{0,1},{1,0},{2,3},{3,2},{4,5},{5,4},{6,7},{7,6},{8,9},{9,8},{10,11... | collective-permute-start | bytes 2359304 | tf_op jit(solution)/shard_map/ppermute | solution.py:169
  115.0 1.1 copy-start
  124.4 1.5 collective-permute-start.15
  157.1 25.7 %all-to-all-start.2 = ((bf16[128,8,256]{2,1,0:T(8,128)(2,1)}), bf16[128,8,256]{2,1,0:T(8,128)(2,1)S(1)}, u32[]{:S(2)}, u32[]{:S(2)}) async-start(bf16[128,8,256]{2,1,0:T(8,128)(2,1)} %broadcast_in_dim.17), calls=%async_computation.2 | async-start | bytes 1048576 | tf_op jit(solution)/shard_map/all_to_all | solution.py:259

commit v6 on v5

--- a/solution.py
+++ b/solution.py
@@ -61,39 +61,6 @@
         compiler_params=pltpu.CompilerParams(vmem_limit_bytes=56 << 20),
         name="incidence",
     )(slots, *after)
-
-
-def mean_kernel(table_ref, weight_ref, start_ref, counts_ref, out_ref):
-    rows = out_ref.shape[0]
-    live = jnp.broadcast_to(counts_ref[...].astype(jnp.float32), (8, rows)).T[:, :1]
-    total = start_ref[...] + jnp.dot(
-        weight_ref[...], table_ref[...], preferred_element_type=jnp.float32
-    )
-    out_ref[...] = (total / live).astype(jnp.bfloat16)
-
-
-def finish_mean(table, weight, start, counts, block=256):
-    nodes, depth = weight.shape
-    width = table.shape[1]
-    return pl.pallas_call(
-        mean_kernel,
-        grid=(nodes // block,),
-        in_specs=[
-            pl.BlockSpec((depth, width), lambda i: (0, 0), pipeline_mode=pl.Buffered(1)),
-            pl.BlockSpec((block, depth), lambda i: (i, 0)),
-            pl.BlockSpec((block, width), lambda i: (i, 0)),
-            pl.BlockSpec((1, block), lambda i: (0, i)),
-        ],
-        out_specs=pl.BlockSpec((block, width), lambda i: (i, 0)),
-        out_shape=jax.ShapeDtypeStruct((nodes, width), jnp.bfloat16),
-        cost_estimate=pl.CostEstimate(
-            flops=2 * nodes * depth * width,
-            bytes_accessed=2 * (nodes * depth + depth * width + 3 * nodes * width),
-            transcendentals=0,
-        ),
-        compiler_params=pltpu.CompilerParams(vmem_limit_bytes=56 << 20),
-        name="finish_mean",
-    )(table, weight, start, counts.reshape(1, nodes))
 
 
 def layer_kernel(core_ref, own, own_far, mean, mean_far, w_self, w_self_far, w_neigh, w_neigh_far,
@@ -182,10 +149,25 @@
     return jnp.minimum(jnp.abs(value[0, 0]), 0)
 
 
-def spread_z(block, picked):
-    near = jnp.concatenate([block] + [shift(block, "z", -ahead) for ahead in (1, 2, 3)], 0)
-    near = near + nothing(picked)
-    return jnp.concatenate([near, shift(near, "z", -4)], 0)
+def exchange(blocks, axes):
+    fixed = [(stride, size) for axis, (stride, size) in LINES.items() if axis not in axes]
+    moving = [LINES[axis] for axis in axes]
+
+    def spots(lines):
+        found = [0]
+        for stride, size in lines:
+            found = [spot + step * stride for spot in found for step in range(size)]
+        return found
+
+    groups = [[base + spot for spot in spots(moving)] for base in spots(fixed)]
+    return lax.all_to_all(
+        blocks, "dom", split_axis=0, concat_axis=0, tiled=True, axis_index_groups=groups
+    )
+
+
+def share(block, axes):
+    count = math.prod(LINES[axis][1] for axis in axes)
+    return exchange(jnp.broadcast_to(block[None], (count,) + block.shape), axes)
 
 
 def spread_y(line):
@@ -213,8 +195,7 @@
     owner = hub >> 5
     ahead_x = ((owner >> 5) - (here >> 5)) & 3
     ahead_y = ((owner >> 3) - (here >> 3)) & 3
-    ahead_z = (owner - here) & 7
-    moved = nodes + (((ahead_x * 4 + ahead_y) * 8 + ahead_z) << 5) + (hub & 31)
+    moved = nodes + ((ahead_x * 4 + ahead_y) << 8) + (hub & 255)
     return jnp.where((hub >= 0) & (hub < hubs), moved, slots)
 
 
@@ -234,7 +215,7 @@
         return dot(onehot, features).astype(jnp.bfloat16)
 
     outgoing = pick(send_rows.reshape(-1))
-    plane = spread_y(spread_z(pick(hub_rows), outgoing))
+    plane = spread_y(share(pick(hub_rows), "z").reshape(-1, half))
     incoming = lax.all_to_all(
         outgoing.reshape(parts, -1, half), "dom", split_axis=0, concat_axis=0, tiled=True
     ).reshape(-1, half)
@@ -245,22 +226,22 @@
         slots, (nodes, hubs, incoming.shape[0]), (plane, features_far, w_self_far, w_neigh_far)
     )
     table = spread_x(plane, after, before, own_weight)
-    near_sum = dot(own_weight, features) + dot(hub_weight, table)
-    neigh_mean = finish_mean(incoming, far_weight, near_sum, counts)
+    total = dot(own_weight, features) + dot(hub_weight, table) + dot(far_weight, incoming)
+    neigh_mean = (total / counts[:, None].astype(jnp.float32)).astype(jnp.bfloat16)
     mean_far = swap(neigh_mean)
     layer_out, mine, other = layer(
         core.astype(jnp.int32).reshape(1), features, features_far, neigh_mean, mean_far,
         w_self, w_self_far, w_neigh, w_neigh_far, cotangent,
     )
-    partial = jnp.concatenate([mine, swap(other)], 0).reshape(parts, -1, half)
-    pieces = lax.all_to_all(partial, "dom", split_axis=0, concat_axis=0, tiled=True)
+    partial = jnp.concatenate([mine, swap(other)], 0).reshape(16, -1, half)
+
+    def added(pieces):
+        return pieces.astype(jnp.float32).sum(0)
+
+    piece = added(exchange(partial, "xy")).astype(jnp.bfloat16)
     factor = 1.0 / math.sqrt(nodes * parts)
-    piece = (pieces.astype(jnp.float32).sum(0) * factor).astype(jnp.bfloat16)
-    sums = lax.all_to_all(
-        jnp.broadcast_to(piece[None], (parts,) + piece.shape),
-        "dom", split_axis=0, concat_axis=0, tiled=True,
-    )
-    sums = sums.reshape(2, 2, half, half).astype(jnp.float32)
+    piece = (added(share(piece, "z")) * factor).astype(jnp.bfloat16)
+    sums = share(piece, "xy").reshape(2, 2, half, half).astype(jnp.float32)
     low = jnp.where(core == 0, sums[0], sums[1])
     high = jnp.where(core == 0, sums[1], sums[0])
     return (

time: 186 us -> 178 us (0.957)
  matrix products: 16.6 us -> 28.1 us
  Pallas kernels: 34.9 us -> 25.3 us
  starting transfers between devices: 45.4 us -> 38.6 us
  blocking collectives: 30.2 us -> 34.9 us
  waiting for transfers between devices: 36.6 us -> 32.5 us
  local copies, waits for them, and re-layouts: 14 us -> 12.1 us
    ppermute x11 -> x7, starting transfers between devices: 26 us -> 10.3 us  [shift(): return lax.ppermute(value, 'dom', pairs)]
    dot_general x4 -> x5, matrix products: 16.6 us -> 28.1 us  [dot(): return jnp.dot(left, right, preferred_element_type=jnp.float32)]
    pallas_call x1 -> x0, Pallas kernels: 9.91 us -> none  [finish_mean(): pl.pallas_call(mean_kernel, grid=(nodes // block,), in_specs=[pl.BlockSpe...]
    all_to_all x1 -> x2, waiting for transfers between devices: 17.2 us -> 9.81 us  [exchange(): lax.all_to_all(blocks, 'dom', split_axis=0, concat_axis=0, tiled=True, ax...]
    all_to_all x1 -> x2, starting transfers between devices: 8.47 us -> 14 us  [exchange(): lax.all_to_all(blocks, 'dom', split_axis=0, concat_axis=0, tiled=True, ax...]
    all_to_all x1 -> x2, blocking collectives: 30.2 us -> 34.9 us  [exchange(): lax.all_to_all(blocks, 'dom', split_axis=0, concat_axis=0, tiled=True, ax...]
    all_to_all x1, starting transfers between devices: 10.2 us -> 13.6 us  [shards(): lax.all_to_all(outgoing.reshape(parts, -1, half), 'dom', split_axis=0, co...]
    ppermute x11 -> x7, waiting for transfers between devices: 15.4 us -> 18.7 us  [shift(): return lax.ppermute(value, 'dom', pairs)]
  transfers between devices with their start and end apart: 18 -> 15, of which waited for: 8 -> 9; matrix products, arithmetic and copies ran while one was open for 15% -> 15% of each run, Pallas kernels for 9% -> 10%
where the time goes in v6:
time: 178 us; the launch traced here: 177 us
  starting transfers between devices  38.6 us (22%)
  blocking collectives  34.9 us (20%)
  waiting for transfers between devices  32.5 us (18%)
  matrix products  28.1 us (16%)
  Pallas kernels  25.3 us (14%)
  local copies, waits for them, and re-layouts  12.1 us (7%)
  other arithmetic  4.02 us (2%)
    all_to_all x2, blocking collectives, exchange(): lax.all_to_all(blocks, 'dom', split_axis=0, concat_axis=0, tiled=True, ax...  34.9 us
    dot_general x5, matrix products, dot(): return jnp.dot(left, right, preferred_element_type=jnp.float32)  28.1 us
    ppermute x7, waiting for transfers between devices, shift(): return lax.ppermute(value, 'dom', pairs)  18.7 us
    pallas_call x1, Pallas kernels, incidence(): pl.pallas_call(functools.partial(incidence_kernel, len(after)), grid=(gro...  16.9 us
    all_to_all x2, starting transfers between devices, exchange(): lax.all_to_all(blocks, 'dom', split_axis=0, concat_axis=0, tiled=True, ax...  14 us
    all_to_all x1, starting transfers between devices, shards(): lax.all_to_all(outgoing.reshape(parts, -1, half), 'dom', split_axis=0, co...  13.6 us
    ppermute x7, starting transfers between devices, shift(): return lax.ppermute(value, 'dom', pairs)  10.3 us
    all_to_all x2, waiting for transfers between devices, exchange(): lax.all_to_all(blocks, 'dom', split_axis=0, concat_axis=0, tiled=True, ax...  9.81 us
  transfers between devices with their start and end apart: 15, of which 9 were waited for; matrix products, arithmetic and copies ran while one was open for 15% of the time, Pallas kernels for 10%

profile of v6, /device:TPU:8, one launch (start us, length us, event | category | flops | bytes accessed | tf_op | source)
XLA Modules:
  0.0 177.1 jit_solution(12493617012299767920)
XLA Ops:
  0.6 1.4 convolution_convert_fusion
  2.1 0.7 broadcast_in_dim.11
  2.7 8.5 %all-to-all-start = ((bf16[8,32,256]{2,1,0:T(8,128)(2,1)}), bf16[8,32,256]{2,1,0:T(8,128)(2,1)S(1)}, u32[]{:S(2)}, u32[]{:S(2)}) async-start(bf16[8,32,256]{2,1,0:T(8,128)(2,1)} %broadcast_in_dim.11), calls=%async_computation | async-start | bytes 262144 | tf_op jit(solution)/shard_map/all_to_all | solution.py:163
  11.2 0.8 copy.17
  12.0 0.1 eq.35
  12.1 7.1 %fusion.2 = bf16[4096,256]{1,0:T(8,128)(2,1)} fusion(bf16[1536,256]{1,0:T(8,128)(2,1)} %own.1, s32[4096]{0:T(1024)S(1)} %eq.35), kind=kOutput, calls=%fused_computation.3 | convolution fusion | flops 3228565504 | bytes 2899968 | tf_op jit(solution)/shard_map/dot_general | solution.py:203
  19.2 1.1 all-to-all-done
  20.3 0.0 copy-start.15
  20.3 13.6 %all-to-all-start.1 = ((bf16[128,32,256]{2,1,0:T(8,128)(2,1)}), bf16[128,32,256]{2,1,0:T(8,128)(2,1)}, u32[]{:S(2)}, u32[]{:S(2)}) async-start(bf16[128,32,256]{2,1,0:T(8,128)(2,1)} %bitcast.6), calls=%async_computation.1 | async-start | bytes 4194304 | tf_op jit(solution)/shard_map/all_to_all | solution.py:219
  34.0 0.1 collective-permute-start
  34.1 0.5 collective-permute-start.4
  34.6 1.5 collective-permute-start.3
  36.0 1.6 collective-permute-start.2
  37.6 1.7 collective-permute-start.1
  39.3 0.1 bitcast_select_fusion
  39.4 4.1 %collective-permute-done.3 = bf16[256,256]{1,0:T(8,128)(2,1)S(1)} collective-permute-done((bf16[256,256]{1,0:T(8,128)(2,1)S(1)}, bf16[256,256]{1,0:T(8,128)(2,1)S(1)}, u32[]{:S(2)}, u32[]{:S(2)}) %collective-permute-start.3) | collective-permute-done | bytes 131104 | tf_op jit(solution)/shard_map/ppermute | solution.py:145
  43.5 0.0 collective-permute-start.5
  43.5 3.4 %collective-permute-done.2 = bf16[256,256]{1,0:T(8,128)(2,1)S(1)} collective-permute-done((bf16[256,256]{1,0:T(8,128)(2,1)S(1)}, bf16[256,256]{1,0:T(8,128)(2,1)S(1)}, u32[]{:S(2)}, u32[]{:S(2)}) %collective-permute-start.2) | collective-permute-done | bytes 131104 | tf_op jit(solution)/shard_map/ppermute | solution.py:145
  46.9 3.9 %collective-permute-done.1 = bf16[256,256]{1,0:T(8,128)(2,1)S(1)} collective-permute-done((bf16[256,256]{1,0:T(8,128)(2,1)S(1)}, bf16[256,256]{1,0:T(8,128)(2,1)S(1)}, u32[]{:S(2)}, u32[]{:S(2)}) %collective-permute-start.1) | collective-permute-done | bytes 131104 | tf_op jit(solution)/shard_map/ppermute | solution.py:145
  50.8 0.8 pad_maximum_fusion.refs_0_
  51.6 1.9 %collective-permute-start.6 = (bf16[1024,256]{1,0:T(8,128)(2,1)}, bf16[1024,256]{1,0:T(8,128)(2,1)}, u32[]{:S(2)}, u32[]{:S(2)}) collective-permute-start(bf16[1024,256]{1,0:T(8,128)(2,1)} %pad_maximum_fusion.refs_0_), channel_id=1, source_target_pairs={{0,192},{2,194},{4,196},{6,198},{8,200},{10,202},{12,204},{14,206}... | collective-permute-start | bytes 1572872 | tf_op jit(solution)/shard_map/ppermute | solution.py:145
  53.6 0.7 pad_select_fusion
  54.2 1.2 reshape.62
  55.4 0.9 copy.15
  56.3 1.7 copy.16.slots_ref
  58.0 0.1 collective-permute-start.8
  58.1 0.9 constant_dynamic-update-slice_fusion.6
  59.0 0.9 constant_dynamic-update-slice_fusion.5
  59.9 0.0 collective-permute-done.4.refs_2_.w_self_far
  60.0 0.0 copy-start.3
  60.0 0.0 collective-permute-done.5.refs_3_.w_neigh_far
  60.0 0.0 collective-permute-done.refs_1_.own_far
  60.0 0.7 copy-done.3
  60.7 0.1 copy-done.5
  60.7 0.9 copy-done.1
  61.6 16.9 %incidence.1 = (bf16[1536,1536]{1,0:T(8,128)(2,1)}, bf16[1536,4096]{1,0:T(8,128)(2,1)}, bf16[1536,4096]{1,0:T(8,128)(2,1)}) custom-call(s32[96,256]{1,0:T(8,128)} %copy.16.slots_ref, bf16[1024,256]{1,0:T(8,128)(2,1)} %pad_maximum_fusion.refs_0_, bf16[1536,256]{1,0:T(8,128)(2,1)} %copy-done.1, bf16[256,512]{1,0:T(8,128)(2,1)} %copy-done.3, ...), custom_call_target="tpu_custom_call" | custom-call | flops 1536 | bytes 1536 | tf_op jit(solution)/shard_map/incidence/pallas_call | solution.py:53
  78.5 1.2 slice.36
  80.3 1.0 slice_add_fusion.1
  81.3 3.2 %collective-permute-start.7 = (bf16[512,256]{1,0:T(8,128)(2,1)S(1)}, bf16[512,256]{1,0:T(8,128)(2,1)S(1)}, u32[]{:S(2)}, u32[]{:S(2)}) collective-permute-start(bf16[512,256]{1,0:T(8,128)(2,1)S(1)} %slice_add_fusion.1), channel_id=1, source_target_pairs={{0,192},{2,194},{4,196},{6,198},{8,200},{10,202},{12,204},{14,206}... | collective-permute-start | bytes 786440 | tf_op jit(solution)/shard_map/ppermute | solution.py:145
  84.5 0.0 collective-permute-done.8
  84.5 0.3 collective-permute-start.9
  84.8 1.1 constant_dynamic-update-slice_fusion.3
  85.9 3.6 %collective-permute-done.7 = bf16[512,256]{1,0:T(8,128)(2,1)S(1)} collective-permute-done((bf16[512,256]{1,0:T(8,128)(2,1)S(1)}, bf16[512,256]{1,0:T(8,128)(2,1)S(1)}, u32[]{:S(2)}, u32[]{:S(2)}) %collective-permute-start.7) | collective-permute-done | bytes 262176 | tf_op jit(solution)/shard_map/ppermute | solution.py:145
  89.5 3.7 %collective-permute-done.9 = bf16[512,256]{1,0:T(8,128)(2,1)S(1)} collective-permute-done((bf16[512,256]{1,0:T(8,128)(2,1)S(1)}, bf16[512,256]{1,0:T(8,128)(2,1)S(1)}, u32[]{:S(2)}, u32[]{:S(2)}) %collective-permute-start.9) | collective-permute-done | bytes 262176 | tf_op jit(solution)/shard_map/ppermute | solution.py:145
  93.3 7.6 %fusion.10 = f32[1536,256]{1,0:T(8,128)} fusion(bf16[1536,4096]{1,0:T(8,128)(2,1)} %get-tuple-element.10, bf16[4096,256]{1,0:T(8,128)(2,1)S(1)} %constant_dynamic-update-slice_fusion), kind=kOutput, calls=%fused_computation.40 | convolution fusion | flops 3221225472 | bytes 16252928 | tf_op jit(solution)/shard_map/dot_general | solution.py:203
  100.8 0.0 all-to-all-done.1
  100.8 7.1 %fusion.11 = f32[1536,256]{1,0:T(8,128)S(1)} fusion(bf16[1536,4096]{1,0:T(8,128)(2,1)} %get-tuple-element.11, bf16[4096,256]{1,0:T(8,128)(2,1)} %bitcast.7), kind=kOutput, calls=%fused_computation.41 | convolution fusion | flops 3221225472 | bytes 16252928 | tf_op jit(solution)/shard_map/dot_general | solution.py:203
  108.0 0.0 copy-start.2
  108.0 0.0 copy-start.4
  108.0 0.0 copy-start.7
  108.0 4.9 %fusion.5.mean = bf16[1536,256]{1,0:T(8,128)(2,1)} fusion(f32[1536,256]{1,0:T(8,128)S(1)} %fusion.11, f32[1536,256]{1,0:T(8,128)S(1)} %copy-done.16, bf16[1536,1536]{1,0:T(8,128)(2,1)} %get-tuple-element.9, bf16[1536,256]{1,0:T(8,128)(2,1)S(1)} %copy-done, f32[1536]{0:T(1024)S(1)} %convert_element_type.33), kind=kOutput, calls=%fused_computation.7 | convolution fusion | flops 1209532416 | bytes 9443328 | tf_op jit(solution)/shard_map/dot_general | solution.py:203
  112.9 2.6 %collective-permute-done.10.mean_far = bf16[1536,256]{1,0:T(8,128)(2,1)} collective-permute-done((bf16[1536,256]{1,0:T(8,128)(2,1)}, bf16[1536,256]{1,0:T(8,128)(2,1)}, u32[]{:S(2)}, u32[]{:S(2)}) %collective-permute-start.10) | collective-permute-done | bytes 786464 | tf_op jit(solution)/shard_map/ppermute | solution.py:136
  115.6 8.4 %layer.1 = (bf16[1536,256]{1,0:T(8,128)(2,1)}, bf16[512,256]{1,0:T(8,128)(2,1)S(1)}, bf16[512,256]{1,0:T(8,128)(2,1)S(1)}) custom-call(s32[1]{0:T(128)} %bitcast.core_ref, bf16[1536,256]{1,0:T(8,128)(2,1)S(1)} %copy-done, bf16[1536,256]{1,0:T(8,128)(2,1)S(1)} %copy-done.2, bf16[1536,256]{1,0:T(8,128)(2,1)} %fusion.5.mean, ...), custom_call_target="tpu_custom_call" | custom-call | flops 1610612736 | bytes 4718592 | tf_op jit(solution)/shard_map/layer/pallas_call | solution.py:113
  123.9 0.1 collective-permute-start.11
  124.1 1.4 collective-permute-done.11
  125.5 15.3 %all_to_all.25 = bf16[16,64,256]{2,1,0:T(8,128)(2,1)S(1)} all-to-all(bf16[16,64,256]{2,1,0:T(8,128)(2,1)S(1)} %bitcast.44), channel_id=1, replica_groups={{0,16,32,48,64,80,96,112,128,144,160,176,192,208,224,240},{2,18,34,50,6..., dimensions={0} | all-to-all | bytes 1048576 | tf_op jit(solution)/shard_map/all_to_all | solution.py:163
  140.8 0.1 reduce_sum.21
  140.9 19.6 %all_to_all.26 = bf16[8,64,256]{2,1,0:T(8,128)(2,1)S(1)} all-to-all(bf16[8,64,256]{2,1,0:T(8,128)(2,1)S(1)} %broadcast_in_dim.12), channel_id=1, replica_groups={{0,2,4,6,8,10,12,14},{16,18,20,22,24,26,28,30},{32,34,36,38,40,42,44,46..., dimensions={0} | all-to-all | bytes 524288 | tf_op jit(solution)/shard_map/all_to_all | solution.py:163
  160.5 0.8 broadcast_in_dim.13
  161.4 5.6 %all-to-all-start.4 = ((bf16[16,64,256]{2,1,0:T(8,128)(2,1)}), bf16[16,64,256]{2,1,0:T(8,128)(2,1)S(1)}, u32[]{:S(2)}, u32[]{:S(2)}) async-start(bf16[16,64,256]{2,1,0:T(8,128)(2,1)} %broadcast_in_dim.13), calls=%async_computation.4 | async-start | bytes 1048576 | tf_op jit(solution)/shard_map/all_to_all | solution.py:163
  167.0 8.7 %all-to-all-done.4 = bf16[16,64,256]{2,1,0:T(8,128)(2,1)S(1)} async-done(((bf16[16,64,256]{2,1,0:T(8,128)(2,1)}), bf16[16,64,256]{2,1,0:T(8,128)(2,1)S(1)}, u32[]{:S(2)}, u32[]{:S(2)}) %all-to-all-start.4) | async-done | bytes 524320 | tf_op jit(solution)/shard_map/all_to_all | solution.py:163
  175.7 0.1 convert_element_type.37
  175.8 0.1 slice_select_fusion.1
  176.0 1.1 pad_maximum_fusion.2
  (41 shorter events, 0.3 us)
Async XLA Ops:
  2.7 17.6 %all-to-all-start = ((bf16[8,32,256]{2,1,0:T(8,128)(2,1)}), bf16[8,32,256]{2,1,0:T(8,128)(2,1)S(1)}, u32[]{:S(2)}, u32[]{:S(2)}) async-start(bf16[8,32,256]{2,1,0:T(8,128)(2,1)} %broadcast_in_dim.11), calls=%async_computation | async-start | bytes 262144 | tf_op jit(solution)/shard_map/all_to_all | solution.py:163
  20.3 13.7 %copy-start = (bf16[1536,256]{1,0:T(8,128)(2,1)S(1)}, bf16[1536,256]{1,0:T(8,128)(2,1)}, u32[]{:S(2)}) copy-start(bf16[1536,256]{1,0:T(8,128)(2,1)} %own.1) | copy-start | bytes 2359300
  20.3 13.8 %copy-start.8 = (bf16[256,512]{1,0:T(8,128)(2,1)S(1)}, bf16[256,512]{1,0:T(8,128)(2,1)}, u32[]{:S(2)}) copy-start(bf16[256,512]{1,0:T(8,128)(2,1)} %w_self.1) | copy-start | bytes 786436
  20.3 19.0 %copy-start.14 = (s32[1536,12]{0,1:T(8,128)S(1)}, s32[1536,12]{0,1:T(8,128)}, u32[]{:S(2)}) copy-start(s32[1536,12]{0,1:T(8,128)} %param.14) | copy-start | bytes 221188
  20.3 23.2 %copy-start.9 = (bf16[256,512]{1,0:T(8,128)(2,1)S(1)}, bf16[256,512]{1,0:T(8,128)(2,1)}, u32[]{:S(2)}) copy-start(bf16[256,512]{1,0:T(8,128)(2,1)} %w_neigh.1) | copy-start | bytes 786436
  20.3 33.3 %copy-start.15 = (s32[1536]{0:T(1024)S(1)}, s32[1536]{0:T(1024)}, u32[]{:S(2)}) copy-start(s32[1536]{0:T(1024)} %param.15) | copy-start | bytes 18436
  20.3 80.5 %all-to-all-start.1 = ((bf16[128,32,256]{2,1,0:T(8,128)(2,1)}), bf16[128,32,256]{2,1,0:T(8,128)(2,1)}, u32[]{:S(2)}, u32[]{:S(2)}) async-start(bf16[128,32,256]{2,1,0:T(8,128)(2,1)} %bitcast.6), calls=%async_computation.1 | async-start | bytes 4194304 | tf_op jit(solution)/shard_map/all_to_all | solution.py:219
  34.0 26.0 %collective-permute-start = (bf16[1536,256]{1,0:T(8,128)(2,1)S(1)}, bf16[1536,256]{1,0:T(8,128)(2,1)S(1)}, u32[]{:S(2)}, u32[]{:S(2)}) collective-permute-start(bf16[1536,256]{1,0:T(8,128)(2,1)S(1)} %copy-done), channel_id=1, source_target_pairs={{0,1},{1,0},{2,3},{3,2},{4,5},{5,4},{6,7},{7,6},{8,9},{9,8},{10,11... | collective-permute-start | bytes 2359304 | tf_op jit(solution)/shard_map/ppermute | solution.py:136
  34.1 25.9 %collective-permute-start.4 = (bf16[256,512]{1,0:T(8,128)(2,1)S(1)}, bf16[256,512]{1,0:T(8,128)(2,1)S(1)}, u32[]{:S(2)}, u32[]{:S(2)}) collective-permute-start(bf16[256,512]{1,0:T(8,128)(2,1)S(1)} %copy-done.8), channel_id=1, source_target_pairs={{0,1},{1,0},{2,3},{3,2},{4,5},{5,4},{6,7},{7,6},{8,9},{9,8},{10,11... | collective-permute-start | bytes 786440 | tf_op jit(solution)/shard_map/ppermute | solution.py:136
  34.6 8.9 %collective-permute-start.3 = (bf16[256,256]{1,0:T(8,128)(2,1)S(1)}, bf16[256,256]{1,0:T(8,128)(2,1)S(1)}, u32[]{:S(2)}, u32[]{:S(2)}) collective-permute-start(bf16[256,256]{1,0:T(8,128)(2,1)S(1)} %bitcast.45), channel_id=1, source_target_pairs={{0,16},{2,18},{4,20},{6,22},{8,24},{10,26},{12,28},{14,30},{16,32}... | collective-permute-start | bytes 393224 | tf_op jit(solution)/shard_map/ppermute | solution.py:145
  36.0 10.8 %collective-permute-start.2 = (bf16[256,256]{1,0:T(8,128)(2,1)S(1)}, bf16[256,256]{1,0:T(8,128)(2,1)S(1)}, u32[]{:S(2)}, u32[]{:S(2)}) collective-permute-start(bf16[256,256]{1,0:T(8,128)(2,1)S(1)} %bitcast.46), channel_id=1, source_target_pairs={{0,32},{2,34},{4,36},{6,38},{8,40},{10,42},{12,44},{14,46},{16,48}... | collective-permute-start | bytes 393224 | tf_op jit(solution)/shard_map/ppermute | solution.py:145
  37.6 13.2 %collective-permute-start.1 = (bf16[256,256]{1,0:T(8,128)(2,1)S(1)}, bf16[256,256]{1,0:T(8,128)(2,1)S(1)}, u32[]{:S(2)}, u32[]{:S(2)}) collective-permute-start(bf16[256,256]{1,0:T(8,128)(2,1)S(1)} %bitcast.47), channel_id=1, source_target_pairs={{0,48},{2,50},{4,52},{6,54},{8,56},{10,58},{12,60},{14,62},{16,0},... | collective-permute-start | bytes 393224 | tf_op jit(solution)/shard_map/ppermute | solution.py:145
  43.5 10.8 %copy-start.10 = (bf16[256,256]{1,0:T(8,128)(2,1)}, bf16[256,256]{1,0:T(8,128)(2,1)S(1)}, u32[]{:S(2)}) copy-start(bf16[256,256]{1,0:T(8,128)(2,1)S(1)} %collective-permute-done.3) | copy-start | bytes 393220
  43.5 16.5 %collective-permute-start.5 = (bf16[256,512]{1,0:T(8,128)(2,1)S(1)}, bf16[256,512]{1,0:T(8,128)(2,1)S(1)}, u32[]{:S(2)}, u32[]{:S(2)}) collective-permute-start(bf16[256,512]{1,0:T(8,128)(2,1)S(1)} %copy-done.9), channel_id=1, source_target_pairs={{0,1},{1,0},{2,3},{3,2},{4,5},{5,4},{6,7},{7,6},{8,9},{9,8},{10,11... | collective-permute-start | bytes 786440 | tf_op jit(solution)/shard_map/ppermute | solution.py:136
  46.9 7.3 %copy-start.12 = (bf16[256,256]{1,0:T(8,128)(2,1)}, bf16[256,256]{1,0:T(8,128)(2,1)S(1)}, u32[]{:S(2)}) copy-start(bf16[256,256]{1,0:T(8,128)(2,1)S(1)} %collective-permute-done.2) | copy-start | bytes 393220
  50.8 3.4 %copy-start.13 = (bf16[256,256]{1,0:T(8,128)(2,1)}, bf16[256,256]{1,0:T(8,128)(2,1)S(1)}, u32[]{:S(2)}) copy-start(bf16[256,256]{1,0:T(8,128)(2,1)S(1)} %collective-permute-done.1) | copy-start | bytes 393220
  51.6 28.7 %collective-permute-start.6 = (bf16[1024,256]{1,0:T(8,128)(2,1)}, bf16[1024,256]{1,0:T(8,128)(2,1)}, u32[]{:S(2)}, u32[]{:S(2)}) collective-permute-start(bf16[1024,256]{1,0:T(8,128)(2,1)} %pad_maximum_fusion.refs_0_), channel_id=1, source_target_pairs={{0,192},{2,194},{4,196},{6,198},{8,200},{10,202},{12,204},{14,206}... | collective-permute-start | bytes 1572872 | tf_op jit(solution)/shard_map/ppermute | solution.py:145
  56.3 28.5 %copy-start.11 = (bf16[256,256]{1,0:T(8,128)(2,1)S(1)}, bf16[256,256]{1,0:T(8,128)(2,1)}, u32[]{:S(2)}) copy-start(bf16[256,256]{1,0:T(8,128)(2,1)} %copy-done.10) | copy-start | bytes 393220
  58.0 26.5 %collective-permute-start.8 = (bf16[1024,256]{1,0:T(8,128)(2,1)}, bf16[1024,256]{1,0:T(8,128)(2,1)S(1)}, u32[]{:S(2)}, u32[]{:S(2)}) collective-permute-start(bf16[1024,256]{1,0:T(8,128)(2,1)} %pad_maximum_fusion.refs_0_), channel_id=1, source_target_pairs={{0,64},{2,66},{4,68},{6,70},{8,72},{10,74},{12,76},{14,78},{16,80}... | collective-permute-start | bytes 1572872 | tf_op jit(solution)/shard_map/ppermute | solution.py:145
  60.0 0.7 copy-start.3
  60.0 0.8 copy-start.5
  60.7 0.9 copy-start.1
  81.3 8.2 %collective-permute-start.7 = (bf16[512,256]{1,0:T(8,128)(2,1)S(1)}, bf16[512,256]{1,0:T(8,128)(2,1)S(1)}, u32[]{:S(2)}, u32[]{:S(2)}) collective-permute-start(bf16[512,256]{1,0:T(8,128)(2,1)S(1)} %slice_add_fusion.1), channel_id=1, source_target_pairs={{0,192},{2,194},{4,196},{6,198},{8,200},{10,202},{12,204},{14,206}... | collective-permute-start | bytes 786440 | tf_op jit(solution)/shard_map/ppermute | solution.py:145
  84.5 8.7 %collective-permute-start.9 = (bf16[512,256]{1,0:T(8,128)(2,1)S(1)}, bf16[512,256]{1,0:T(8,128)(2,1)S(1)}, u32[]{:S(2)}, u32[]{:S(2)}) collective-permute-start(bf16[512,256]{1,0:T(8,128)(2,1)S(1)} %slice_add_fusion), channel_id=1, source_target_pairs={{0,64},{2,66},{4,68},{6,70},{8,72},{10,74},{12,76},{14,78},{16,80}... | collective-permute-start | bytes 786440 | tf_op jit(solution)/shard_map/ppermute | solution.py:145
  100.8 7.2 %copy-start.16 = (f32[1536,256]{1,0:T(8,128)S(1)}, f32[1536,256]{1,0:T(8,128)}, u32[]{:S(2)}) copy-start(f32[1536,256]{1,0:T(8,128)} %fusion.10) | copy-start | bytes 4718596
  108.0 7.5 %copy-start.2 = (bf16[1536,256]{1,0:T(8,128)(2,1)S(1)}, bf16[1536,256]{1,0:T(8,128)(2,1)}, u32[]{:S(2)}) copy-start(bf16[1536,256]{1,0:T(8,128)(2,1)} %copy-done.1) | copy-start | bytes 2359300
  108.0 7.5 %copy-start.4 = (bf16[256,512]{1,0:T(8,128)(2,1)S(1)}, bf16[256,512]{1,0:T(8,128)(2,1)}, u32[]{:S(2)}) copy-start(bf16[256,512]{1,0:T(8,128)(2,1)} %copy-done.3) | copy-start | bytes 786436
  108.0 7.5 %copy-start.6 = (bf16[256,512]{1,0:T(8,128)(2,1)S(1)}, bf16[256,512]{1,0:T(8,128)(2,1)}, u32[]{:S(2)}) copy-start(bf16[256,512]{1,0:T(8,128)(2,1)} %copy-done.5) | copy-start | bytes 786436
  108.0 7.5 %copy-start.7 = (bf16[1536,256]{1,0:T(8,128)(2,1)S(1)}, bf16[1536,256]{1,0:T(8,128)(2,1)}, u32[]{:S(2)}) copy-start(bf16[1536,256]{1,0:T(8,128)(2,1)} %cotangent_ref.1) | copy-start | bytes 2359300
  112.9 2.6 %collective-permute-start.10 = (bf16[1536,256]{1,0:T(8,128)(2,1)}, bf16[1536,256]{1,0:T(8,128)(2,1)}, u32[]{:S(2)}, u32[]{:S(2)}) collective-permute-start(bf16[1536,256]{1,0:T(8,128)(2,1)} %fusion.5.mean), channel_id=1, source_target_pairs={{0,1},{1,0},{2,3},{3,2},{4,5},{5,4},{6,7},{7,6},{8,9},{9,8},{10,11... | collective-permute-start | bytes 2359304 | tf_op jit(solution)/shard_map/ppermute | solution.py:136
  123.9 1.5 collective-permute-start.11
  161.4 14.3 %all-to-all-start.4 = ((bf16[16,64,256]{2,1,0:T(8,128)(2,1)}), bf16[16,64,256]{2,1,0:T(8,128)(2,1)S(1)}, u32[]{:S(2)}, u32[]{:S(2)}) async-start(bf16[16,64,256]{2,1,0:T(8,128)(2,1)} %broadcast_in_dim.13), calls=%async_computation.4 | async-start | bytes 1048576 | tf_op jit(solution)/shard_map/all_to_all | solution.py:163

commit v7 on v6

--- a/solution.py
+++ b/solution.py
@@ -214,8 +214,9 @@
         onehot = (rows[:, None] == lanes).astype(jnp.bfloat16)
         return dot(onehot, features).astype(jnp.bfloat16)
 
-    outgoing = pick(send_rows.reshape(-1))
-    plane = spread_y(share(pick(hub_rows), "z").reshape(-1, half))
+    line = share(pick(hub_rows), "z").reshape(-1, half)
+    plane = spread_y(line)
+    outgoing = pick(send_rows.reshape(-1) + nothing(line).astype(jnp.int32))
     incoming = lax.all_to_all(
         outgoing.reshape(parts, -1, half), "dom", split_axis=0, concat_axis=0, tiled=True
     ).reshape(-1, half)
@@ -226,7 +227,8 @@
         slots, (nodes, hubs, incoming.shape[0]), (plane, features_far, w_self_far, w_neigh_far)
     )
     table = spread_x(plane, after, before, own_weight)
-    total = dot(own_weight, features) + dot(hub_weight, table) + dot(far_weight, incoming)
+    near_sum = lax.optimization_barrier(dot(own_weight, features) + dot(hub_weight, table))
+    total = near_sum + dot(far_weight, incoming)
     neigh_mean = (total / counts[:, None].astype(jnp.float32)).astype(jnp.bfloat16)
     mean_far = swap(neigh_mean)
     layer_out, mine, other = layer(

time: 178 us -> 169 us (0.949)
  starting transfers between devices: 38.6 us -> 34.2 us
  blocking collectives: 34.9 us -> 30.9 us
  matrix products: 28.1 us -> 24.9 us
    all_to_all x2, waiting for transfers between devices: 9.81 us -> 17.3 us  [exchange(): lax.all_to_all(blocks, 'dom', split_axis=0, concat_axis=0, tiled=True, ax...]
    ppermute x7, waiting for transfers between devices: 18.7 us -> 12.5 us  [shift(): return lax.ppermute(value, 'dom', pairs)]
    all_to_all x1, starting transfers between devices: 13.6 us -> 7.79 us  [shards(): lax.all_to_all(outgoing.reshape(parts, -1, half), 'dom', split_axis=0, co...]
    all_to_all x2, blocking collectives: 34.9 us -> 30.9 us  [exchange(): lax.all_to_all(blocks, 'dom', split_axis=0, concat_axis=0, tiled=True, ax...]
    dot_general x5, matrix products: 28.1 us -> 24.9 us  [dot(): return jnp.dot(left, right, preferred_element_type=jnp.float32)]
    unnamed x42 -> x43, local copies, waits for them, and re-layouts: 5.47 us -> 5.26 us
  transfers between devices with their start and end apart: 15 -> 15, of which waited for: 9 -> 6; matrix products, arithmetic and copies ran while one was open for 15% -> 16% of each run, Pallas kernels for 10% -> 10%
where the time goes in v7:
time: 169 us; the launch traced here: 168 us
  starting transfers between devices  34.2 us (20%)
  waiting for transfers between devices  33.6 us (20%)
  blocking collectives  30.9 us (18%)
  Pallas kernels  25.2 us (15%)
  matrix products  24.9 us (15%)
  local copies, waits for them, and re-layouts  12.5 us (7%)
  other arithmetic  4.35 us (3%)
  between operations  2.42 us (1%)
    all_to_all x2, blocking collectives, exchange(): lax.all_to_all(blocks, 'dom', split_axis=0, concat_axis=0, tiled=True, ax...  30.9 us
    dot_general x5, matrix products, dot(): return jnp.dot(left, right, preferred_element_type=jnp.float32)  24.9 us
    all_to_all x2, waiting for transfers between devices, exchange(): lax.all_to_all(blocks, 'dom', split_axis=0, concat_axis=0, tiled=True, ax...  17.3 us
    pallas_call x1, Pallas kernels, incidence(): pl.pallas_call(functools.partial(incidence_kernel, len(after)), grid=(gro...  16.9 us
    all_to_all x2, starting transfers between devices, exchange(): lax.all_to_all(blocks, 'dom', split_axis=0, concat_axis=0, tiled=True, ax...  13.7 us
    ppermute x7, waiting for transfers between devices, shift(): return lax.ppermute(value, 'dom', pairs)  12.5 us
    ppermute x7, starting transfers between devices, shift(): return lax.ppermute(value, 'dom', pairs)  11.9 us
    pallas_call x1, Pallas kernels, layer(): pl.pallas_call(layer_kernel, grid_spec=pltpu.PrefetchScalarGridSpec(num_s...  8.26 us
  transfers between devices with their start and end apart: 15, of which 6 were waited for; matrix products, arithmetic and copies ran while one was open for 16% of the time, Pallas kernels for 10%

profile of v7, /device:TPU:8, one launch (start us, length us, event | category | flops | bytes accessed | tf_op | source)
XLA Modules:
  0.0 168.1 jit_solution(14586310193276588109)
XLA Ops:
  0.6 1.4 convolution_convert_fusion
  2.1 0.7 broadcast_in_dim.11
  2.7 8.5 %all-to-all-start = ((bf16[8,32,256]{2,1,0:T(8,128)(2,1)}), bf16[8,32,256]{2,1,0:T(8,128)(2,1)S(1)}, u32[]{:S(2)}, u32[]{:S(2)}) async-start(bf16[8,32,256]{2,1,0:T(8,128)(2,1)} %broadcast_in_dim.11), calls=%async_computation | async-start | bytes 262144 | tf_op jit(solution)/shard_map/all_to_all | solution.py:163
  11.2 0.0 collective-permute-start
  11.2 0.5 collective-permute-start.4
  11.7 8.6 %all-to-all-done = bf16[8,32,256]{2,1,0:T(8,128)(2,1)S(1)} async-done(((bf16[8,32,256]{2,1,0:T(8,128)(2,1)}), bf16[8,32,256]{2,1,0:T(8,128)(2,1)S(1)}, u32[]{:S(2)}, u32[]{:S(2)}) %all-to-all-start) | async-done | bytes 131104 | tf_op jit(solution)/shard_map/all_to_all | solution.py:163
  20.3 1.6 collective-permute-start.3
  21.9 0.9 collective-permute-start.2
  22.8 2.4 %collective-permute-start.1 = (bf16[256,256]{1,0:T(8,128)(2,1)S(1)}, bf16[256,256]{1,0:T(8,128)(2,1)}, u32[]{:S(2)}, u32[]{:S(2)}) collective-permute-start(bf16[256,256]{1,0:T(8,128)(2,1)S(1)} %bitcast.49), channel_id=1, source_target_pairs={{0,48},{2,50},{4,52},{6,54},{8,56},{10,58},{12,60},{14,62},{16,0},... | collective-permute-start | bytes 393224 | tf_op jit(solution)/shard_map/ppermute | solution.py:145
  25.2 0.5 slice.50
  26.4 0.7 broadcast_add_fusion
  27.1 0.1 copy.17
  27.2 0.1 add.50
  27.3 7.1 %fusion.2 = bf16[4096,256]{1,0:T(8,128)(2,1)} fusion(bf16[1536,256]{1,0:T(8,128)(2,1)} %own.1, s32[4096]{0:T(1024)S(1)} %add.50), kind=kOutput, calls=%fused_computation.3 | convolution fusion | flops 3228565504 | bytes 2899968 | tf_op jit(solution)/shard_map/dot_general | solution.py:203
  34.5 7.8 %all-to-all-start.1 = ((bf16[128,32,256]{2,1,0:T(8,128)(2,1)}), bf16[128,32,256]{2,1,0:T(8,128)(2,1)}, u32[]{:S(2)}, u32[]{:S(2)}) async-start(bf16[128,32,256]{2,1,0:T(8,128)(2,1)} %bitcast.7), calls=%async_computation.1 | async-start | bytes 4194304 | tf_op jit(solution)/shard_map/all_to_all | solution.py:220
  42.3 0.1 bitcast_select_fusion
  42.4 0.1 collective-permute-start.5
  42.5 0.0 collective-permute-done.2
  42.5 0.5 copy-done.12
  43.0 1.0 pad_maximum_fusion.refs_0_
  44.0 0.0 copy-start.10
  44.0 3.4 %collective-permute-start.6 = (bf16[1024,256]{1,0:T(8,128)(2,1)S(1)}, bf16[1024,256]{1,0:T(8,128)(2,1)S(1)}, u32[]{:S(2)}, u32[]{:S(2)}) collective-permute-start(bf16[1024,256]{1,0:T(8,128)(2,1)S(1)} %pad_maximum_fusion.refs_0_), channel_id=1, source_target_pairs={{0,192},{2,194},{4,196},{6,198},{8,200},{10,202},{12,204},{14,206}... | collective-permute-start | bytes 1572872 | tf_op jit(solution)/shard_map/ppermute | solution.py:145
  47.4 0.7 pad_select_fusion
  48.1 1.2 reshape.74
  49.3 0.9 copy.15
  50.2 1.7 copy.16.slots_ref
  51.8 0.0 collective-permute-start.8
  51.9 0.9 constant_dynamic-update-slice_fusion.6
  52.8 0.9 constant_dynamic-update-slice_fusion.5
  53.7 0.0 copy-start.3
  53.7 0.0 collective-permute-done.5.refs_3_.w_neigh_far
  53.8 0.7 copy-done.3
  54.4 0.1 copy-done.5
  54.5 0.9 copy-done.1
  55.4 16.9 %incidence.1 = (bf16[1536,1536]{1,0:T(8,128)(2,1)}, bf16[1536,4096]{1,0:T(8,128)(2,1)}, bf16[1536,4096]{1,0:T(8,128)(2,1)}) custom-call(s32[96,256]{1,0:T(8,128)} %copy.16.slots_ref, bf16[1024,256]{1,0:T(8,128)(2,1)} %copy-done.10, bf16[1536,256]{1,0:T(8,128)(2,1)} %copy-done.1, bf16[256,512]{1,0:T(8,128)(2,1)} %copy-done.3, bf16[256,512]{1,0:T(8,128)(2,1)} %copy-done.5), custom_call_target="tpu_custom_call" | custom-call | flops 1536 | bytes 1536 | tf_op jit(solution)/shard_map/incidence/pallas_call | solution.py:53
  72.3 1.1 slice.39
  74.1 3.3 %collective-permute-start.7 = (bf16[512,256]{1,0:T(8,128)(2,1)S(1)}, bf16[512,256]{1,0:T(8,128)(2,1)S(1)}, u32[]{:S(2)}, u32[]{:S(2)}) collective-permute-start(bf16[512,256]{1,0:T(8,128)(2,1)S(1)} %slice_add_fusion.1), channel_id=1, source_target_pairs={{0,192},{2,194},{4,196},{6,198},{8,200},{10,202},{12,204},{14,206}... | collective-permute-start | bytes 786440 | tf_op jit(solution)/shard_map/ppermute | solution.py:145
  77.5 0.3 collective-permute-start.9
  77.8 8.4 %collective-permute-done.7 = bf16[512,256]{1,0:T(8,128)(2,1)S(1)} collective-permute-done((bf16[512,256]{1,0:T(8,128)(2,1)S(1)}, bf16[512,256]{1,0:T(8,128)(2,1)S(1)}, u32[]{:S(2)}, u32[]{:S(2)}) %collective-permute-start.7) | collective-permute-done | bytes 262176 | tf_op jit(solution)/shard_map/ppermute | solution.py:145
  86.2 4.1 %collective-permute-done.9 = bf16[512,256]{1,0:T(8,128)(2,1)S(1)} collective-permute-done((bf16[512,256]{1,0:T(8,128)(2,1)S(1)}, bf16[512,256]{1,0:T(8,128)(2,1)S(1)}, u32[]{:S(2)}, u32[]{:S(2)}) %collective-permute-start.9) | collective-permute-done | bytes 262176 | tf_op jit(solution)/shard_map/ppermute | solution.py:145
  90.4 0.0 copy-start
  90.4 6.6 %fusion.7 = f32[1536,256]{1,0:T(8,128)S(1)} fusion(bf16[1536,4096]{1,0:T(8,128)(2,1)} %get-tuple-element.10, bf16[4096,256]{1,0:T(8,128)(2,1)S(1)} %constant_dynamic-update-slice_fusion), kind=kOutput, calls=%fused_computation.39 | convolution fusion | flops 3221225472 | bytes 16252928 | tf_op jit(solution)/shard_map/dot_general | solution.py:203
  97.0 2.6 %convolution_add_fusion = f32[1536,256]{1,0:T(8,128)} fusion(f32[1536,256]{1,0:T(8,128)S(1)} %fusion.7, bf16[1536,1536]{1,0:T(8,128)(2,1)S(1)} %bitcast.55, bf16[1536,256]{1,0:T(8,128)(2,1)S(1)} %copy-done), kind=kOutput, calls=%fused_computation.4 | convolution fusion | flops 1208352768 | bytes 8650752 | tf_op jit(solution)/shard_map/dot_general | solution.py:203
  99.7 7.2 %fusion.8 = f32[1536,256]{1,0:T(8,128)S(1)} fusion(bf16[1536,4096]{1,0:T(8,128)(2,1)} %get-tuple-element.11, bf16[4096,256]{1,0:T(8,128)(2,1)} %bitcast.8), kind=kOutput, calls=%fused_computation.40 | convolution fusion | flops 3221225472 | bytes 16252928 | tf_op jit(solution)/shard_map/dot_general | solution.py:203
  106.8 0.0 copy-start.2
  106.9 0.0 copy-start.4
  106.9 0.0 copy-start.8
  106.9 0.4 divide_convert_fusion.mean
  107.3 0.1 collective-permute-start.10
  107.4 2.4 %collective-permute-done.10.mean_far = bf16[1536,256]{1,0:T(8,128)(2,1)} collective-permute-done((bf16[1536,256]{1,0:T(8,128)(2,1)S(1)}, bf16[1536,256]{1,0:T(8,128)(2,1)}, u32[]{:S(2)}, u32[]{:S(2)}) %collective-permute-start.10) | collective-permute-done | bytes 786464 | tf_op jit(solution)/shard_map/ppermute | solution.py:136
  109.8 0.0 copy-start.7
  109.8 1.1 copy-done.7
  110.9 8.3 %layer.1 = (bf16[1536,256]{1,0:T(8,128)(2,1)}, bf16[512,256]{1,0:T(8,128)(2,1)S(1)}, bf16[512,256]{1,0:T(8,128)(2,1)S(1)}) custom-call(s32[1]{0:T(128)} %bitcast.core_ref, bf16[1536,256]{1,0:T(8,128)(2,1)S(1)} %copy-done, bf16[1536,256]{1,0:T(8,128)(2,1)S(1)} %copy-done.2, bf16[1536,256]{1,0:T(8,128)(2,1)S(1)} %divide_convert_fusion.mean, ...), custom_call_target="tpu_custom_call" | custom-call | flops 1610612736 | bytes 4718592 | tf_op jit(solution)/shard_map/layer/pallas_call | solution.py:113
  119.2 0.1 collective-permute-start.11
  119.3 1.4 collective-permute-done.11
  120.8 14.7 %all_to_all.25 = bf16[16,64,256]{2,1,0:T(8,128)(2,1)S(1)} all-to-all(bf16[16,64,256]{2,1,0:T(8,128)(2,1)S(1)} %bitcast.46), channel_id=1, replica_groups={{0,16,32,48,64,80,96,112,128,144,160,176,192,208,224,240},{2,18,34,50,6..., dimensions={0} | all-to-all | bytes 1048576 | tf_op jit(solution)/shard_map/all_to_all | solution.py:163
  135.5 0.1 reduce_sum.21
  135.6 16.2 %all_to_all.26 = bf16[8,64,256]{2,1,0:T(8,128)(2,1)S(1)} all-to-all(bf16[8,64,256]{2,1,0:T(8,128)(2,1)S(1)} %broadcast_in_dim.12), channel_id=1, replica_groups={{0,2,4,6,8,10,12,14},{16,18,20,22,24,26,28,30},{32,34,36,38,40,42,44,46..., dimensions={0} | all-to-all | bytes 524288 | tf_op jit(solution)/shard_map/all_to_all | solution.py:163
  151.8 0.8 broadcast_in_dim.13
  152.7 5.3 %all-to-all-start.4 = ((bf16[16,64,256]{2,1,0:T(8,128)(2,1)}), bf16[16,64,256]{2,1,0:T(8,128)(2,1)S(1)}, u32[]{:S(2)}, u32[]{:S(2)}) async-start(bf16[16,64,256]{2,1,0:T(8,128)(2,1)} %broadcast_in_dim.13), calls=%async_computation.4 | async-start | bytes 1048576 | tf_op jit(solution)/shard_map/all_to_all | solution.py:163
  157.9 8.7 %all-to-all-done.4 = bf16[16,64,256]{2,1,0:T(8,128)(2,1)S(1)} async-done(((bf16[16,64,256]{2,1,0:T(8,128)(2,1)}), bf16[16,64,256]{2,1,0:T(8,128)(2,1)S(1)}, u32[]{:S(2)}, u32[]{:S(2)}) %all-to-all-start.4) | async-done | bytes 524320 | tf_op jit(solution)/shard_map/all_to_all | solution.py:163
  166.7 0.1 convert_element_type.45
  166.8 0.1 slice_select_fusion.1
  167.0 1.1 pad_maximum_fusion.2
  (47 shorter events, 0.4 us)
Async XLA Ops:
  2.7 17.6 %all-to-all-start = ((bf16[8,32,256]{2,1,0:T(8,128)(2,1)}), bf16[8,32,256]{2,1,0:T(8,128)(2,1)S(1)}, u32[]{:S(2)}, u32[]{:S(2)}) async-start(bf16[8,32,256]{2,1,0:T(8,128)(2,1)} %broadcast_in_dim.11), calls=%async_computation | async-start | bytes 262144 | tf_op jit(solution)/shard_map/all_to_all | solution.py:163
  11.2 42.6 %collective-permute-start = (bf16[1536,256]{1,0:T(8,128)(2,1)}, bf16[1536,256]{1,0:T(8,128)(2,1)S(1)}, u32[]{:S(2)}, u32[]{:S(2)}) collective-permute-start(bf16[1536,256]{1,0:T(8,128)(2,1)} %own.1), channel_id=1, source_target_pairs={{0,1},{1,0},{2,3},{3,2},{4,5},{5,4},{6,7},{7,6},{8,9},{9,8},{10,11... | collective-permute-start | bytes 2359304 | tf_op jit(solution)/shard_map/ppermute | solution.py:136
  11.2 42.5 %collective-permute-start.4 = (bf16[256,512]{1,0:T(8,128)(2,1)}, bf16[256,512]{1,0:T(8,128)(2,1)S(1)}, u32[]{:S(2)}, u32[]{:S(2)}) collective-permute-start(bf16[256,512]{1,0:T(8,128)(2,1)} %w_self.1), channel_id=1, source_target_pairs={{0,1},{1,0},{2,3},{3,2},{4,5},{5,4},{6,7},{7,6},{8,9},{9,8},{10,11... | collective-permute-start | bytes 786440 | tf_op jit(solution)/shard_map/ppermute | solution.py:136
  20.3 22.1 %collective-permute-start.3 = (bf16[256,256]{1,0:T(8,128)(2,1)S(1)}, bf16[256,256]{1,0:T(8,128)(2,1)S(1)}, u32[]{:S(2)}, u32[]{:S(2)}) collective-permute-start(bf16[256,256]{1,0:T(8,128)(2,1)S(1)} %bitcast.47), channel_id=1, source_target_pairs={{0,16},{2,18},{4,20},{6,22},{8,24},{10,26},{12,28},{14,30},{16,32}... | collective-permute-start | bytes 393224 | tf_op jit(solution)/shard_map/ppermute | solution.py:145
  21.9 20.6 %collective-permute-start.2 = (bf16[256,256]{1,0:T(8,128)(2,1)S(1)}, bf16[256,256]{1,0:T(8,128)(2,1)}, u32[]{:S(2)}, u32[]{:S(2)}) collective-permute-start(bf16[256,256]{1,0:T(8,128)(2,1)S(1)} %bitcast.48), channel_id=1, source_target_pairs={{0,32},{2,34},{4,36},{6,38},{8,40},{10,42},{12,44},{14,46},{16,48}... | collective-permute-start | bytes 393224 | tf_op jit(solution)/shard_map/ppermute | solution.py:145
  22.8 19.7 %collective-permute-start.1 = (bf16[256,256]{1,0:T(8,128)(2,1)S(1)}, bf16[256,256]{1,0:T(8,128)(2,1)}, u32[]{:S(2)}, u32[]{:S(2)}) collective-permute-start(bf16[256,256]{1,0:T(8,128)(2,1)S(1)} %bitcast.49), channel_id=1, source_target_pairs={{0,48},{2,50},{4,52},{6,54},{8,56},{10,58},{12,60},{14,62},{16,0},... | collective-permute-start | bytes 393224 | tf_op jit(solution)/shard_map/ppermute | solution.py:145
  34.5 7.8 %copy-start.14 = (s32[1536,12]{0,1:T(8,128)S(1)}, s32[1536,12]{0,1:T(8,128)}, u32[]{:S(2)}) copy-start(s32[1536,12]{0,1:T(8,128)} %param.14) | copy-start | bytes 221188
  34.5 7.9 %copy-start.9 = (bf16[256,512]{1,0:T(8,128)(2,1)S(1)}, bf16[256,512]{1,0:T(8,128)(2,1)}, u32[]{:S(2)}) copy-start(bf16[256,512]{1,0:T(8,128)(2,1)} %w_neigh.1) | copy-start | bytes 786436
  34.5 13.0 %copy-start.15 = (s32[1536]{0:T(1024)S(1)}, s32[1536]{0:T(1024)}, u32[]{:S(2)}) copy-start(s32[1536]{0:T(1024)} %param.15) | copy-start | bytes 18436
  34.5 65.2 %all-to-all-start.1 = ((bf16[128,32,256]{2,1,0:T(8,128)(2,1)}), bf16[128,32,256]{2,1,0:T(8,128)(2,1)}, u32[]{:S(2)}, u32[]{:S(2)}) async-start(bf16[128,32,256]{2,1,0:T(8,128)(2,1)} %bitcast.7), calls=%async_computation.1 | async-start | bytes 4194304 | tf_op jit(solution)/shard_map/all_to_all | solution.py:220
  42.4 0.7 copy-start.12
  42.4 11.3 %collective-permute-start.5 = (bf16[256,512]{1,0:T(8,128)(2,1)S(1)}, bf16[256,512]{1,0:T(8,128)(2,1)S(1)}, u32[]{:S(2)}, u32[]{:S(2)}) collective-permute-start(bf16[256,512]{1,0:T(8,128)(2,1)S(1)} %copy-done.9), channel_id=1, source_target_pairs={{0,1},{1,0},{2,3},{3,2},{4,5},{5,4},{6,7},{7,6},{8,9},{9,8},{10,11... | collective-permute-start | bytes 786440 | tf_op jit(solution)/shard_map/ppermute | solution.py:136
  44.0 9.7 %copy-start.10 = (bf16[1024,256]{1,0:T(8,128)(2,1)}, bf16[1024,256]{1,0:T(8,128)(2,1)S(1)}, u32[]{:S(2)}) copy-start(bf16[1024,256]{1,0:T(8,128)(2,1)S(1)} %pad_maximum_fusion.refs_0_) | copy-start | bytes 1572868
  44.0 30.1 %collective-permute-start.6 = (bf16[1024,256]{1,0:T(8,128)(2,1)S(1)}, bf16[1024,256]{1,0:T(8,128)(2,1)S(1)}, u32[]{:S(2)}, u32[]{:S(2)}) collective-permute-start(bf16[1024,256]{1,0:T(8,128)(2,1)S(1)} %pad_maximum_fusion.refs_0_), channel_id=1, source_target_pairs={{0,192},{2,194},{4,196},{6,198},{8,200},{10,202},{12,204},{14,206}... | collective-permute-start | bytes 1572872 | tf_op jit(solution)/shard_map/ppermute | solution.py:145
  50.2 27.6 %copy-start.13 = (bf16[256,256]{1,0:T(8,128)(2,1)S(1)}, bf16[256,256]{1,0:T(8,128)(2,1)}, u32[]{:S(2)}) copy-start(bf16[256,256]{1,0:T(8,128)(2,1)} %copy-done.12) | copy-start | bytes 393220
  51.8 25.6 %collective-permute-start.8 = (bf16[1024,256]{1,0:T(8,128)(2,1)S(1)}, bf16[1024,256]{1,0:T(8,128)(2,1)S(1)}, u32[]{:S(2)}, u32[]{:S(2)}) collective-permute-start(bf16[1024,256]{1,0:T(8,128)(2,1)S(1)} %pad_maximum_fusion.refs_0_), channel_id=1, source_target_pairs={{0,64},{2,66},{4,68},{6,70},{8,72},{10,74},{12,76},{14,78},{16,80}... | collective-permute-start | bytes 1572872 | tf_op jit(solution)/shard_map/ppermute | solution.py:145
  53.7 0.7 copy-start.3
  53.7 0.8 copy-start.5
  54.5 0.9 copy-start.1
  74.1 12.1 %collective-permute-start.7 = (bf16[512,256]{1,0:T(8,128)(2,1)S(1)}, bf16[512,256]{1,0:T(8,128)(2,1)S(1)}, u32[]{:S(2)}, u32[]{:S(2)}) collective-permute-start(bf16[512,256]{1,0:T(8,128)(2,1)S(1)} %slice_add_fusion.1), channel_id=1, source_target_pairs={{0,192},{2,194},{4,196},{6,198},{8,200},{10,202},{12,204},{14,206}... | collective-permute-start | bytes 786440 | tf_op jit(solution)/shard_map/ppermute | solution.py:145
  77.5 12.8 %collective-permute-start.9 = (bf16[512,256]{1,0:T(8,128)(2,1)S(1)}, bf16[512,256]{1,0:T(8,128)(2,1)S(1)}, u32[]{:S(2)}, u32[]{:S(2)}) collective-permute-start(bf16[512,256]{1,0:T(8,128)(2,1)S(1)} %slice_add_fusion), channel_id=1, source_target_pairs={{0,64},{2,66},{4,68},{6,70},{8,72},{10,74},{12,76},{14,78},{16,80}... | collective-permute-start | bytes 786440 | tf_op jit(solution)/shard_map/ppermute | solution.py:145
  90.3 6.7 %slice-start = ((s8[4718592]{0:T(1024)(128)(4,1)}), s8[4194304]{0:T(1024)(128)(4,1)S(1)}, s32[]{:S(2)}) async-start(s8[4718592]{0:T(1024)(128)(4,1)} %bitcast.54), calls=%async_computation.5 | async-start | bytes 8388608
  90.4 6.6 %copy-start = (bf16[1536,256]{1,0:T(8,128)(2,1)S(1)}, bf16[1536,256]{1,0:T(8,128)(2,1)}, u32[]{:S(2)}) copy-start(bf16[1536,256]{1,0:T(8,128)(2,1)} %own.1) | copy-start | bytes 2359300
  90.4 6.6 %slice-start.1 = ((s8[4718592]{0:T(1024)(128)(4,1)}), s8[524288]{0:T(1024)(128)(4,1)S(1)}, s32[]{:S(2)}) async-start(s8[4718592]{0:T(1024)(128)(4,1)} %bitcast.54), calls=%async_computation.6 | async-start | bytes 1048576
  99.7 7.2 %copy-start.11 = (f32[1536,256]{1,0:T(8,128)S(1)}, f32[1536,256]{1,0:T(8,128)}, u32[]{:S(2)}) copy-start(f32[1536,256]{1,0:T(8,128)} %convolution_add_fusion) | copy-start | bytes 4718596
  106.8 2.9 %copy-start.2 = (bf16[1536,256]{1,0:T(8,128)(2,1)S(1)}, bf16[1536,256]{1,0:T(8,128)(2,1)}, u32[]{:S(2)}) copy-start(bf16[1536,256]{1,0:T(8,128)(2,1)} %copy-done.1) | copy-start | bytes 2359300
  106.9 2.9 %copy-start.4 = (bf16[256,512]{1,0:T(8,128)(2,1)S(1)}, bf16[256,512]{1,0:T(8,128)(2,1)}, u32[]{:S(2)}) copy-start(bf16[256,512]{1,0:T(8,128)(2,1)} %copy-done.3) | copy-start | bytes 786436
  106.9 2.9 %copy-start.6 = (bf16[256,512]{1,0:T(8,128)(2,1)S(1)}, bf16[256,512]{1,0:T(8,128)(2,1)}, u32[]{:S(2)}) copy-start(bf16[256,512]{1,0:T(8,128)(2,1)} %copy-done.5) | copy-start | bytes 786436
  106.9 2.9 %copy-start.8 = (bf16[256,512]{1,0:T(8,128)(2,1)S(1)}, bf16[256,512]{1,0:T(8,128)(2,1)}, u32[]{:S(2)}) copy-start(bf16[256,512]{1,0:T(8,128)(2,1)} %w_self.1) | copy-start | bytes 786436
  107.3 2.5 %collective-permute-start.10 = (bf16[1536,256]{1,0:T(8,128)(2,1)S(1)}, bf16[1536,256]{1,0:T(8,128)(2,1)}, u32[]{:S(2)}, u32[]{:S(2)}) collective-permute-start(bf16[1536,256]{1,0:T(8,128)(2,1)S(1)} %divide_convert_fusion.mean), channel_id=1, source_target_pairs={{0,1},{1,0},{2,3},{3,2},{4,5},{5,4},{6,7},{7,6},{8,9},{9,8},{10,11... | collective-permute-start | bytes 2359304 | tf_op jit(solution)/shard_map/ppermute | solution.py:136
  109.8 1.1 copy-start.7
  119.2 1.5 collective-permute-start.11
  152.7 14.0 %all-to-all-start.4 = ((bf16[16,64,256]{2,1,0:T(8,128)(2,1)}), bf16[16,64,256]{2,1,0:T(8,128)(2,1)S(1)}, u32[]{:S(2)}, u32[]{:S(2)}) async-start(bf16[16,64,256]{2,1,0:T(8,128)(2,1)} %broadcast_in_dim.13), calls=%async_computation.4 | async-start | bytes 1048576 | tf_op jit(solution)/shard_map/all_to_all | solution.py:163

commit v8 on v7

--- a/solution.py
+++ b/solution.py
@@ -15,6 +15,8 @@
 
 
 def incidence_kernel(waits, slots_ref, *refs):
+    *outs, token_ref = refs[waits:]
+    token_ref[...] = jnp.zeros_like(token_ref)
     slots = slots_ref[...]
     low = (slots & (SPAN - 1)).astype(jnp.float32).T
     high = slots >> 8
@@ -27,7 +29,7 @@
         right = jnp.where(low[:, g:g + 1] == lane, 1.0, 0.0).astype(jnp.bfloat16)
         mine = jnp.where(own, jnp.broadcast_to(high[g:g + 1, :], (GROUP, SPAN)), -1).astype(jnp.int16)
         first = 0
-        for out in refs[waits:]:
+        for out in outs:
             tiles = out.shape[1] // SPAN
             left = jnp.concatenate([jnp.where(mine == jnp.int16(first + t), one, zero) for t in range(tiles)], 0)
             made = jnp.dot(left, right, preferred_element_type=jnp.float32).astype(jnp.bfloat16)
@@ -45,22 +47,32 @@
     return slots.reshape(depth, groups, GROUP).transpose(1, 0, 2).reshape(groups, SPAN)
 
 
-def incidence(slots, widths, after, batch=8):
+def incidence(slots, widths, after, made=None, batch=8):
     groups = slots.shape[0]
     nodes = groups * GROUP
     total = sum(widths)
     block = batch * GROUP
-    return pl.pallas_call(
-        functools.partial(incidence_kernel, len(after)),
-        grid=(groups // batch,),
-        in_specs=[pl.BlockSpec((batch, SPAN), lambda i: (i, 0))]
-        + [pl.BlockSpec(memory_space=pl.ANY)] * len(after),
-        out_specs=[pl.BlockSpec((block, w), lambda i: (i, 0)) for w in widths],
-        out_shape=[jax.ShapeDtypeStruct((nodes, w), jnp.bfloat16) for w in widths],
-        cost_estimate=pl.CostEstimate(flops=nodes, bytes_accessed=nodes, transcendentals=0),
+    steps = groups // batch // 2
+    first = 0 if made is None else steps
+    made = made or ()
+    waits = len(made) + len(after)
+    *weights, token = pl.pallas_call(
+        functools.partial(incidence_kernel, waits),
+        grid=(steps,),
+        in_specs=[pl.BlockSpec((batch, SPAN), lambda i: (i + first, 0))]
+        + [pl.BlockSpec(memory_space=pl.ANY)] * waits,
+        out_specs=[pl.BlockSpec((block, w), lambda i: (i + first, 0)) for w in widths]
+        + [pl.BlockSpec((8, 128), lambda i: (0, 0))],
+        out_shape=[jax.ShapeDtypeStruct((nodes, w), jnp.bfloat16) for w in widths]
+        + [jax.ShapeDtypeStruct((8, 128), jnp.int32)],
+        input_output_aliases={1 + i: i for i in range(len(made))},
+        cost_estimate=pl.CostEstimate(
+            flops=len(made) * 1000 * nodes * total // 3 + nodes, bytes_accessed=nodes, transcendentals=0
+        ),
         compiler_params=pltpu.CompilerParams(vmem_limit_bytes=56 << 20),
         name="incidence",
-    )(slots, *after)
+    )(slots, *made, *after)
+    return weights, token[0, 0]
 
 
 def layer_kernel(core_ref, own, own_far, mean, mean_far, w_self, w_self_far, w_neigh, w_neigh_far,
@@ -174,9 +186,9 @@
     return jnp.concatenate([line] + [shift(line, "y", -ahead) for ahead in (1, 2, 3)], 0)
 
 
-def spread_x(plane, after, before, weight):
+def spread_x(plane, after, before, token):
     middle = plane.shape[0] // 2
-    zero = nothing(weight)
+    zero = token.astype(plane.dtype)
     return jnp.concatenate(
         [
             plane,
@@ -214,20 +226,23 @@
         onehot = (rows[:, None] == lanes).astype(jnp.bfloat16)
         return dot(onehot, features).astype(jnp.bfloat16)
 
+    hubs = parts * hub_rows.shape[0]
+    slots = pack_slots(table_order(neighbours.T, nodes, hubs), counts)
+    widths = (nodes, hubs, parts * send_rows.shape[2])
+    made, token = incidence(slots, widths, ())
     line = share(pick(hub_rows), "z").reshape(-1, half)
     plane = spread_y(line)
-    outgoing = pick(send_rows.reshape(-1) + nothing(line).astype(jnp.int32))
+    outgoing = pick(send_rows.reshape(-1) + (nothing(line).astype(jnp.int32) + token))
     incoming = lax.all_to_all(
         outgoing.reshape(parts, -1, half), "dom", split_axis=0, concat_axis=0, tiled=True
     ).reshape(-1, half)
-    hubs = parts * hub_rows.shape[0]
-    slots = pack_slots(table_order(neighbours.T, nodes, hubs), counts)
     after, before = shift(plane, "x", -1), shift(plane, "x", 1)
-    own_weight, hub_weight, far_weight = incidence(
-        slots, (nodes, hubs, incoming.shape[0]), (plane, features_far, w_self_far, w_neigh_far)
-    )
-    table = spread_x(plane, after, before, own_weight)
-    near_sum = lax.optimization_barrier(dot(own_weight, features) + dot(hub_weight, table))
+    (own_weight, hub_weight, far_weight), token = incidence(
+        slots, widths, (plane, features_far, w_self_far, w_neigh_far), made
+    )
+    table = spread_x(plane, after, before, token)
+    own_sum = lax.optimization_barrier(dot(own_weight, features))
+    near_sum = lax.optimization_barrier(own_sum + dot(hub_weight, table))
     total = near_sum + dot(far_weight, incoming)
     neigh_mean = (total / counts[:, None].astype(jnp.float32)).astype(jnp.bfloat16)
     mean_far = swap(neigh_mean)

time: 169 us -> 174 us (1.030)
  starting transfers between devices: 34.2 us -> 39.3 us
  local copies, waits for them, and re-layouts: 12.5 us -> 9.31 us
  other arithmetic: 4.35 us -> 6.97 us
  Pallas kernels: 25.2 us -> 27 us
    all_to_all x2, waiting for transfers between devices: 17.3 us -> 8.74 us  [exchange(): lax.all_to_all(blocks, 'dom', split_axis=0, concat_axis=0, tiled=True, ax...]
    ppermute x7, waiting for transfers between devices: 12.5 us -> 19.3 us  [shift(): return lax.ppermute(value, 'dom', pairs)]
    all_to_all x1, starting transfers between devices: 7.79 us -> 13.3 us  [shards(): lax.all_to_all(outgoing.reshape(parts, -1, half), 'dom', split_axis=0, co...]
    reshape x2, local copies, waits for them, and re-layouts: 2.83 us -> 1.02 us  [pack_slots(): slots.reshape(depth, groups, GROUP).transpose(1, 0, 2).reshape(groups, SPAN)]
    pallas_call x1 -> x2, Pallas kernels: 16.9 us -> 18.7 us  [incidence(): pl.pallas_call(functools.partial(incidence_kernel, waits), grid=(steps,),...]
    unnamed x43 -> x37, local copies, waits for them, and re-layouts: 5.26 us -> 4.01 us
  transfers between devices with their start and end apart: 15 -> 15, of which waited for: 6 -> 6; matrix products, arithmetic and copies ran while one was open for 16% -> 16% of each run, Pallas kernels for 10% -> 11%
where the time goes in v8:
time: 174 us
  starting transfers between devices  39.3 us (23%)
  blocking collectives  32 us (18%)
  waiting for transfers between devices  31.9 us (18%)
  Pallas kernels  27 us (16%)
  matrix products  24.8 us (14%)
  local copies, waits for them, and re-layouts  9.31 us (5%)
  other arithmetic  6.97 us (4%)
  between operations  2.37 us (1%)
    all_to_all x2, blocking collectives, exchange(): lax.all_to_all(blocks, 'dom', split_axis=0, concat_axis=0, tiled=True, ax...  32 us
    dot_general x5, matrix products, dot(): return jnp.dot(left, right, preferred_element_type=jnp.float32)  24.8 us
    ppermute x7, waiting for transfers between devices, shift(): return lax.ppermute(value, 'dom', pairs)  19.3 us
    pallas_call x2, Pallas kernels, incidence(): pl.pallas_call(functools.partial(incidence_kernel, waits), grid=(steps,),...  18.7 us
    all_to_all x2, starting transfers between devices, exchange(): lax.all_to_all(blocks, 'dom', split_axis=0, concat_axis=0, tiled=True, ax...  13.7 us
    all_to_all x1, starting transfers between devices, shards(): lax.all_to_all(outgoing.reshape(parts, -1, half), 'dom', split_axis=0, co...  13.3 us
    ppermute x7, starting transfers between devices, shift(): return lax.ppermute(value, 'dom', pairs)  11.7 us
    all_to_all x2, waiting for transfers between devices, exchange(): lax.all_to_all(blocks, 'dom', split_axis=0, concat_axis=0, tiled=True, ax...  8.74 us
  transfers between devices with their start and end apart: 15, of which 6 were waited for; matrix products, arithmetic and copies ran while one was open for 16% of the time, Pallas kernels for 11%

profile of v8, /device:TPU:8, one launch (start us, length us, event | category | flops | bytes accessed | tf_op | source)
XLA Modules:
  0.0 173.6 jit_solution(10717296309403814546)
XLA Ops:
  0.6 0.0 copy-start.13
  0.7 0.1 collective-permute-start
  0.8 1.5 convolution_convert_fusion
  2.3 0.7 broadcast_in_dim.11
  2.9 8.5 %all-to-all-start = ((bf16[8,32,256]{2,1,0:T(8,128)(2,1)}), bf16[8,32,256]{2,1,0:T(8,128)(2,1)S(1)}, u32[]{:S(2)}, u32[]{:S(2)}) async-start(bf16[8,32,256]{2,1,0:T(8,128)(2,1)} %broadcast_in_dim.11), calls=%async_computation | async-start | bytes 262144 | tf_op jit(solution)/shard_map/all_to_all | solution.py:175
  11.4 1.0 bitcast_select_fusion
  12.4 0.7 pad_select_fusion
  13.1 0.3 reshape.72
  13.4 0.2 copy.19
  13.6 0.7 copy.21.slots_ref
  14.3 0.2 collective-permute-start.4
  14.5 9.3 %incidence.2 = (bf16[1536,1536]{1,0:T(8,128)(2,1)}, bf16[1536,4096]{1,0:T(8,128)(2,1)}, bf16[1536,4096]{1,0:T(8,128)(2,1)}, s32[8,128]{1,0:T(8,128)}) custom-call(s32[96,256]{1,0:T(8,128)} %copy.21.slots_ref), custom_call_target="tpu_custom_call" | custom-call | flops 1536 | bytes 1536 | tf_op jit(solution)/shard_map/incidence/pallas_call | solution.py:59
  23.8 1.2 slice.46
  25.0 0.5 collective-permute-start.1
  25.5 2.6 %collective-permute-start.2 = (bf16[256,256]{1,0:T(8,128)(2,1)S(1)}, bf16[256,256]{1,0:T(8,128)(2,1)S(1)}, u32[]{:S(2)}, u32[]{:S(2)}) collective-permute-start(bf16[256,256]{1,0:T(8,128)(2,1)S(1)} %bitcast.48), channel_id=1, source_target_pairs={{0,32},{2,34},{4,36},{6,38},{8,40},{10,42},{12,44},{14,46},{16,48}... | collective-permute-start | bytes 393224 | tf_op jit(solution)/shard_map/ppermute | solution.py:157
  28.1 1.9 %collective-permute-start.3 = (bf16[256,256]{1,0:T(8,128)(2,1)S(1)}, bf16[256,256]{1,0:T(8,128)(2,1)S(1)}, u32[]{:S(2)}, u32[]{:S(2)}) collective-permute-start(bf16[256,256]{1,0:T(8,128)(2,1)S(1)} %bitcast.49), channel_id=1, source_target_pairs={{0,16},{2,18},{4,20},{6,22},{8,24},{10,26},{12,28},{14,30},{16,32}... | collective-permute-start | bytes 393224 | tf_op jit(solution)/shard_map/ppermute | solution.py:157
  30.0 0.5 slice.55
  31.8 0.1 copy.22
  31.9 0.1 add.58
  32.0 0.0 copy-done
  32.0 6.0 %fusion.2 = bf16[4096,256]{1,0:T(8,128)(2,1)} fusion(bf16[1536,256]{1,0:T(8,128)(2,1)S(1)} %copy-done, s32[4096]{0:T(1024)S(1)} %add.58), kind=kOutput, calls=%fused_computation.3 | convolution fusion | flops 3228565504 | bytes 2899968 | tf_op jit(solution)/shard_map/dot_general | solution.py:215
  38.0 13.3 %all-to-all-start.1 = ((bf16[128,32,256]{2,1,0:T(8,128)(2,1)}), bf16[128,32,256]{2,1,0:T(8,128)(2,1)}, u32[]{:S(2)}, u32[]{:S(2)}) async-start(bf16[128,32,256]{2,1,0:T(8,128)(2,1)} %bitcast.45), calls=%async_computation.1 | async-start | bytes 4194304 | tf_op jit(solution)/shard_map/all_to_all | solution.py:236
  51.3 0.1 collective-permute-start.5
  51.5 0.0 copy-start.12
  51.5 3.3 %collective-permute-start.6 = (bf16[1024,256]{1,0:T(8,128)(2,1)S(1)}, bf16[1024,256]{1,0:T(8,128)(2,1)S(1)}, u32[]{:S(2)}, u32[]{:S(2)}) collective-permute-start(bf16[1024,256]{1,0:T(8,128)(2,1)S(1)} %pad_maximum_fusion.refs_3_), channel_id=1, source_target_pairs={{0,192},{2,194},{4,196},{6,198},{8,200},{10,202},{12,204},{14,206}... | collective-permute-start | bytes 1572872 | tf_op jit(solution)/shard_map/ppermute | solution.py:157
  54.9 0.0 copy-start.7
  55.0 0.0 copy-start.2
  55.0 0.6 copy-done.7
  55.6 0.1 copy-done.9
  55.7 0.3 copy-done.2
  56.0 9.4 %incidence.3 = (bf16[1536,1536]{1,0:T(8,128)(2,1)}, bf16[1536,4096]{1,0:T(8,128)(2,1)}, bf16[1536,4096]{1,0:T(8,128)(2,1)}, s32[8,128]{1,0:T(8,128)}) custom-call(s32[96,256]{1,0:T(8,128)} %copy.21.slots_ref, bf16[1536,1536]{1,0:T(8,128)(2,1)} %get-tuple-element.14.refs_0_, ...), custom_call_target="tpu_custom_call", output_to_operand_aliasing={{0}: (1, {}), {1}: (2, {}), {2}: (3, {})} | custom-call | flops 14942210048 | bytes 1536 | tf_op jit(solution)/shard_map/incidence/pallas_call | solution.py:59
  65.4 0.7 convert.4
  66.0 0.5 slice.43
  66.6 9.7 %collective-permute-done.6 = bf16[1024,256]{1,0:T(8,128)(2,1)S(1)} collective-permute-done((bf16[1024,256]{1,0:T(8,128)(2,1)S(1)}, bf16[1024,256]{1,0:T(8,128)(2,1)S(1)}, u32[]{:S(2)}, u32[]{:S(2)}) %collective-permute-start.6) | collective-permute-done | bytes 524320 | tf_op jit(solution)/shard_map/ppermute | solution.py:157
  76.2 0.7 slice_add_fusion.1
  76.9 3.4 %collective-permute-start.7 = (bf16[512,256]{1,0:T(8,128)(2,1)S(1)}, bf16[512,256]{1,0:T(8,128)(2,1)S(1)}, u32[]{:S(2)}, u32[]{:S(2)}) collective-permute-start(bf16[512,256]{1,0:T(8,128)(2,1)S(1)} %slice_add_fusion.1), channel_id=1, source_target_pairs={{0,192},{2,194},{4,196},{6,198},{8,200},{10,202},{12,204},{14,206}... | collective-permute-start | bytes 786440 | tf_op jit(solution)/shard_map/ppermute | solution.py:157
  80.3 0.7 slice_add_fusion
  81.0 0.1 collective-permute-start.9
  81.1 3.7 %fusion.7 = f32[1536,256]{1,0:T(8,128)S(1)} fusion(bf16[1536,1536]{1,0:T(8,128)(2,1)} %get-tuple-element.17, bf16[1536,256]{1,0:T(8,128)(2,1)S(1)} %copy-done), kind=kOutput, calls=%fused_computation.38 | convolution fusion | flops 1207959552 | bytes 7077888 | tf_op jit(solution)/shard_map/dot_general | solution.py:215
  84.8 6.0 %collective-permute-done.7 = bf16[512,256]{1,0:T(8,128)(2,1)S(1)} collective-permute-done((bf16[512,256]{1,0:T(8,128)(2,1)S(1)}, bf16[512,256]{1,0:T(8,128)(2,1)S(1)}, u32[]{:S(2)}, u32[]{:S(2)}) %collective-permute-start.7) | collective-permute-done | bytes 262176 | tf_op jit(solution)/shard_map/ppermute | solution.py:157
  90.8 3.6 %collective-permute-done.9 = bf16[512,256]{1,0:T(8,128)(2,1)S(1)} collective-permute-done((bf16[512,256]{1,0:T(8,128)(2,1)S(1)}, bf16[512,256]{1,0:T(8,128)(2,1)S(1)}, u32[]{:S(2)}, u32[]{:S(2)}) %collective-permute-start.9) | collective-permute-done | bytes 262176 | tf_op jit(solution)/shard_map/ppermute | solution.py:157
  94.6 6.4 %fusion.8 = f32[1536,256]{1,0:T(8,128)S(1)} fusion(bf16[1536,4096]{1,0:T(8,128)(2,1)} %get-tuple-element.18, bf16[4096,256]{1,0:T(8,128)(2,1)S(1)} %constant_dynamic-update-slice_fusion), kind=kOutput, calls=%fused_computation.39 | convolution fusion | flops 3221225472 | bytes 16252928 | tf_op jit(solution)/shard_map/dot_general | solution.py:215
  101.0 1.4 add.53
  102.4 7.1 %fusion.9 = f32[1536,256]{1,0:T(8,128)S(1)} fusion(bf16[1536,4096]{1,0:T(8,128)(2,1)} %get-tuple-element.20, bf16[4096,256]{1,0:T(8,128)(2,1)} %bitcast.8), kind=kOutput, calls=%fused_computation.40 | convolution fusion | flops 3221225472 | bytes 16252928 | tf_op jit(solution)/shard_map/dot_general | solution.py:215
  109.5 0.0 copy-start.1
  109.5 0.0 copy-start.3
  109.6 0.4 divide_convert_fusion.mean
  109.9 0.1 collective-permute-start.10
  110.0 2.4 %collective-permute-done.10.mean_far = bf16[1536,256]{1,0:T(8,128)(2,1)} collective-permute-done((bf16[1536,256]{1,0:T(8,128)(2,1)S(1)}, bf16[1536,256]{1,0:T(8,128)(2,1)}, u32[]{:S(2)}, u32[]{:S(2)}) %collective-permute-start.10) | collective-permute-done | bytes 786464 | tf_op jit(solution)/shard_map/ppermute | solution.py:148
  112.5 0.9 copy-done.6
  113.4 0.9 copy-done.8
  114.4 0.9 copy-done.10
  115.3 8.3 %layer.1 = (bf16[1536,256]{1,0:T(8,128)(2,1)}, bf16[512,256]{1,0:T(8,128)(2,1)S(1)}, bf16[512,256]{1,0:T(8,128)(2,1)S(1)}) custom-call(s32[1]{0:T(128)} %bitcast.core_ref, bf16[1536,256]{1,0:T(8,128)(2,1)S(1)} %copy-done, bf16[1536,256]{1,0:T(8,128)(2,1)S(1)} %copy-done.3, bf16[1536,256]{1,0:T(8,128)(2,1)S(1)} %divide_convert_fusion.mean, ...), custom_call_target="tpu_custom_call" | custom-call | flops 1610612736 | bytes 4718592 | tf_op jit(solution)/shard_map/layer/pallas_call | solution.py:125
  123.6 0.1 collective-permute-start.11
  123.8 1.4 collective-permute-done.11
  125.2 16.9 %all_to_all.25 = bf16[16,64,256]{2,1,0:T(8,128)(2,1)S(1)} all-to-all(bf16[16,64,256]{2,1,0:T(8,128)(2,1)S(1)} %bitcast.46), channel_id=1, replica_groups={{0,16,32,48,64,80,96,112,128,144,160,176,192,208,224,240},{2,18,34,50,6..., dimensions={0} | all-to-all | bytes 1048576 | tf_op jit(solution)/shard_map/all_to_all | solution.py:175
  142.1 0.1 reduce_sum.21
  142.2 15.0 %all_to_all.26 = bf16[8,64,256]{2,1,0:T(8,128)(2,1)S(1)} all-to-all(bf16[8,64,256]{2,1,0:T(8,128)(2,1)S(1)} %broadcast_in_dim.12), channel_id=1, replica_groups={{0,2,4,6,8,10,12,14},{16,18,20,22,24,26,28,30},{32,34,36,38,40,42,44,46..., dimensions={0} | all-to-all | bytes 524288 | tf_op jit(solution)/shard_map/all_to_all | solution.py:175
  157.3 0.8 broadcast_in_dim.13
  158.2 5.3 %all-to-all-start.4 = ((bf16[16,64,256]{2,1,0:T(8,128)(2,1)}), bf16[16,64,256]{2,1,0:T(8,128)(2,1)S(1)}, u32[]{:S(2)}, u32[]{:S(2)}) async-start(bf16[16,64,256]{2,1,0:T(8,128)(2,1)} %broadcast_in_dim.13), calls=%async_computation.4 | async-start | bytes 1048576 | tf_op jit(solution)/shard_map/all_to_all | solution.py:175
  163.4 8.7 %all-to-all-done.4 = bf16[16,64,256]{2,1,0:T(8,128)(2,1)S(1)} async-done(((bf16[16,64,256]{2,1,0:T(8,128)(2,1)}), bf16[16,64,256]{2,1,0:T(8,128)(2,1)S(1)}, u32[]{:S(2)}, u32[]{:S(2)}) %all-to-all-start.4) | async-done | bytes 524320 | tf_op jit(solution)/shard_map/all_to_all | solution.py:175
  172.2 0.1 convert_element_type.47
  172.3 0.1 slice_select_fusion.1
  172.5 1.1 pad_maximum_fusion.2
  (44 shorter events, 0.4 us)
Async XLA Ops:
  0.6 31.4 %copy-start = (bf16[1536,256]{1,0:T(8,128)(2,1)S(1)}, bf16[1536,256]{1,0:T(8,128)(2,1)}, u32[]{:S(2)}) copy-start(bf16[1536,256]{1,0:T(8,128)(2,1)} %own.1) | copy-start | bytes 2359300
  0.6 23.2 %copy-start.13 = (s32[1536]{0:T(1024)S(1)}, s32[1536]{0:T(1024)}, u32[]{:S(2)}) copy-start(s32[1536]{0:T(1024)} %param.15) | copy-start | bytes 18436
  0.7 13.7 %copy-start.4 = (bf16[256,512]{1,0:T(8,128)(2,1)S(1)}, bf16[256,512]{1,0:T(8,128)(2,1)}, u32[]{:S(2)}) copy-start(bf16[256,512]{1,0:T(8,128)(2,1)} %w_self.1) | copy-start | bytes 786436
  0.7 31.1 %copy-start.14 = (s32[1,128,32]{1,2,0:T(8,128)S(1)}, s32[1,128,32]{1,2,0:T(8,128)}, u32[]{:S(2)}) copy-start(s32[1,128,32]{1,2,0:T(8,128)} %param.13) | copy-start | bytes 49156
  0.7 54.3 %collective-permute-start = (bf16[1536,256]{1,0:T(8,128)(2,1)}, bf16[1536,256]{1,0:T(8,128)(2,1)S(1)}, u32[]{:S(2)}, u32[]{:S(2)}) collective-permute-start(bf16[1536,256]{1,0:T(8,128)(2,1)} %own.1), channel_id=1, source_target_pairs={{0,1},{1,0},{2,3},{3,2},{4,5},{5,4},{6,7},{7,6},{8,9},{9,8},{10,11... | collective-permute-start | bytes 2359304 | tf_op jit(solution)/shard_map/ppermute | solution.py:148
  2.9 22.1 %all-to-all-start = ((bf16[8,32,256]{2,1,0:T(8,128)(2,1)}), bf16[8,32,256]{2,1,0:T(8,128)(2,1)S(1)}, u32[]{:S(2)}, u32[]{:S(2)}) async-start(bf16[8,32,256]{2,1,0:T(8,128)(2,1)} %broadcast_in_dim.11), calls=%async_computation | async-start | bytes 262144 | tf_op jit(solution)/shard_map/all_to_all | solution.py:175
  14.3 40.6 %collective-permute-start.4 = (bf16[256,512]{1,0:T(8,128)(2,1)S(1)}, bf16[256,512]{1,0:T(8,128)(2,1)S(1)}, u32[]{:S(2)}, u32[]{:S(2)}) collective-permute-start(bf16[256,512]{1,0:T(8,128)(2,1)S(1)} %copy-done.4), channel_id=1, source_target_pairs={{0,1},{1,0},{2,3},{3,2},{4,5},{5,4},{6,7},{7,6},{8,9},{9,8},{10,11... | collective-permute-start | bytes 786440 | tf_op jit(solution)/shard_map/ppermute | solution.py:148
  25.0 26.3 %collective-permute-start.1 = (bf16[256,256]{1,0:T(8,128)(2,1)S(1)}, bf16[256,256]{1,0:T(8,128)(2,1)S(1)}, u32[]{:S(2)}, u32[]{:S(2)}) collective-permute-start(bf16[256,256]{1,0:T(8,128)(2,1)S(1)} %bitcast.47), channel_id=1, source_target_pairs={{0,48},{2,50},{4,52},{6,54},{8,56},{10,58},{12,60},{14,62},{16,0},... | collective-permute-start | bytes 393224 | tf_op jit(solution)/shard_map/ppermute | solution.py:157
  25.5 25.9 %collective-permute-start.2 = (bf16[256,256]{1,0:T(8,128)(2,1)S(1)}, bf16[256,256]{1,0:T(8,128)(2,1)S(1)}, u32[]{:S(2)}, u32[]{:S(2)}) collective-permute-start(bf16[256,256]{1,0:T(8,128)(2,1)S(1)} %bitcast.48), channel_id=1, source_target_pairs={{0,32},{2,34},{4,36},{6,38},{8,40},{10,42},{12,44},{14,46},{16,48}... | collective-permute-start | bytes 393224 | tf_op jit(solution)/shard_map/ppermute | solution.py:157
  28.1 23.4 %collective-permute-start.3 = (bf16[256,256]{1,0:T(8,128)(2,1)S(1)}, bf16[256,256]{1,0:T(8,128)(2,1)S(1)}, u32[]{:S(2)}, u32[]{:S(2)}) collective-permute-start(bf16[256,256]{1,0:T(8,128)(2,1)S(1)} %bitcast.49), channel_id=1, source_target_pairs={{0,16},{2,18},{4,20},{6,22},{8,24},{10,26},{12,28},{14,30},{16,32}... | collective-permute-start | bytes 393224 | tf_op jit(solution)/shard_map/ppermute | solution.py:157
  38.0 13.3 %copy-start.5 = (bf16[256,512]{1,0:T(8,128)(2,1)S(1)}, bf16[256,512]{1,0:T(8,128)(2,1)}, u32[]{:S(2)}) copy-start(bf16[256,512]{1,0:T(8,128)(2,1)} %w_neigh.1) | copy-start | bytes 786436
  38.0 64.4 %all-to-all-start.1 = ((bf16[128,32,256]{2,1,0:T(8,128)(2,1)}), bf16[128,32,256]{2,1,0:T(8,128)(2,1)}, u32[]{:S(2)}, u32[]{:S(2)}) async-start(bf16[128,32,256]{2,1,0:T(8,128)(2,1)} %bitcast.45), calls=%async_computation.1 | async-start | bytes 4194304 | tf_op jit(solution)/shard_map/all_to_all | solution.py:236
  51.3 3.6 %collective-permute-start.5 = (bf16[256,512]{1,0:T(8,128)(2,1)S(1)}, bf16[256,512]{1,0:T(8,128)(2,1)S(1)}, u32[]{:S(2)}, u32[]{:S(2)}) collective-permute-start(bf16[256,512]{1,0:T(8,128)(2,1)S(1)} %copy-done.5), channel_id=1, source_target_pairs={{0,1},{1,0},{2,3},{3,2},{4,5},{5,4},{6,7},{7,6},{8,9},{9,8},{10,11... | collective-permute-start | bytes 786440 | tf_op jit(solution)/shard_map/ppermute | solution.py:148
  51.5 3.5 %copy-start.12 = (bf16[1024,256]{1,0:T(8,128)(2,1)}, bf16[1024,256]{1,0:T(8,128)(2,1)S(1)}, u32[]{:S(2)}) copy-start(bf16[1024,256]{1,0:T(8,128)(2,1)S(1)} %pad_maximum_fusion.refs_3_) | copy-start | bytes 1572868
  51.5 24.7 %collective-permute-start.6 = (bf16[1024,256]{1,0:T(8,128)(2,1)S(1)}, bf16[1024,256]{1,0:T(8,128)(2,1)S(1)}, u32[]{:S(2)}, u32[]{:S(2)}) collective-permute-start(bf16[1024,256]{1,0:T(8,128)(2,1)S(1)} %pad_maximum_fusion.refs_3_), channel_id=1, source_target_pairs={{0,192},{2,194},{4,196},{6,198},{8,200},{10,202},{12,204},{14,206}... | collective-permute-start | bytes 1572872 | tf_op jit(solution)/shard_map/ppermute | solution.py:157
  54.8 25.5 %collective-permute-start.8 = (bf16[1024,256]{1,0:T(8,128)(2,1)S(1)}, bf16[1024,256]{1,0:T(8,128)(2,1)S(1)}, u32[]{:S(2)}, u32[]{:S(2)}) collective-permute-start(bf16[1024,256]{1,0:T(8,128)(2,1)S(1)} %pad_maximum_fusion.refs_3_), channel_id=1, source_target_pairs={{0,64},{2,66},{4,68},{6,70},{8,72},{10,74},{12,76},{14,78},{16,80}... | collective-permute-start | bytes 1572872 | tf_op jit(solution)/shard_map/ppermute | solution.py:157
  54.9 0.7 copy-start.7
  54.9 0.8 copy-start.9
  55.0 1.0 copy-start.2
  76.9 13.9 %collective-permute-start.7 = (bf16[512,256]{1,0:T(8,128)(2,1)S(1)}, bf16[512,256]{1,0:T(8,128)(2,1)S(1)}, u32[]{:S(2)}, u32[]{:S(2)}) collective-permute-start(bf16[512,256]{1,0:T(8,128)(2,1)S(1)} %slice_add_fusion.1), channel_id=1, source_target_pairs={{0,192},{2,194},{4,196},{6,198},{8,200},{10,202},{12,204},{14,206}... | collective-permute-start | bytes 786440 | tf_op jit(solution)/shard_map/ppermute | solution.py:157
  81.0 13.5 %collective-permute-start.9 = (bf16[512,256]{1,0:T(8,128)(2,1)S(1)}, bf16[512,256]{1,0:T(8,128)(2,1)S(1)}, u32[]{:S(2)}, u32[]{:S(2)}) collective-permute-start(bf16[512,256]{1,0:T(8,128)(2,1)S(1)} %slice_add_fusion), channel_id=1, source_target_pairs={{0,64},{2,66},{4,68},{6,70},{8,72},{10,74},{12,76},{14,78},{16,80}... | collective-permute-start | bytes 786440 | tf_op jit(solution)/shard_map/ppermute | solution.py:157
  102.4 7.2 %copy-start.11 = (f32[1536,256]{1,0:T(8,128)S(1)}, f32[1536,256]{1,0:T(8,128)}, u32[]{:S(2)}) copy-start(f32[1536,256]{1,0:T(8,128)} %add.53) | copy-start | bytes 4718596
  109.5 2.9 %copy-start.1 = (bf16[1536,256]{1,0:T(8,128)(2,1)S(1)}, bf16[1536,256]{1,0:T(8,128)(2,1)}, u32[]{:S(2)}) copy-start(bf16[1536,256]{1,0:T(8,128)(2,1)} %cotangent_ref.1) | copy-start | bytes 2359300
  109.5 2.9 %copy-start.3 = (bf16[1536,256]{1,0:T(8,128)(2,1)S(1)}, bf16[1536,256]{1,0:T(8,128)(2,1)}, u32[]{:S(2)}) copy-start(bf16[1536,256]{1,0:T(8,128)(2,1)} %copy-done.2) | copy-start | bytes 2359300
  109.9 2.5 %collective-permute-start.10 = (bf16[1536,256]{1,0:T(8,128)(2,1)S(1)}, bf16[1536,256]{1,0:T(8,128)(2,1)}, u32[]{:S(2)}, u32[]{:S(2)}) collective-permute-start(bf16[1536,256]{1,0:T(8,128)(2,1)S(1)} %divide_convert_fusion.mean), channel_id=1, source_target_pairs={{0,1},{1,0},{2,3},{3,2},{4,5},{5,4},{6,7},{7,6},{8,9},{9,8},{10,11... | collective-permute-start | bytes 2359304 | tf_op jit(solution)/shard_map/ppermute | solution.py:148
  112.4 1.0 copy-start.6
  113.4 0.9 copy-start.8
  114.4 0.9 copy-start.10
  123.6 1.5 collective-permute-start.11
  158.2 14.0 %all-to-all-start.4 = ((bf16[16,64,256]{2,1,0:T(8,128)(2,1)}), bf16[16,64,256]{2,1,0:T(8,128)(2,1)S(1)}, u32[]{:S(2)}, u32[]{:S(2)}) async-start(bf16[16,64,256]{2,1,0:T(8,128)(2,1)} %broadcast_in_dim.13), calls=%async_computation.4 | async-start | bytes 1048576 | tf_op jit(solution)/shard_map/all_to_all | solution.py:175

commit v9 on v8

--- a/solution.py
+++ b/solution.py
@@ -67,7 +67,7 @@
         + [jax.ShapeDtypeStruct((8, 128), jnp.int32)],
         input_output_aliases={1 + i: i for i in range(len(made))},
         cost_estimate=pl.CostEstimate(
-            flops=len(made) * 1000 * nodes * total // 3 + nodes, bytes_accessed=nodes, transcendentals=0
+            flops=nodes, bytes_accessed=nodes, transcendentals=0
         ),
         compiler_params=pltpu.CompilerParams(vmem_limit_bytes=56 << 20),
         name="incidence",
@@ -117,17 +117,20 @@
         other_ref[...] = total[mine_ref.shape[0]:]
 
 
-def layer(core, own, own_far, mean, mean_far, w_self, w_self_far, w_neigh, w_neigh_far, cotangent, block=256):
+def layer(core, own, own_far, mean, mean_far, w_self, w_neigh, weights_far, cotangent, block=256):
     nodes, half = own.shape
     rows = pl.BlockSpec((block, half), lambda i, c: (i, 0))
-    weight = pl.BlockSpec((half, half), lambda i, c: (0, c[0]), pipeline_mode=pl.Buffered(1))
+
+    def weight(place):
+        return pl.BlockSpec((half, half), lambda i, c: (place, c[0]), pipeline_mode=pl.Buffered(1))
+
     whole = pl.BlockSpec((2 * half, half), lambda i, c: (0, 0))
     return pl.pallas_call(
         layer_kernel,
         grid_spec=pltpu.PrefetchScalarGridSpec(
             num_scalar_prefetch=1,
             grid=(nodes // block,),
-            in_specs=[rows] * 4 + [weight] * 4 + [rows],
+            in_specs=[rows] * 4 + [weight(0), weight(0), weight(0), weight(1), rows],
             out_specs=[rows, whole, whole],
             scratch_shapes=[pltpu.VMEM((half, 4 * half), jnp.float32)],
         ),
@@ -141,7 +144,7 @@
         ),
         compiler_params=pltpu.CompilerParams(vmem_limit_bytes=24 << 20),
         name="layer",
-    )(core, own, own_far, mean, mean_far, w_self, w_self_far, w_neigh, w_neigh_far, cotangent)
+    )(core, own, own_far, mean, mean_far, w_self, weights_far, w_neigh, weights_far, cotangent)
 
 
 def swap(value):
@@ -157,10 +160,6 @@
     return lax.ppermute(value, "dom", pairs)
 
 
-def nothing(value):
-    return jnp.minimum(jnp.abs(value[0, 0]), 0)
-
-
 def exchange(blocks, axes):
     fixed = [(stride, size) for axis, (stride, size) in LINES.items() if axis not in axes]
     moving = [LINES[axis] for axis in axes]
@@ -182,22 +181,16 @@
     return exchange(jnp.broadcast_to(block[None], (count,) + block.shape), axes)
 
 
-def spread_y(line):
-    return jnp.concatenate([line] + [shift(line, "y", -ahead) for ahead in (1, 2, 3)], 0)
-
-
-def spread_x(plane, after, before, token):
-    middle = plane.shape[0] // 2
-    zero = token.astype(plane.dtype)
+def spread_y(line, token):
+    rows = [line] + [shift(line, "y", -ahead) for ahead in (1, 2, 3)]
+    return jnp.concatenate(rows, 0) + token.astype(line.dtype)
+
+
+def opposite(after, before, token):
+    middle = after.shape[0] // 2
+    zero = token.astype(after.dtype)
     return jnp.concatenate(
-        [
-            plane,
-            after,
-            shift(after[:middle] + zero, "x", -1),
-            shift(before[middle:] + zero, "x", 1),
-            before,
-        ],
-        0,
+        [shift(after[:middle] + zero, "x", -1), shift(before[middle:] + zero, "x", 1)], 0
     )
 
 
@@ -206,6 +199,7 @@
     hub = slots - nodes
     owner = hub >> 5
     ahead_x = ((owner >> 5) - (here >> 5)) & 3
+    ahead_x = ahead_x ^ (ahead_x >> 1)
     ahead_y = ((owner >> 3) - (here >> 3)) & 3
     moved = nodes + ((ahead_x * 4 + ahead_y) << 8) + (hub & 255)
     return jnp.where((hub >= 0) & (hub < hubs), moved, slots)
@@ -219,7 +213,7 @@
     parts = lax.axis_size("dom")
     nodes, half = features.shape
     core = lax.axis_index("col")
-    features_far, w_self_far, w_neigh_far = swap(features), swap(w_self), swap(w_neigh)
+    features_far, weights_far = swap(features), swap(jnp.concatenate([w_self, w_neigh], 0))
     lanes = jnp.arange(nodes, dtype=jnp.int32)[None, :]
 
     def pick(rows):
@@ -228,27 +222,28 @@
 
     hubs = parts * hub_rows.shape[0]
     slots = pack_slots(table_order(neighbours.T, nodes, hubs), counts)
-    widths = (nodes, hubs, parts * send_rows.shape[2])
-    made, token = incidence(slots, widths, ())
-    line = share(pick(hub_rows), "z").reshape(-1, half)
-    plane = spread_y(line)
-    outgoing = pick(send_rows.reshape(-1) + (nothing(line).astype(jnp.int32) + token))
+    widths = (nodes,) + (hubs // 4,) * 4 + (parts * send_rows.shape[2],)
+    outgoing = pick(send_rows.reshape(-1))
     incoming = lax.all_to_all(
         outgoing.reshape(parts, -1, half), "dom", split_axis=0, concat_axis=0, tiled=True
     ).reshape(-1, half)
+    line = share(pick(hub_rows), "z").reshape(-1, half)
+    made, token = incidence(slots, widths, (line,))
+    plane = spread_y(line, token)
     after, before = shift(plane, "x", -1), shift(plane, "x", 1)
-    (own_weight, hub_weight, far_weight), token = incidence(
-        slots, widths, (plane, features_far, w_self_far, w_neigh_far), made
-    )
-    table = spread_x(plane, after, before, token)
-    own_sum = lax.optimization_barrier(dot(own_weight, features))
-    near_sum = lax.optimization_barrier(own_sum + dot(hub_weight, table))
-    total = near_sum + dot(far_weight, incoming)
+    weights, token = incidence(slots, widths, (plane, features_far, weights_far), made)
+    far = opposite(after, before, token)
+    fence = lax.optimization_barrier
+    total = fence(dot(weights[0], features))
+    for weight, rows in zip(weights[1:4], (plane, after, before)):
+        total = fence(total + dot(weight, rows))
+    total = fence(total + dot(weights[4], far))
+    total = total + dot(weights[5], incoming)
     neigh_mean = (total / counts[:, None].astype(jnp.float32)).astype(jnp.bfloat16)
     mean_far = swap(neigh_mean)
     layer_out, mine, other = layer(
         core.astype(jnp.int32).reshape(1), features, features_far, neigh_mean, mean_far,
-        w_self, w_self_far, w_neigh, w_neigh_far, cotangent,
+        w_self, w_neigh, weights_far, cotangent,
     )
     partial = jnp.concatenate([mine, swap(other)], 0).reshape(16, -1, half)
 

time: 174 us -> 166 us (0.954)
  waiting for transfers between devices: 31.9 us -> 17.6 us
  Pallas kernels: 27 us -> 30.9 us
  other arithmetic: 6.97 us -> 9.34 us
  local copies, waits for them, and re-layouts: 9.31 us -> 11.2 us
    ppermute x7, waiting for transfers between devices: 19.3 us -> 3.99 us  [shift(): return lax.ppermute(value, 'dom', pairs)]
    pallas_call x2, Pallas kernels: 18.7 us -> 22.6 us  [incidence(): pl.pallas_call(functools.partial(incidence_kernel, waits), grid=(steps,),...]
    add x4 -> x7, other arithmetic: 2.72 us -> 5.24 us  [the longest x1 1.84 us: spread_y(): return jnp.concatenate(rows, 0) + token.astype(line.dtype)]
    reshape x2, local copies, waits for them, and re-layouts: 1.02 us -> 2.78 us  [pack_slots(): slots.reshape(depth, groups, GROUP).transpose(1, 0, 2).reshape(groups, SPAN)]
    dot_general x5 -> x8, matrix products: 24.8 us -> 23.5 us  [dot(): return jnp.dot(left, right, preferred_element_type=jnp.float32)]
    unnamed x37 -> x39, local copies, waits for them, and re-layouts: 4.01 us -> 4.71 us
    ppermute x5 -> x4, waiting for transfers between devices: 3.81 us -> 3.81 us  [swap(): return lax.ppermute(value, 'col', SWAP)]
  transfers between devices with their start and end apart: 15 -> 14, of which waited for: 6 -> 5; matrix products, arithmetic and copies ran while one was open for 16% -> 17% of each run, Pallas kernels for 11% -> 14%
where the time goes in v9:
time: 166 us; the launch traced here: 165 us
  starting transfers between devices  39.9 us (24%)
  blocking collectives  31.4 us (19%)
  Pallas kernels  30.9 us (19%)
  matrix products  23.5 us (14%)
  waiting for transfers between devices  17.6 us (11%)
  local copies, waits for them, and re-layouts  11.2 us (7%)
  other arithmetic  9.34 us (6%)
    all_to_all x2, blocking collectives, exchange(): lax.all_to_all(blocks, 'dom', split_axis=0, concat_axis=0, tiled=True, ax...  31.4 us
    dot_general x8, matrix products, dot(): return jnp.dot(left, right, preferred_element_type=jnp.float32)  23.5 us
    pallas_call x2, Pallas kernels, incidence(): pl.pallas_call(functools.partial(incidence_kernel, waits), grid=(steps,),...  22.6 us
    all_to_all x2, starting transfers between devices, exchange(): lax.all_to_all(blocks, 'dom', split_axis=0, concat_axis=0, tiled=True, ax...  13.7 us
    all_to_all x1, starting transfers between devices, shards(): lax.all_to_all(outgoing.reshape(parts, -1, half), 'dom', split_axis=0, co...  13.7 us
    ppermute x7, starting transfers between devices, shift(): return lax.ppermute(value, 'dom', pairs)  11.7 us
    all_to_all x2, waiting for transfers between devices, exchange(): lax.all_to_all(blocks, 'dom', split_axis=0, concat_axis=0, tiled=True, ax...  9.78 us
    pallas_call x1, Pallas kernels, layer(): pl.pallas_call(layer_kernel, grid_spec=pltpu.PrefetchScalarGridSpec(num_s...  8.26 us
  transfers between devices with their start and end apart: 14, of which 5 were waited for; matrix products, arithmetic and copies ran while one was open for 17% of the time, Pallas kernels for 14%

profile of v9, /device:TPU:8, one launch (start us, length us, event | category | flops | bytes accessed | tf_op | source)
XLA Modules:
  0.0 164.7 jit_solution(17201504431506134728)
XLA Ops:
  0.6 1.4 convolution_convert_fusion
  2.1 0.7 broadcast_in_dim.11
  2.7 8.5 %all-to-all-start = ((bf16[8,32,256]{2,1,0:T(8,128)(2,1)}), bf16[8,32,256]{2,1,0:T(8,128)(2,1)S(1)}, u32[]{:S(2)}, u32[]{:S(2)}) async-start(bf16[8,32,256]{2,1,0:T(8,128)(2,1)} %broadcast_in_dim.11), calls=%async_computation | async-start | bytes 262144 | tf_op jit(solution)/shard_map/all_to_all | solution.py:174
  11.2 0.8 copy.25
  12.0 0.1 eq.35
  12.1 7.1 %fusion.2 = bf16[4096,256]{1,0:T(8,128)(2,1)} fusion(bf16[1536,256]{1,0:T(8,128)(2,1)} %own.1, s32[4096]{0:T(1024)S(1)} %eq.35), kind=kOutput, calls=%fused_computation.3 | convolution fusion | flops 3228565504 | bytes 2899968 | tf_op jit(solution)/shard_map/dot_general | solution.py:209
  19.2 0.0 copy-start.17
  19.3 1.0 all-to-all-done
  20.3 13.7 %all-to-all-start.1 = ((bf16[128,32,256]{2,1,0:T(8,128)(2,1)}), bf16[128,32,256]{2,1,0:T(8,128)(2,1)}, u32[]{:S(2)}, u32[]{:S(2)}) async-start(bf16[128,32,256]{2,1,0:T(8,128)(2,1)} %bitcast.7), calls=%async_computation.1 | async-start | bytes 4194304 | tf_op jit(solution)/shard_map/all_to_all | solution.py:227
  34.0 0.1 collective-permute-start
  34.1 0.8 pad_maximum_fusion
  34.9 0.5 collective-permute-start.4
  35.4 0.1 fusion.12
  35.5 1.0 collective-permute-start.1
  36.5 2.0 %collective-permute-start.2 = (bf16[256,256]{1,0:T(8,128)(2,1)S(1)}, bf16[256,256]{1,0:T(8,128)(2,1)}, u32[]{:S(2)}, u32[]{:S(2)}) collective-permute-start(bf16[256,256]{1,0:T(8,128)(2,1)S(1)} %bitcast.52), channel_id=1, source_target_pairs={{0,32},{2,34},{4,36},{6,38},{8,40},{10,42},{12,44},{14,46},{16,48}... | collective-permute-start | bytes 393224 | tf_op jit(solution)/shard_map/ppermute | solution.py:160
  38.5 1.8 %collective-permute-start.3 = (bf16[256,256]{1,0:T(8,128)(2,1)S(1)}, bf16[256,256]{1,0:T(8,128)(2,1)}, u32[]{:S(2)}, u32[]{:S(2)}) collective-permute-start(bf16[256,256]{1,0:T(8,128)(2,1)S(1)} %bitcast.53), channel_id=1, source_target_pairs={{0,16},{2,18},{4,20},{6,22},{8,24},{10,26},{12,28},{14,30},{16,32}... | collective-permute-start | bytes 393224 | tf_op jit(solution)/shard_map/ppermute | solution.py:160
  40.3 0.7 pad_select_fusion
  41.0 1.2 reshape.61
  42.1 0.9 copy.22
  43.0 1.6 copy.24.slots_ref
  44.7 11.3 %incidence.2 = (bf16[1536,1536]{1,0:T(8,128)(2,1)}, bf16[1536,1024]{1,0:T(8,128)(2,1)}, bf16[1536,1024]{1,0:T(8,128)(2,1)}, bf16[1536,1024]{1,0:T(8,128)(2,1)}, ...) custom-call(s32[96,256]{1,0:T(8,128)} %copy.24.slots_ref, bf16[256,256]{1,0:T(8,128)(2,1)} %bitcast.54), custom_call_target="tpu_custom_call" | custom-call | flops 1536 | bytes 1536 | tf_op jit(solution)/shard_map/incidence/pallas_call | solution.py:59
  56.0 0.7 convert.7
  56.7 0.5 slice.40
  57.2 1.8 %maximum_add_fusion.refs_6_ = bf16[1024,256]{1,0:T(8,128)(2,1)S(1)} fusion(bf16[256,256]{1,0:T(8,128)(2,1)} %collective-permute-done.3, bf16[256,256]{1,0:T(8,128)(2,1)} %collective-permute-done.2, bf16[256,256]{1,0:T(8,128)(2,1)} %collective-permute-done.1, bf16[256,256]{1,0:T(8,128)(2,1)} %bitcast.55, bf16[]{:T(256)} %bitcast.5), kind=kLoop, calls=%fused_computation.6 | loop fusion | flops 2621440 | bytes 1048578 | tf_op jit(solution)/shard_map/add | solution.py:186
  59.0 0.0 copy-start.13
  59.0 3.4 %collective-permute-start.5 = (bf16[1024,256]{1,0:T(8,128)(2,1)S(1)}, bf16[1024,256]{1,0:T(8,128)(2,1)S(1)}, u32[]{:S(2)}, u32[]{:S(2)}) collective-permute-start(bf16[1024,256]{1,0:T(8,128)(2,1)S(1)} %maximum_add_fusion.refs_6_), channel_id=1, source_target_pairs={{0,192},{2,194},{4,196},{6,198},{8,200},{10,202},{12,204},{14,206}... | collective-permute-start | bytes 1572872 | tf_op jit(solution)/shard_map/ppermute | solution.py:160
  62.5 0.0 copy-start.1
  62.5 0.8 copy-done.3
  63.3 0.3 copy-done.1
  63.5 11.3 %incidence.3 = (bf16[1536,1536]{1,0:T(8,128)(2,1)}, bf16[1536,1024]{1,0:T(8,128)(2,1)}, bf16[1536,1024]{1,0:T(8,128)(2,1)}, bf16[1536,1024]{1,0:T(8,128)(2,1)}, ...) custom-call(s32[96,256]{1,0:T(8,128)} %copy.24.slots_ref, ...), custom_call_target="tpu_custom_call", output_to_operand_aliasing={{0}: (1, {}), {1}: (2, {}), {2}: (3, {}), {3}: (4, {}), {4}... | custom-call | flops 1536 | bytes 1536 | tf_op jit(solution)/shard_map/incidence/pallas_call | solution.py:59
  74.8 0.0 copy-start.14
  74.8 3.9 %fusion.18 = f32[1536,256]{1,0:T(8,128)S(1)} fusion(bf16[1536,1536]{1,0:T(8,128)(2,1)} %get-tuple-element.27, bf16[1536,256]{1,0:T(8,128)(2,1)S(1)} %copy-done), kind=kOutput, calls=%fused_computation.41 | convolution fusion | flops 1207959552 | bytes 7077888 | tf_op jit(solution)/shard_map/dot_general | solution.py:209
  78.7 0.6 slice.42
  79.3 1.0 fusion.19
  80.3 0.2 add.48
  80.5 0.8 slice_add_fusion.1
  81.3 3.4 %collective-permute-start.7 = (bf16[512,256]{1,0:T(8,128)(2,1)S(1)}, bf16[512,256]{1,0:T(8,128)(2,1)S(1)}, u32[]{:S(2)}, u32[]{:S(2)}) collective-permute-start(bf16[512,256]{1,0:T(8,128)(2,1)S(1)} %slice_add_fusion.1), channel_id=1, source_target_pairs={{0,192},{2,194},{4,196},{6,198},{8,200},{10,202},{12,204},{14,206}... | collective-permute-start | bytes 786440 | tf_op jit(solution)/shard_map/ppermute | solution.py:160
  84.7 0.6 slice_add_fusion
  85.4 0.1 collective-permute-start.8
  85.5 1.0 fusion.20
  86.5 0.2 add.49
  86.7 1.7 %copy-done.11 = bf16[1536,1024]{1,0:T(8,128)(2,1)S(1)} copy-done((bf16[1536,1024]{1,0:T(8,128)(2,1)S(1)}, bf16[1536,1024]{1,0:T(8,128)(2,1)}, u32[]{:S(2)}) %copy-start.11) | copy-done | bytes 3145752
  88.4 1.0 fusion.21
  89.4 0.2 add.50
  89.6 4.0 %collective-permute-done.8 = bf16[512,256]{1,0:T(8,128)(2,1)S(1)} collective-permute-done((bf16[512,256]{1,0:T(8,128)(2,1)S(1)}, bf16[512,256]{1,0:T(8,128)(2,1)S(1)}, u32[]{:S(2)}, u32[]{:S(2)}) %collective-permute-start.8) | collective-permute-done | bytes 262176 | tf_op jit(solution)/shard_map/ppermute | solution.py:160
  93.6 1.0 fusion.3
  94.5 1.3 add.54
  95.9 7.2 %fusion.22 = f32[1536,256]{1,0:T(8,128)S(1)} fusion(bf16[1536,4096]{1,0:T(8,128)(2,1)} %get-tuple-element.33, bf16[4096,256]{1,0:T(8,128)(2,1)} %bitcast.8), kind=kOutput, calls=%fused_computation.45 | convolution fusion | flops 3221225472 | bytes 16252928 | tf_op jit(solution)/shard_map/dot_general | solution.py:209
  103.1 0.4 divide_convert_fusion.mean
  103.5 0.1 collective-permute-start.9
  103.6 2.4 %collective-permute-done.9.mean_far = bf16[1536,256]{1,0:T(8,128)(2,1)} collective-permute-done((bf16[1536,256]{1,0:T(8,128)(2,1)S(1)}, bf16[1536,256]{1,0:T(8,128)(2,1)}, u32[]{:S(2)}, u32[]{:S(2)}) %collective-permute-start.9) | collective-permute-done | bytes 786464 | tf_op jit(solution)/shard_map/ppermute | solution.py:151
  106.0 1.1 copy-done.7
  107.1 8.3 %layer.1 = (bf16[1536,256]{1,0:T(8,128)(2,1)}, bf16[512,256]{1,0:T(8,128)(2,1)S(1)}, bf16[512,256]{1,0:T(8,128)(2,1)S(1)}) custom-call(s32[1]{0:T(128)} %bitcast.core_ref, bf16[1536,256]{1,0:T(8,128)(2,1)S(1)} %copy-done, bf16[1536,256]{1,0:T(8,128)(2,1)S(1)} %copy-done.2, bf16[1536,256]{1,0:T(8,128)(2,1)S(1)} %divide_convert_fusion.mean, ...), custom_call_target="tpu_custom_call" | custom-call | flops 1610612736 | bytes 4718592 | tf_op jit(solution)/shard_map/layer/pallas_call | solution.py:128
  115.4 0.1 collective-permute-start.10
  115.5 1.4 collective-permute-done.10
  117.0 14.4 %all_to_all.25 = bf16[16,64,256]{2,1,0:T(8,128)(2,1)S(1)} all-to-all(bf16[16,64,256]{2,1,0:T(8,128)(2,1)S(1)} %bitcast.50), channel_id=1, replica_groups={{0,16,32,48,64,80,96,112,128,144,160,176,192,208,224,240},{2,18,34,50,6..., dimensions={0} | all-to-all | bytes 1048576 | tf_op jit(solution)/shard_map/all_to_all | solution.py:174
  131.3 0.1 reduce_sum.21
  131.4 17.0 %all_to_all.26 = bf16[8,64,256]{2,1,0:T(8,128)(2,1)S(1)} all-to-all(bf16[8,64,256]{2,1,0:T(8,128)(2,1)S(1)} %broadcast_in_dim.12), channel_id=1, replica_groups={{0,2,4,6,8,10,12,14},{16,18,20,22,24,26,28,30},{32,34,36,38,40,42,44,46..., dimensions={0} | all-to-all | bytes 524288 | tf_op jit(solution)/shard_map/all_to_all | solution.py:174
  148.5 0.8 broadcast_in_dim.13
  149.3 5.3 %all-to-all-start.4 = ((bf16[16,64,256]{2,1,0:T(8,128)(2,1)}), bf16[16,64,256]{2,1,0:T(8,128)(2,1)S(1)}, u32[]{:S(2)}, u32[]{:S(2)}) async-start(bf16[16,64,256]{2,1,0:T(8,128)(2,1)} %broadcast_in_dim.13), calls=%async_computation.4 | async-start | bytes 1048576 | tf_op jit(solution)/shard_map/all_to_all | solution.py:174
  154.6 8.7 %all-to-all-done.4 = bf16[16,64,256]{2,1,0:T(8,128)(2,1)S(1)} async-done(((bf16[16,64,256]{2,1,0:T(8,128)(2,1)}), bf16[16,64,256]{2,1,0:T(8,128)(2,1)S(1)}, u32[]{:S(2)}, u32[]{:S(2)}) %all-to-all-start.4) | async-done | bytes 524320 | tf_op jit(solution)/shard_map/all_to_all | solution.py:174
  163.3 0.1 convert_element_type.47
  163.4 0.1 slice_select_fusion.1
  163.6 1.1 pad_maximum_fusion.2
  (48 shorter events, 0.3 us)
Async XLA Ops:
  2.7 17.6 %all-to-all-start = ((bf16[8,32,256]{2,1,0:T(8,128)(2,1)}), bf16[8,32,256]{2,1,0:T(8,128)(2,1)S(1)}, u32[]{:S(2)}, u32[]{:S(2)}) async-start(bf16[8,32,256]{2,1,0:T(8,128)(2,1)} %broadcast_in_dim.11), calls=%async_computation | async-start | bytes 262144 | tf_op jit(solution)/shard_map/all_to_all | solution.py:174
  19.2 14.7 %copy-start = (bf16[1536,256]{1,0:T(8,128)(2,1)S(1)}, bf16[1536,256]{1,0:T(8,128)(2,1)}, u32[]{:S(2)}) copy-start(bf16[1536,256]{1,0:T(8,128)(2,1)} %own.1) | copy-start | bytes 2359300
  19.2 14.9 %copy-start.5 = (bf16[256,512]{1,0:T(8,128)(2,1)S(1)}, bf16[256,512]{1,0:T(8,128)(2,1)}, u32[]{:S(2)}) copy-start(bf16[256,512]{1,0:T(8,128)(2,1)} %w_neigh.1) | copy-start | bytes 786436
  19.2 14.9 %copy-start.6 = (bf16[256,512]{1,0:T(8,128)(2,1)S(1)}, bf16[256,512]{1,0:T(8,128)(2,1)}, u32[]{:S(2)}) copy-start(bf16[256,512]{1,0:T(8,128)(2,1)} %w_self.1) | copy-start | bytes 786436
  19.2 16.2 %copy-start.16 = (s32[1536,12]{0,1:T(8,128)S(1)}, s32[1536,12]{0,1:T(8,128)}, u32[]{:S(2)}) copy-start(s32[1536,12]{0,1:T(8,128)} %param.14) | copy-start | bytes 221188
  19.2 21.1 %copy-start.17 = (s32[1536]{0:T(1024)S(1)}, s32[1536]{0:T(1024)}, u32[]{:S(2)}) copy-start(s32[1536]{0:T(1024)} %param.15) | copy-start | bytes 18436
  20.3 21.8 %copy-start.15 = (bf16[8,32,256]{2,1,0:T(8,128)(2,1)}, bf16[8,32,256]{2,1,0:T(8,128)(2,1)S(1)}, u32[]{:S(2)}) copy-start(bf16[8,32,256]{2,1,0:T(8,128)(2,1)S(1)} %all-to-all-done) | copy-start | bytes 393220
  20.3 75.6 %all-to-all-start.1 = ((bf16[128,32,256]{2,1,0:T(8,128)(2,1)}), bf16[128,32,256]{2,1,0:T(8,128)(2,1)}, u32[]{:S(2)}, u32[]{:S(2)}) async-start(bf16[128,32,256]{2,1,0:T(8,128)(2,1)} %bitcast.7), calls=%async_computation.1 | async-start | bytes 4194304 | tf_op jit(solution)/shard_map/all_to_all | solution.py:227
  34.0 28.5 %collective-permute-start = (bf16[1536,256]{1,0:T(8,128)(2,1)S(1)}, bf16[1536,256]{1,0:T(8,128)(2,1)S(1)}, u32[]{:S(2)}, u32[]{:S(2)}) collective-permute-start(bf16[1536,256]{1,0:T(8,128)(2,1)S(1)} %copy-done), channel_id=1, source_target_pairs={{0,1},{1,0},{2,3},{3,2},{4,5},{5,4},{6,7},{7,6},{8,9},{9,8},{10,11... | collective-permute-start | bytes 2359304 | tf_op jit(solution)/shard_map/ppermute | solution.py:151
  34.9 27.5 %collective-permute-start.4 = (bf16[512,512]{1,0:T(8,128)(2,1)}, bf16[512,512]{1,0:T(8,128)(2,1)S(1)}, u32[]{:S(2)}, u32[]{:S(2)}) collective-permute-start(bf16[512,512]{1,0:T(8,128)(2,1)} %pad_maximum_fusion), channel_id=1, source_target_pairs={{0,1},{1,0},{2,3},{3,2},{4,5},{5,4},{6,7},{7,6},{8,9},{9,8},{10,11... | collective-permute-start | bytes 1572872 | tf_op jit(solution)/shard_map/ppermute | solution.py:151
  35.5 21.7 %collective-permute-start.1 = (bf16[256,256]{1,0:T(8,128)(2,1)S(1)}, bf16[256,256]{1,0:T(8,128)(2,1)}, u32[]{:S(2)}, u32[]{:S(2)}) collective-permute-start(bf16[256,256]{1,0:T(8,128)(2,1)S(1)} %bitcast.51), channel_id=1, source_target_pairs={{0,48},{2,50},{4,52},{6,54},{8,56},{10,58},{12,60},{14,62},{16,0},... | collective-permute-start | bytes 393224 | tf_op jit(solution)/shard_map/ppermute | solution.py:160
  36.5 20.6 %collective-permute-start.2 = (bf16[256,256]{1,0:T(8,128)(2,1)S(1)}, bf16[256,256]{1,0:T(8,128)(2,1)}, u32[]{:S(2)}, u32[]{:S(2)}) collective-permute-start(bf16[256,256]{1,0:T(8,128)(2,1)S(1)} %bitcast.52), channel_id=1, source_target_pairs={{0,32},{2,34},{4,36},{6,38},{8,40},{10,42},{12,44},{14,46},{16,48}... | collective-permute-start | bytes 393224 | tf_op jit(solution)/shard_map/ppermute | solution.py:160
  38.5 18.7 %collective-permute-start.3 = (bf16[256,256]{1,0:T(8,128)(2,1)S(1)}, bf16[256,256]{1,0:T(8,128)(2,1)}, u32[]{:S(2)}, u32[]{:S(2)}) collective-permute-start(bf16[256,256]{1,0:T(8,128)(2,1)S(1)} %bitcast.53), channel_id=1, source_target_pairs={{0,16},{2,18},{4,20},{6,22},{8,24},{10,26},{12,28},{14,30},{16,32}... | collective-permute-start | bytes 393224 | tf_op jit(solution)/shard_map/ppermute | solution.py:160
  59.0 3.5 %copy-start.13 = (bf16[1024,256]{1,0:T(8,128)(2,1)}, bf16[1024,256]{1,0:T(8,128)(2,1)S(1)}, u32[]{:S(2)}) copy-start(bf16[1024,256]{1,0:T(8,128)(2,1)S(1)} %maximum_add_fusion.refs_6_) | copy-start | bytes 1572868
  59.0 21.5 %collective-permute-start.5 = (bf16[1024,256]{1,0:T(8,128)(2,1)S(1)}, bf16[1024,256]{1,0:T(8,128)(2,1)S(1)}, u32[]{:S(2)}, u32[]{:S(2)}) collective-permute-start(bf16[1024,256]{1,0:T(8,128)(2,1)S(1)} %maximum_add_fusion.refs_6_), channel_id=1, source_target_pairs={{0,192},{2,194},{4,196},{6,198},{8,200},{10,202},{12,204},{14,206}... | collective-permute-start | bytes 1572872 | tf_op jit(solution)/shard_map/ppermute | solution.py:160
  62.5 22.3 %collective-permute-start.6 = (bf16[1024,256]{1,0:T(8,128)(2,1)S(1)}, bf16[1024,256]{1,0:T(8,128)(2,1)S(1)}, u32[]{:S(2)}, u32[]{:S(2)}) collective-permute-start(bf16[1024,256]{1,0:T(8,128)(2,1)S(1)} %maximum_add_fusion.refs_6_), channel_id=1, source_target_pairs={{0,64},{2,66},{4,68},{6,70},{8,72},{10,74},{12,76},{14,78},{16,80}... | collective-permute-start | bytes 1572872 | tf_op jit(solution)/shard_map/ppermute | solution.py:160
  62.5 0.8 copy-start.3
  62.5 1.0 copy-start.1
  74.8 3.9 %copy-start.18 = (s32[8,128]{1,0:T(8,128)S(1)}, s32[8,128]{1,0:T(8,128)}, u32[]{:S(2)}) copy-start(s32[8,128]{1,0:T(8,128)} %get-tuple-element.32) | copy-start | bytes 12292
  74.8 4.5 %copy-start.9 = (bf16[1536,1024]{1,0:T(8,128)(2,1)S(1)}, bf16[1536,1024]{1,0:T(8,128)(2,1)}, u32[]{:S(2)}) copy-start(bf16[1536,1024]{1,0:T(8,128)(2,1)} %get-tuple-element.28) | copy-start | bytes 9437188
  74.8 4.5 %copy-start.14 = (bf16[1024,256]{1,0:T(8,128)(2,1)S(1)}, bf16[1024,256]{1,0:T(8,128)(2,1)}, u32[]{:S(2)}) copy-start(bf16[1024,256]{1,0:T(8,128)(2,1)} %copy-done.13) | copy-start | bytes 1572868
  80.3 5.2 %copy-start.10 = (bf16[1536,1024]{1,0:T(8,128)(2,1)S(1)}, bf16[1536,1024]{1,0:T(8,128)(2,1)}, u32[]{:S(2)}) copy-start(bf16[1536,1024]{1,0:T(8,128)(2,1)} %get-tuple-element.29) | copy-start | bytes 9437188
  81.3 8.2 %collective-permute-start.7 = (bf16[512,256]{1,0:T(8,128)(2,1)S(1)}, bf16[512,256]{1,0:T(8,128)(2,1)S(1)}, u32[]{:S(2)}, u32[]{:S(2)}) collective-permute-start(bf16[512,256]{1,0:T(8,128)(2,1)S(1)} %slice_add_fusion.1), channel_id=1, source_target_pairs={{0,192},{2,194},{4,196},{6,198},{8,200},{10,202},{12,204},{14,206}... | collective-permute-start | bytes 786440 | tf_op jit(solution)/shard_map/ppermute | solution.py:160
  85.4 8.2 %collective-permute-start.8 = (bf16[512,256]{1,0:T(8,128)(2,1)S(1)}, bf16[512,256]{1,0:T(8,128)(2,1)S(1)}, u32[]{:S(2)}, u32[]{:S(2)}) collective-permute-start(bf16[512,256]{1,0:T(8,128)(2,1)S(1)} %slice_add_fusion), channel_id=1, source_target_pairs={{0,64},{2,66},{4,68},{6,70},{8,72},{10,74},{12,76},{14,78},{16,80}... | collective-permute-start | bytes 786440 | tf_op jit(solution)/shard_map/ppermute | solution.py:160
  86.5 1.9 %copy-start.11 = (bf16[1536,1024]{1,0:T(8,128)(2,1)S(1)}, bf16[1536,1024]{1,0:T(8,128)(2,1)}, u32[]{:S(2)}) copy-start(bf16[1536,1024]{1,0:T(8,128)(2,1)} %get-tuple-element.30) | copy-start | bytes 9437188
  89.3 4.2 %copy-start.12 = (bf16[1536,1024]{1,0:T(8,128)(2,1)S(1)}, bf16[1536,1024]{1,0:T(8,128)(2,1)}, u32[]{:S(2)}) copy-start(bf16[1536,1024]{1,0:T(8,128)(2,1)} %get-tuple-element.31) | copy-start | bytes 9437188
  95.9 7.2 %copy-start.8 = (f32[1536,256]{1,0:T(8,128)S(1)}, f32[1536,256]{1,0:T(8,128)}, u32[]{:S(2)}) copy-start(f32[1536,256]{1,0:T(8,128)} %add.54) | copy-start | bytes 4718596
  103.1 2.9 %copy-start.2 = (bf16[1536,256]{1,0:T(8,128)(2,1)S(1)}, bf16[1536,256]{1,0:T(8,128)(2,1)}, u32[]{:S(2)}) copy-start(bf16[1536,256]{1,0:T(8,128)(2,1)} %copy-done.1) | copy-start | bytes 2359300
  103.1 2.9 %copy-start.4 = (bf16[512,512]{1,0:T(8,128)(2,1)S(1)}, bf16[512,512]{1,0:T(8,128)(2,1)}, u32[]{:S(2)}) copy-start(bf16[512,512]{1,0:T(8,128)(2,1)} %copy-done.3) | copy-start | bytes 1572868
  103.5 2.5 %collective-permute-start.9 = (bf16[1536,256]{1,0:T(8,128)(2,1)S(1)}, bf16[1536,256]{1,0:T(8,128)(2,1)}, u32[]{:S(2)}, u32[]{:S(2)}) collective-permute-start(bf16[1536,256]{1,0:T(8,128)(2,1)S(1)} %divide_convert_fusion.mean), channel_id=1, source_target_pairs={{0,1},{1,0},{2,3},{3,2},{4,5},{5,4},{6,7},{7,6},{8,9},{9,8},{10,11... | collective-permute-start | bytes 2359304 | tf_op jit(solution)/shard_map/ppermute | solution.py:151
  106.0 1.1 copy-start.7
  115.4 1.5 collective-permute-start.10
  149.3 14.0 %all-to-all-start.4 = ((bf16[16,64,256]{2,1,0:T(8,128)(2,1)}), bf16[16,64,256]{2,1,0:T(8,128)(2,1)S(1)}, u32[]{:S(2)}, u32[]{:S(2)}) async-start(bf16[16,64,256]{2,1,0:T(8,128)(2,1)} %broadcast_in_dim.13), calls=%async_computation.4 | async-start | bytes 1048576 | tf_op jit(solution)/shard_map/all_to_all | solution.py:174

commit v10 on v9

--- a/solution.py
+++ b/solution.py
@@ -47,31 +47,25 @@
     return slots.reshape(depth, groups, GROUP).transpose(1, 0, 2).reshape(groups, SPAN)
 
 
-def incidence(slots, widths, after, made=None, batch=8):
+def incidence(slots, widths, after, batch=8):
     groups = slots.shape[0]
     nodes = groups * GROUP
-    total = sum(widths)
     block = batch * GROUP
-    steps = groups // batch // 2
-    first = 0 if made is None else steps
-    made = made or ()
-    waits = len(made) + len(after)
     *weights, token = pl.pallas_call(
-        functools.partial(incidence_kernel, waits),
-        grid=(steps,),
-        in_specs=[pl.BlockSpec((batch, SPAN), lambda i: (i + first, 0))]
-        + [pl.BlockSpec(memory_space=pl.ANY)] * waits,
-        out_specs=[pl.BlockSpec((block, w), lambda i: (i + first, 0)) for w in widths]
+        functools.partial(incidence_kernel, len(after)),
+        grid=(groups // batch,),
+        in_specs=[pl.BlockSpec((batch, SPAN), lambda i: (i, 0))]
+        + [pl.BlockSpec(memory_space=pl.ANY)] * len(after),
+        out_specs=[pl.BlockSpec((block, w), lambda i: (i, 0)) for w in widths]
         + [pl.BlockSpec((8, 128), lambda i: (0, 0))],
         out_shape=[jax.ShapeDtypeStruct((nodes, w), jnp.bfloat16) for w in widths]
         + [jax.ShapeDtypeStruct((8, 128), jnp.int32)],
-        input_output_aliases={1 + i: i for i in range(len(made))},
         cost_estimate=pl.CostEstimate(
             flops=nodes, bytes_accessed=nodes, transcendentals=0
         ),
         compiler_params=pltpu.CompilerParams(vmem_limit_bytes=56 << 20),
         name="incidence",
-    )(slots, *made, *after)
+    )(slots, *after)
     return weights, token[0, 0]
 
 
@@ -228,10 +222,9 @@
         outgoing.reshape(parts, -1, half), "dom", split_axis=0, concat_axis=0, tiled=True
     ).reshape(-1, half)
     line = share(pick(hub_rows), "z").reshape(-1, half)
-    made, token = incidence(slots, widths, (line,))
-    plane = spread_y(line, token)
+    plane = spread_y(line, jnp.minimum(jnp.abs(slots[0, 0]), 0))
     after, before = shift(plane, "x", -1), shift(plane, "x", 1)
-    weights, token = incidence(slots, widths, (plane, features_far, weights_far), made)
+    weights, token = incidence(slots, widths, (plane, features_far, weights_far))
     far = opposite(after, before, token)
     fence = lax.optimization_barrier
     total = fence(dot(weights[0], features))

time: 166 us -> 173 us (1.042)
  waiting for transfers between devices: 17.6 us -> 25.3 us
  blocking collectives: 31.4 us -> 37.5 us
  local copies, waits for them, and re-layouts: 11.2 us -> 8.76 us
  Pallas kernels: 30.9 us -> 28.9 us
  other arithmetic: 9.34 us -> 7.43 us
    ppermute x7, waiting for transfers between devices: 3.99 us -> 11.6 us  [shift(): return lax.ppermute(value, 'dom', pairs)]
    all_to_all x2, blocking collectives: 31.4 us -> 37.5 us  [exchange(): lax.all_to_all(blocks, 'dom', split_axis=0, concat_axis=0, tiled=True, ax...]
    pallas_call x2 -> x1, Pallas kernels: 22.6 us -> 20.6 us  [incidence(): pl.pallas_call(functools.partial(incidence_kernel, len(after)), grid=(gro...]
    reshape x2, local copies, waits for them, and re-layouts: 2.78 us -> 1.01 us  [pack_slots(): slots.reshape(depth, groups, GROUP).transpose(1, 0, 2).reshape(groups, SPAN)]
    unnamed x39 -> x37, local copies, waits for them, and re-layouts: 4.71 us -> 4.81 us
  transfers between devices with their start and end apart: 14 -> 14, of which waited for: 5 -> 9; matrix products, arithmetic and copies ran while one was open for 17% -> 14% of each run, Pallas kernels for 14% -> 12%
where the time goes in v10:
time: 173 us; the launch traced here: 172 us
  starting transfers between devices  38.9 us (22%)
  blocking collectives  37.5 us (22%)
  Pallas kernels  28.9 us (17%)
  waiting for transfers between devices  25.3 us (15%)
  matrix products  23.5 us (14%)
  local copies, waits for them, and re-layouts  8.76 us (5%)
  other arithmetic  7.43 us (4%)
    all_to_all x2, blocking collectives, exchange(): lax.all_to_all(blocks, 'dom', split_axis=0, concat_axis=0, tiled=True, ax...  37.5 us
    dot_general x8, matrix products, dot(): return jnp.dot(left, right, preferred_element_type=jnp.float32)  23.5 us
    pallas_call x1, Pallas kernels, incidence(): pl.pallas_call(functools.partial(incidence_kernel, len(after)), grid=(gro...  20.6 us
    all_to_all x2, starting transfers between devices, exchange(): lax.all_to_all(blocks, 'dom', split_axis=0, concat_axis=0, tiled=True, ax...  13.7 us
    all_to_all x1, starting transfers between devices, shards(): lax.all_to_all(outgoing.reshape(parts, -1, half), 'dom', split_axis=0, co...  13.5 us
    ppermute x7, waiting for transfers between devices, shift(): return lax.ppermute(value, 'dom', pairs)  11.6 us
    ppermute x7, starting transfers between devices, shift(): return lax.ppermute(value, 'dom', pairs)  10.8 us
    all_to_all x2, waiting for transfers between devices, exchange(): lax.all_to_all(blocks, 'dom', split_axis=0, concat_axis=0, tiled=True, ax...  9.89 us
  transfers between devices with their start and end apart: 14, of which 9 were waited for; matrix products, arithmetic and copies ran while one was open for 14% of the time, Pallas kernels for 12%

profile of v10, /device:TPU:8, one launch (start us, length us, event | category | flops | bytes accessed | tf_op | source)
XLA Modules:
  0.0 171.9 jit_solution(4902051310126363601)
XLA Ops:
  0.6 1.4 convolution_convert_fusion
  2.1 0.7 broadcast_in_dim.11
  2.7 8.5 %all-to-all-start = ((bf16[8,32,256]{2,1,0:T(8,128)(2,1)}), bf16[8,32,256]{2,1,0:T(8,128)(2,1)}, u32[]{:S(2)}, u32[]{:S(2)}) async-start(bf16[8,32,256]{2,1,0:T(8,128)(2,1)} %broadcast_in_dim.11), calls=%async_computation | async-start | bytes 262144 | tf_op jit(solution)/shard_map/all_to_all | solution.py:168
  11.2 0.8 copy.17
  12.0 0.1 eq.35
  12.1 7.1 %fusion.2 = bf16[4096,256]{1,0:T(8,128)(2,1)} fusion(bf16[1536,256]{1,0:T(8,128)(2,1)} %own.1, s32[4096]{0:T(1024)S(1)} %eq.35), kind=kOutput, calls=%fused_computation.3 | convolution fusion | flops 3228565504 | bytes 2899968 | tf_op jit(solution)/shard_map/dot_general | solution.py:203
  19.2 1.2 all-to-all-done
  20.4 13.5 %all-to-all-start.1 = ((bf16[128,32,256]{2,1,0:T(8,128)(2,1)}), bf16[128,32,256]{2,1,0:T(8,128)(2,1)}, u32[]{:S(2)}, u32[]{:S(2)}) async-start(bf16[128,32,256]{2,1,0:T(8,128)(2,1)} %bitcast.7), calls=%async_computation.1 | async-start | bytes 4194304 | tf_op jit(solution)/shard_map/all_to_all | solution.py:221
  34.0 0.1 collective-permute-start
  34.1 0.8 pad_maximum_fusion
  34.9 0.5 collective-permute-start.4
  35.4 0.1 fusion.12
  35.5 1.5 collective-permute-start.3
  37.0 1.6 collective-permute-start.2
  38.6 1.7 collective-permute-start.1
  40.3 0.3 reshape.64
  40.6 0.2 copy.15
  40.8 0.7 copy.16.slots_ref
  41.6 0.5 slice.49
  42.7 2.4 %collective-permute-done.3 = bf16[256,256]{1,0:T(8,128)(2,1)} collective-permute-done((bf16[256,256]{1,0:T(8,128)(2,1)}, bf16[256,256]{1,0:T(8,128)(2,1)}, u32[]{:S(2)}, u32[]{:S(2)}) %collective-permute-start.3) | collective-permute-done | bytes 131104 | tf_op jit(solution)/shard_map/ppermute | solution.py:154
  45.2 2.0 %collective-permute-done.2 = bf16[256,256]{1,0:T(8,128)(2,1)} collective-permute-done((bf16[256,256]{1,0:T(8,128)(2,1)}, bf16[256,256]{1,0:T(8,128)(2,1)}, u32[]{:S(2)}, u32[]{:S(2)}) %collective-permute-start.2) | collective-permute-done | bytes 131104 | tf_op jit(solution)/shard_map/ppermute | solution.py:154
  47.1 3.9 %collective-permute-done.1 = bf16[256,256]{1,0:T(8,128)(2,1)} collective-permute-done((bf16[256,256]{1,0:T(8,128)(2,1)}, bf16[256,256]{1,0:T(8,128)(2,1)}, u32[]{:S(2)}, u32[]{:S(2)}) %collective-permute-start.1) | collective-permute-done | bytes 131104 | tf_op jit(solution)/shard_map/ppermute | solution.py:154
  51.1 1.2 maximum_add_fusion.refs_0_
  52.3 0.0 copy-start.9
  52.3 2.6 %collective-permute-start.5 = (bf16[1024,256]{1,0:T(8,128)(2,1)S(1)}, bf16[1024,256]{1,0:T(8,128)(2,1)S(1)}, u32[]{:S(2)}, u32[]{:S(2)}) collective-permute-start(bf16[1024,256]{1,0:T(8,128)(2,1)S(1)} %maximum_add_fusion.refs_0_), channel_id=1, source_target_pairs={{0,192},{2,194},{4,196},{6,198},{8,200},{10,202},{12,204},{14,206}... | collective-permute-start | bytes 1572872 | tf_op jit(solution)/shard_map/ppermute | solution.py:154
  54.9 0.8 copy-done.3
  55.7 0.9 copy-done.1
  56.5 20.6 %incidence.1 = (bf16[1536,1536]{1,0:T(8,128)(2,1)}, bf16[1536,1024]{1,0:T(8,128)(2,1)}, bf16[1536,1024]{1,0:T(8,128)(2,1)}, bf16[1536,1024]{1,0:T(8,128)(2,1)}, ...) custom-call(s32[96,256]{1,0:T(8,128)} %copy.16.slots_ref, bf16[1024,256]{1,0:T(8,128)(2,1)} %copy-done.9, ...), custom_call_target="tpu_custom_call" | custom-call | flops 1536 | bytes 1536 | tf_op jit(solution)/shard_map/incidence/pallas_call | solution.py:54
  77.1 3.9 %fusion.18 = f32[1536,256]{1,0:T(8,128)S(1)} fusion(bf16[1536,1536]{1,0:T(8,128)(2,1)} %get-tuple-element.13, bf16[1536,256]{1,0:T(8,128)(2,1)S(1)} %copy-done), kind=kOutput, calls=%fused_computation.41 | convolution fusion | flops 1207959552 | bytes 7077888 | tf_op jit(solution)/shard_map/dot_general | solution.py:203
  81.0 1.0 fusion.19
  82.0 0.2 add.48
  82.3 0.5 copy-done.13
  82.7 0.5 slice.41
  83.2 0.7 copy-done.16
  83.9 1.0 fusion.20
  84.9 0.2 add.49
  85.2 0.8 slice_add_fusion
  86.0 0.5 collective-permute-start.8
  86.5 0.7 slice_add_fusion.1
  87.2 2.9 %collective-permute-start.7 = (bf16[512,256]{1,0:T(8,128)(2,1)S(1)}, bf16[512,256]{1,0:T(8,128)(2,1)S(1)}, u32[]{:S(2)}, u32[]{:S(2)}) collective-permute-start(bf16[512,256]{1,0:T(8,128)(2,1)S(1)} %slice_add_fusion.1), channel_id=1, source_target_pairs={{0,192},{2,194},{4,196},{6,198},{8,200},{10,202},{12,204},{14,206}... | collective-permute-start | bytes 786440 | tf_op jit(solution)/shard_map/ppermute | solution.py:154
  90.1 1.0 fusion.21
  91.1 0.2 add.50
  91.3 2.9 %collective-permute-done.8 = bf16[512,256]{1,0:T(8,128)(2,1)S(1)} collective-permute-done((bf16[512,256]{1,0:T(8,128)(2,1)S(1)}, bf16[512,256]{1,0:T(8,128)(2,1)S(1)}, u32[]{:S(2)}, u32[]{:S(2)}) %collective-permute-start.8) | collective-permute-done | bytes 262176 | tf_op jit(solution)/shard_map/ppermute | solution.py:154
  94.2 0.3 collective-permute-done.7
  94.5 1.0 fusion.3
  95.5 1.3 add.54
  96.9 7.1 %fusion.22 = f32[1536,256]{1,0:T(8,128)S(1)} fusion(bf16[1536,4096]{1,0:T(8,128)(2,1)} %get-tuple-element.19, bf16[4096,256]{1,0:T(8,128)(2,1)} %bitcast.8), kind=kOutput, calls=%fused_computation.45 | convolution fusion | flops 3221225472 | bytes 16252928 | tf_op jit(solution)/shard_map/dot_general | solution.py:203
  104.0 0.0 copy-start.2
  104.1 0.4 divide_convert_fusion.mean
  104.5 0.1 collective-permute-start.9
  104.6 2.4 %collective-permute-done.9.mean_far = bf16[1536,256]{1,0:T(8,128)(2,1)} collective-permute-done((bf16[1536,256]{1,0:T(8,128)(2,1)S(1)}, bf16[1536,256]{1,0:T(8,128)(2,1)}, u32[]{:S(2)}, u32[]{:S(2)}) %collective-permute-start.9) | collective-permute-done | bytes 786464 | tf_op jit(solution)/shard_map/ppermute | solution.py:145
  107.0 1.1 copy-done.7
  108.1 8.3 %layer.1 = (bf16[1536,256]{1,0:T(8,128)(2,1)}, bf16[512,256]{1,0:T(8,128)(2,1)S(1)}, bf16[512,256]{1,0:T(8,128)(2,1)S(1)}) custom-call(s32[1]{0:T(128)} %bitcast.core_ref, bf16[1536,256]{1,0:T(8,128)(2,1)S(1)} %copy-done, bf16[1536,256]{1,0:T(8,128)(2,1)S(1)} %copy-done.2, bf16[1536,256]{1,0:T(8,128)(2,1)S(1)} %divide_convert_fusion.mean, ...), custom_call_target="tpu_custom_call" | custom-call | flops 1610612736 | bytes 4718592 | tf_op jit(solution)/shard_map/layer/pallas_call | solution.py:122
  116.4 0.1 collective-permute-start.10
  116.5 1.4 collective-permute-done.10
  118.0 18.5 %all_to_all.25 = bf16[16,64,256]{2,1,0:T(8,128)(2,1)S(1)} all-to-all(bf16[16,64,256]{2,1,0:T(8,128)(2,1)S(1)} %bitcast.50), channel_id=1, replica_groups={{0,16,32,48,64,80,96,112,128,144,160,176,192,208,224,240},{2,18,34,50,6..., dimensions={0} | all-to-all | bytes 1048576 | tf_op jit(solution)/shard_map/all_to_all | solution.py:168
  136.5 0.1 reduce_sum.21
  136.6 19.0 %all_to_all.26 = bf16[8,64,256]{2,1,0:T(8,128)(2,1)S(1)} all-to-all(bf16[8,64,256]{2,1,0:T(8,128)(2,1)S(1)} %broadcast_in_dim.12), channel_id=1, replica_groups={{0,2,4,6,8,10,12,14},{16,18,20,22,24,26,28,30},{32,34,36,38,40,42,44,46..., dimensions={0} | all-to-all | bytes 524288 | tf_op jit(solution)/shard_map/all_to_all | solution.py:168
  155.6 0.8 broadcast_in_dim.13
  156.5 5.3 %all-to-all-start.4 = ((bf16[16,64,256]{2,1,0:T(8,128)(2,1)}), bf16[16,64,256]{2,1,0:T(8,128)(2,1)S(1)}, u32[]{:S(2)}, u32[]{:S(2)}) async-start(bf16[16,64,256]{2,1,0:T(8,128)(2,1)} %broadcast_in_dim.13), calls=%async_computation.4 | async-start | bytes 1048576 | tf_op jit(solution)/shard_map/all_to_all | solution.py:168
  161.7 8.7 %all-to-all-done.4 = bf16[16,64,256]{2,1,0:T(8,128)(2,1)S(1)} async-done(((bf16[16,64,256]{2,1,0:T(8,128)(2,1)}), bf16[16,64,256]{2,1,0:T(8,128)(2,1)S(1)}, u32[]{:S(2)}, u32[]{:S(2)}) %all-to-all-start.4) | async-done | bytes 524320 | tf_op jit(solution)/shard_map/all_to_all | solution.py:168
  170.5 0.1 convert_element_type.50
  170.6 0.1 slice_select_fusion.1
  170.8 1.1 pad_maximum_fusion.2
  (44 shorter events, 0.3 us)
Async XLA Ops:
  2.7 17.7 %all-to-all-start = ((bf16[8,32,256]{2,1,0:T(8,128)(2,1)}), bf16[8,32,256]{2,1,0:T(8,128)(2,1)}, u32[]{:S(2)}, u32[]{:S(2)}) async-start(bf16[8,32,256]{2,1,0:T(8,128)(2,1)} %broadcast_in_dim.11), calls=%async_computation | async-start | bytes 262144 | tf_op jit(solution)/shard_map/all_to_all | solution.py:168
  19.2 14.7 %copy-start = (bf16[1536,256]{1,0:T(8,128)(2,1)S(1)}, bf16[1536,256]{1,0:T(8,128)(2,1)}, u32[]{:S(2)}) copy-start(bf16[1536,256]{1,0:T(8,128)(2,1)} %own.1) | copy-start | bytes 2359300
  19.2 14.8 %copy-start.5 = (bf16[256,512]{1,0:T(8,128)(2,1)S(1)}, bf16[256,512]{1,0:T(8,128)(2,1)}, u32[]{:S(2)}) copy-start(bf16[256,512]{1,0:T(8,128)(2,1)} %w_neigh.1) | copy-start | bytes 786436
  19.2 14.9 %copy-start.6 = (bf16[256,512]{1,0:T(8,128)(2,1)S(1)}, bf16[256,512]{1,0:T(8,128)(2,1)}, u32[]{:S(2)}) copy-start(bf16[256,512]{1,0:T(8,128)(2,1)} %w_self.1) | copy-start | bytes 786436
  19.2 16.2 %copy-start.11 = (s32[1536,12]{0,1:T(8,128)S(1)}, s32[1536,12]{0,1:T(8,128)}, u32[]{:S(2)}) copy-start(s32[1536,12]{0,1:T(8,128)} %param.14) | copy-start | bytes 221188
  19.2 21.1 %copy-start.12 = (s32[1536]{0:T(1024)S(1)}, s32[1536]{0:T(1024)}, u32[]{:S(2)}) copy-start(s32[1536]{0:T(1024)} %param.15) | copy-start | bytes 18436
  20.4 76.5 %all-to-all-start.1 = ((bf16[128,32,256]{2,1,0:T(8,128)(2,1)}), bf16[128,32,256]{2,1,0:T(8,128)(2,1)}, u32[]{:S(2)}, u32[]{:S(2)}) async-start(bf16[128,32,256]{2,1,0:T(8,128)(2,1)} %bitcast.7), calls=%async_computation.1 | async-start | bytes 4194304 | tf_op jit(solution)/shard_map/all_to_all | solution.py:221
  34.0 20.9 %collective-permute-start = (bf16[1536,256]{1,0:T(8,128)(2,1)S(1)}, bf16[1536,256]{1,0:T(8,128)(2,1)S(1)}, u32[]{:S(2)}, u32[]{:S(2)}) collective-permute-start(bf16[1536,256]{1,0:T(8,128)(2,1)S(1)} %copy-done), channel_id=1, source_target_pairs={{0,1},{1,0},{2,3},{3,2},{4,5},{5,4},{6,7},{7,6},{8,9},{9,8},{10,11... | collective-permute-start | bytes 2359304 | tf_op jit(solution)/shard_map/ppermute | solution.py:145
  34.9 20.0 %collective-permute-start.4 = (bf16[512,512]{1,0:T(8,128)(2,1)}, bf16[512,512]{1,0:T(8,128)(2,1)S(1)}, u32[]{:S(2)}, u32[]{:S(2)}) collective-permute-start(bf16[512,512]{1,0:T(8,128)(2,1)} %pad_maximum_fusion), channel_id=1, source_target_pairs={{0,1},{1,0},{2,3},{3,2},{4,5},{5,4},{6,7},{7,6},{8,9},{9,8},{10,11... | collective-permute-start | bytes 1572872 | tf_op jit(solution)/shard_map/ppermute | solution.py:145
  35.5 9.7 %collective-permute-start.3 = (bf16[256,256]{1,0:T(8,128)(2,1)}, bf16[256,256]{1,0:T(8,128)(2,1)}, u32[]{:S(2)}, u32[]{:S(2)}) collective-permute-start(bf16[256,256]{1,0:T(8,128)(2,1)} %bitcast.4), channel_id=1, source_target_pairs={{0,16},{2,18},{4,20},{6,22},{8,24},{10,26},{12,28},{14,30},{16,32}... | collective-permute-start | bytes 393224 | tf_op jit(solution)/shard_map/ppermute | solution.py:154
  37.0 10.1 %collective-permute-start.2 = (bf16[256,256]{1,0:T(8,128)(2,1)}, bf16[256,256]{1,0:T(8,128)(2,1)}, u32[]{:S(2)}, u32[]{:S(2)}) collective-permute-start(bf16[256,256]{1,0:T(8,128)(2,1)} %bitcast.4), channel_id=1, source_target_pairs={{0,32},{2,34},{4,36},{6,38},{8,40},{10,42},{12,44},{14,46},{16,48}... | collective-permute-start | bytes 393224 | tf_op jit(solution)/shard_map/ppermute | solution.py:154
  38.6 12.5 %collective-permute-start.1 = (bf16[256,256]{1,0:T(8,128)(2,1)}, bf16[256,256]{1,0:T(8,128)(2,1)}, u32[]{:S(2)}, u32[]{:S(2)}) collective-permute-start(bf16[256,256]{1,0:T(8,128)(2,1)} %bitcast.4), channel_id=1, source_target_pairs={{0,48},{2,50},{4,52},{6,54},{8,56},{10,58},{12,60},{14,62},{16,0},... | collective-permute-start | bytes 393224 | tf_op jit(solution)/shard_map/ppermute | solution.py:154
  52.3 2.6 %copy-start.9 = (bf16[1024,256]{1,0:T(8,128)(2,1)}, bf16[1024,256]{1,0:T(8,128)(2,1)S(1)}, u32[]{:S(2)}) copy-start(bf16[1024,256]{1,0:T(8,128)(2,1)S(1)} %maximum_add_fusion.refs_0_) | copy-start | bytes 1572868
  52.3 31.0 %collective-permute-start.5 = (bf16[1024,256]{1,0:T(8,128)(2,1)S(1)}, bf16[1024,256]{1,0:T(8,128)(2,1)S(1)}, u32[]{:S(2)}, u32[]{:S(2)}) collective-permute-start(bf16[1024,256]{1,0:T(8,128)(2,1)S(1)} %maximum_add_fusion.refs_0_), channel_id=1, source_target_pairs={{0,192},{2,194},{4,196},{6,198},{8,200},{10,202},{12,204},{14,206}... | collective-permute-start | bytes 1572872 | tf_op jit(solution)/shard_map/ppermute | solution.py:154
  54.9 30.3 %collective-permute-start.6 = (bf16[1024,256]{1,0:T(8,128)(2,1)S(1)}, bf16[1024,256]{1,0:T(8,128)(2,1)S(1)}, u32[]{:S(2)}, u32[]{:S(2)}) collective-permute-start(bf16[1024,256]{1,0:T(8,128)(2,1)S(1)} %maximum_add_fusion.refs_0_), channel_id=1, source_target_pairs={{0,64},{2,66},{4,68},{6,70},{8,72},{10,74},{12,76},{14,78},{16,80}... | collective-permute-start | bytes 1572872 | tf_op jit(solution)/shard_map/ppermute | solution.py:154
  54.9 0.8 copy-start.3
  55.7 0.9 copy-start.1
  77.1 3.9 %copy-start.10 = (bf16[1024,256]{1,0:T(8,128)(2,1)S(1)}, bf16[1024,256]{1,0:T(8,128)(2,1)}, u32[]{:S(2)}) copy-start(bf16[1024,256]{1,0:T(8,128)(2,1)} %copy-done.9) | copy-start | bytes 1572868
  77.1 3.9 %copy-start.17 = (bf16[1536,1024]{1,0:T(8,128)(2,1)S(1)}, bf16[1536,1024]{1,0:T(8,128)(2,1)}, u32[]{:S(2)}) copy-start(bf16[1536,1024]{1,0:T(8,128)(2,1)} %get-tuple-element.14) | copy-start | bytes 9437188
  82.0 0.7 copy-start.13
  82.0 1.9 %copy-start.16 = (bf16[1536,1024]{1,0:T(8,128)(2,1)S(1)}, bf16[1536,1024]{1,0:T(8,128)(2,1)}, u32[]{:S(2)}) copy-start(bf16[1536,1024]{1,0:T(8,128)(2,1)} %get-tuple-element.15) | copy-start | bytes 9437188
  84.9 5.1 %copy-start.15 = (bf16[1536,1024]{1,0:T(8,128)(2,1)S(1)}, bf16[1536,1024]{1,0:T(8,128)(2,1)}, u32[]{:S(2)}) copy-start(bf16[1536,1024]{1,0:T(8,128)(2,1)} %get-tuple-element.16) | copy-start | bytes 9437188
  86.0 8.2 %collective-permute-start.8 = (bf16[512,256]{1,0:T(8,128)(2,1)S(1)}, bf16[512,256]{1,0:T(8,128)(2,1)S(1)}, u32[]{:S(2)}, u32[]{:S(2)}) collective-permute-start(bf16[512,256]{1,0:T(8,128)(2,1)S(1)} %slice_add_fusion), channel_id=1, source_target_pairs={{0,64},{2,66},{4,68},{6,70},{8,72},{10,74},{12,76},{14,78},{16,80}... | collective-permute-start | bytes 786440 | tf_op jit(solution)/shard_map/ppermute | solution.py:154
  87.2 7.4 %collective-permute-start.7 = (bf16[512,256]{1,0:T(8,128)(2,1)S(1)}, bf16[512,256]{1,0:T(8,128)(2,1)S(1)}, u32[]{:S(2)}, u32[]{:S(2)}) collective-permute-start(bf16[512,256]{1,0:T(8,128)(2,1)S(1)} %slice_add_fusion.1), channel_id=1, source_target_pairs={{0,192},{2,194},{4,196},{6,198},{8,200},{10,202},{12,204},{14,206}... | collective-permute-start | bytes 786440 | tf_op jit(solution)/shard_map/ppermute | solution.py:154
  91.1 3.5 %copy-start.14 = (bf16[1536,1024]{1,0:T(8,128)(2,1)S(1)}, bf16[1536,1024]{1,0:T(8,128)(2,1)}, u32[]{:S(2)}) copy-start(bf16[1536,1024]{1,0:T(8,128)(2,1)} %get-tuple-element.17) | copy-start | bytes 9437188
  96.9 7.2 %copy-start.8 = (f32[1536,256]{1,0:T(8,128)S(1)}, f32[1536,256]{1,0:T(8,128)}, u32[]{:S(2)}) copy-start(f32[1536,256]{1,0:T(8,128)} %add.54) | copy-start | bytes 4718596
  104.0 2.9 %copy-start.2 = (bf16[1536,256]{1,0:T(8,128)(2,1)S(1)}, bf16[1536,256]{1,0:T(8,128)(2,1)}, u32[]{:S(2)}) copy-start(bf16[1536,256]{1,0:T(8,128)(2,1)} %copy-done.1) | copy-start | bytes 2359300
  104.1 2.9 %copy-start.4 = (bf16[512,512]{1,0:T(8,128)(2,1)S(1)}, bf16[512,512]{1,0:T(8,128)(2,1)}, u32[]{:S(2)}) copy-start(bf16[512,512]{1,0:T(8,128)(2,1)} %copy-done.3) | copy-start | bytes 1572868
  104.5 2.5 %collective-permute-start.9 = (bf16[1536,256]{1,0:T(8,128)(2,1)S(1)}, bf16[1536,256]{1,0:T(8,128)(2,1)}, u32[]{:S(2)}, u32[]{:S(2)}) collective-permute-start(bf16[1536,256]{1,0:T(8,128)(2,1)S(1)} %divide_convert_fusion.mean), channel_id=1, source_target_pairs={{0,1},{1,0},{2,3},{3,2},{4,5},{5,4},{6,7},{7,6},{8,9},{9,8},{10,11... | collective-permute-start | bytes 2359304 | tf_op jit(solution)/shard_map/ppermute | solution.py:145
  107.0 1.1 copy-start.7
  116.4 1.5 collective-permute-start.10
  156.5 14.0 %all-to-all-start.4 = ((bf16[16,64,256]{2,1,0:T(8,128)(2,1)}), bf16[16,64,256]{2,1,0:T(8,128)(2,1)S(1)}, u32[]{:S(2)}, u32[]{:S(2)}) async-start(bf16[16,64,256]{2,1,0:T(8,128)(2,1)} %broadcast_in_dim.13), calls=%async_computation.4 | async-start | bytes 1048576 | tf_op jit(solution)/shard_map/all_to_all | solution.py:168

commit v11 on v9

--- a/solution.py
+++ b/solution.py
@@ -234,8 +234,8 @@
     weights, token = incidence(slots, widths, (plane, features_far, weights_far), made)
     far = opposite(after, before, token)
     fence = lax.optimization_barrier
-    total = fence(dot(weights[0], features))
-    for weight, rows in zip(weights[1:4], (plane, after, before)):
+    total = fence(dot(weights[2], after))
+    for weight, rows in zip((weights[3], weights[1], weights[0]), (before, plane, features)):
         total = fence(total + dot(weight, rows))
     total = fence(total + dot(weights[4], far))
     total = total + dot(weights[5], incoming)

time: 166 us -> 165 us (level)
  transfers between devices with their start and end apart: 14 -> 14, of which waited for: 5 -> 6; matrix products, arithmetic and copies ran while one was open for 17% -> 17% of each run, Pallas kernels for 14% -> 14%
where the time goes in v11:
time: 165 us; the launch traced here: 164 us
  starting transfers between devices  40.1 us (24%)
  Pallas kernels  30.9 us (19%)
  blocking collectives  30.7 us (19%)
  matrix products  23.5 us (14%)
  waiting for transfers between devices  18.2 us (11%)
  local copies, waits for them, and re-layouts  10.3 us (6%)
  other arithmetic  9.19 us (6%)
    all_to_all x2, blocking collectives, exchange(): lax.all_to_all(blocks, 'dom', split_axis=0, concat_axis=0, tiled=True, ax...  30.7 us
    dot_general x8, matrix products, dot(): return jnp.dot(left, right, preferred_element_type=jnp.float32)  23.5 us
    pallas_call x2, Pallas kernels, incidence(): pl.pallas_call(functools.partial(incidence_kernel, waits), grid=(steps,),...  22.6 us
    all_to_all x2, starting transfers between devices, exchange(): lax.all_to_all(blocks, 'dom', split_axis=0, concat_axis=0, tiled=True, ax...  13.7 us
    all_to_all x1, starting transfers between devices, shards(): lax.all_to_all(outgoing.reshape(parts, -1, half), 'dom', split_axis=0, co...  13.7 us
    ppermute x7, starting transfers between devices, shift(): return lax.ppermute(value, 'dom', pairs)  11.9 us
    all_to_all x2, waiting for transfers between devices, exchange(): lax.all_to_all(blocks, 'dom', split_axis=0, concat_axis=0, tiled=True, ax...  9.78 us
    pallas_call x1, Pallas kernels, layer(): pl.pallas_call(layer_kernel, grid_spec=pltpu.PrefetchScalarGridSpec(num_s...  8.26 us
  transfers between devices with their start and end apart: 14, of which 6 were waited for; matrix products, arithmetic and copies ran while one was open for 17% of the time, Pallas kernels for 14%

profile of v11, /device:TPU:8, one launch (start us, length us, event | category | flops | bytes accessed | tf_op | source)
XLA Modules:
  0.0 163.8 jit_solution(1050363608701234245)
XLA Ops:
  0.6 1.4 convolution_convert_fusion
  2.1 0.7 broadcast_in_dim.11
  2.7 8.5 %all-to-all-start = ((bf16[8,32,256]{2,1,0:T(8,128)(2,1)}), bf16[8,32,256]{2,1,0:T(8,128)(2,1)S(1)}, u32[]{:S(2)}, u32[]{:S(2)}) async-start(bf16[8,32,256]{2,1,0:T(8,128)(2,1)} %broadcast_in_dim.11), calls=%async_computation | async-start | bytes 262144 | tf_op jit(solution)/shard_map/all_to_all | solution.py:174
  11.2 0.8 copy.25
  12.0 0.1 eq.35
  12.1 7.1 %fusion.2 = bf16[4096,256]{1,0:T(8,128)(2,1)} fusion(bf16[1536,256]{1,0:T(8,128)(2,1)} %own.1, s32[4096]{0:T(1024)S(1)} %eq.35), kind=kOutput, calls=%fused_computation.3 | convolution fusion | flops 3228565504 | bytes 2899968 | tf_op jit(solution)/shard_map/dot_general | solution.py:209
  19.3 1.0 all-to-all-done
  20.3 13.7 %all-to-all-start.1 = ((bf16[128,32,256]{2,1,0:T(8,128)(2,1)}), bf16[128,32,256]{2,1,0:T(8,128)(2,1)}, u32[]{:S(2)}, u32[]{:S(2)}) async-start(bf16[128,32,256]{2,1,0:T(8,128)(2,1)} %bitcast.7), calls=%async_computation.1 | async-start | bytes 4194304 | tf_op jit(solution)/shard_map/all_to_all | solution.py:227
  34.0 0.1 collective-permute-start
  34.1 0.8 pad_maximum_fusion
  34.9 0.5 collective-permute-start.4
  35.4 0.1 fusion.12
  35.5 1.0 collective-permute-start.1
  36.5 2.0 %collective-permute-start.2 = (bf16[256,256]{1,0:T(8,128)(2,1)S(1)}, bf16[256,256]{1,0:T(8,128)(2,1)}, u32[]{:S(2)}, u32[]{:S(2)}) collective-permute-start(bf16[256,256]{1,0:T(8,128)(2,1)S(1)} %bitcast.52), channel_id=1, source_target_pairs={{0,32},{2,34},{4,36},{6,38},{8,40},{10,42},{12,44},{14,46},{16,48}... | collective-permute-start | bytes 393224 | tf_op jit(solution)/shard_map/ppermute | solution.py:160
  38.5 1.8 %collective-permute-start.3 = (bf16[256,256]{1,0:T(8,128)(2,1)S(1)}, bf16[256,256]{1,0:T(8,128)(2,1)}, u32[]{:S(2)}, u32[]{:S(2)}) collective-permute-start(bf16[256,256]{1,0:T(8,128)(2,1)S(1)} %bitcast.53), channel_id=1, source_target_pairs={{0,16},{2,18},{4,20},{6,22},{8,24},{10,26},{12,28},{14,30},{16,32}... | collective-permute-start | bytes 393224 | tf_op jit(solution)/shard_map/ppermute | solution.py:160
  40.3 0.7 pad_select_fusion
  41.0 1.2 reshape.61
  42.1 0.9 copy.22
  43.0 1.6 copy.24.slots_ref
  44.7 11.3 %incidence.2 = (bf16[1536,1536]{1,0:T(8,128)(2,1)}, bf16[1536,1024]{1,0:T(8,128)(2,1)}, bf16[1536,1024]{1,0:T(8,128)(2,1)}, bf16[1536,1024]{1,0:T(8,128)(2,1)}, ...) custom-call(s32[96,256]{1,0:T(8,128)} %copy.24.slots_ref, bf16[256,256]{1,0:T(8,128)(2,1)} %bitcast.54), custom_call_target="tpu_custom_call" | custom-call | flops 1536 | bytes 1536 | tf_op jit(solution)/shard_map/incidence/pallas_call | solution.py:59
  56.0 0.7 convert.7
  56.7 0.5 slice.40
  57.2 1.8 %maximum_add_fusion.refs_6_ = bf16[1024,256]{1,0:T(8,128)(2,1)S(1)} fusion(bf16[256,256]{1,0:T(8,128)(2,1)} %collective-permute-done.3, bf16[256,256]{1,0:T(8,128)(2,1)} %collective-permute-done.2, bf16[256,256]{1,0:T(8,128)(2,1)} %collective-permute-done.1, bf16[256,256]{1,0:T(8,128)(2,1)} %bitcast.55, bf16[]{:T(256)} %bitcast.5), kind=kLoop, calls=%fused_computation.6 | loop fusion | flops 2621440 | bytes 1048578 | tf_op jit(solution)/shard_map/add | solution.py:186
  59.0 0.0 copy-start.13
  59.0 3.4 %collective-permute-start.5 = (bf16[1024,256]{1,0:T(8,128)(2,1)S(1)}, bf16[1024,256]{1,0:T(8,128)(2,1)S(1)}, u32[]{:S(2)}, u32[]{:S(2)}) collective-permute-start(bf16[1024,256]{1,0:T(8,128)(2,1)S(1)} %maximum_add_fusion.refs_6_), channel_id=1, source_target_pairs={{0,192},{2,194},{4,196},{6,198},{8,200},{10,202},{12,204},{14,206}... | collective-permute-start | bytes 1572872 | tf_op jit(solution)/shard_map/ppermute | solution.py:160
  62.5 0.8 copy-done.3
  63.3 0.3 copy-done.1
  63.5 11.3 %incidence.3 = (bf16[1536,1536]{1,0:T(8,128)(2,1)}, bf16[1536,1024]{1,0:T(8,128)(2,1)}, bf16[1536,1024]{1,0:T(8,128)(2,1)}, bf16[1536,1024]{1,0:T(8,128)(2,1)}, ...) custom-call(s32[96,256]{1,0:T(8,128)} %copy.24.slots_ref, ...), custom_call_target="tpu_custom_call", output_to_operand_aliasing={{0}: (1, {}), {1}: (2, {}), {2}: (3, {}), {3}: (4, {}), {4}... | custom-call | flops 1536 | bytes 1536 | tf_op jit(solution)/shard_map/incidence/pallas_call | solution.py:59
  74.8 0.0 copy-start.14
  74.8 3.9 %fusion.21 = f32[1536,256]{1,0:T(8,128)S(1)} fusion(bf16[1536,1536]{1,0:T(8,128)(2,1)} %get-tuple-element.30, bf16[1536,256]{1,0:T(8,128)(2,1)S(1)} %copy-done), kind=kOutput, calls=%fused_computation.44 | convolution fusion | flops 1207959552 | bytes 7077888 | tf_op jit(solution)/shard_map/dot_general | solution.py:209
  78.7 0.6 slice.42
  79.3 1.0 fusion.20
  80.3 0.6 slice_add_fusion.1
  81.0 3.6 %collective-permute-start.7 = (bf16[512,256]{1,0:T(8,128)(2,1)S(1)}, bf16[512,256]{1,0:T(8,128)(2,1)S(1)}, u32[]{:S(2)}, u32[]{:S(2)}) collective-permute-start(bf16[512,256]{1,0:T(8,128)(2,1)S(1)} %slice_add_fusion.1), channel_id=1, source_target_pairs={{0,192},{2,194},{4,196},{6,198},{8,200},{10,202},{12,204},{14,206}... | collective-permute-start | bytes 786440 | tf_op jit(solution)/shard_map/ppermute | solution.py:160
  84.6 0.6 slice_add_fusion
  85.2 0.1 collective-permute-start.8
  85.3 1.0 fusion.18
  86.3 0.8 copy-done.11
  87.1 1.0 fusion.19
  88.1 0.2 add.48
  88.3 0.2 add.49
  88.5 0.2 add.50
  88.7 0.4 collective-permute-done.7
  89.2 4.2 %collective-permute-done.8 = bf16[512,256]{1,0:T(8,128)(2,1)S(1)} collective-permute-done((bf16[512,256]{1,0:T(8,128)(2,1)S(1)}, bf16[512,256]{1,0:T(8,128)(2,1)S(1)}, u32[]{:S(2)}, u32[]{:S(2)}) %collective-permute-start.8) | collective-permute-done | bytes 262176 | tf_op jit(solution)/shard_map/ppermute | solution.py:160
  93.3 1.0 fusion.3
  94.3 1.3 add.54
  95.7 7.2 %fusion.22 = f32[1536,256]{1,0:T(8,128)S(1)} fusion(bf16[1536,4096]{1,0:T(8,128)(2,1)} %get-tuple-element.33, bf16[4096,256]{1,0:T(8,128)(2,1)} %bitcast.8), kind=kOutput, calls=%fused_computation.45 | convolution fusion | flops 3221225472 | bytes 16252928 | tf_op jit(solution)/shard_map/dot_general | solution.py:209
  102.8 0.0 copy-start.2
  102.8 0.4 divide_convert_fusion.mean
  103.2 0.1 collective-permute-start.9
  103.3 2.4 %collective-permute-done.9.mean_far = bf16[1536,256]{1,0:T(8,128)(2,1)} collective-permute-done((bf16[1536,256]{1,0:T(8,128)(2,1)S(1)}, bf16[1536,256]{1,0:T(8,128)(2,1)}, u32[]{:S(2)}, u32[]{:S(2)}) %collective-permute-start.9) | collective-permute-done | bytes 786464 | tf_op jit(solution)/shard_map/ppermute | solution.py:151
  105.7 1.1 copy-done.7
  106.9 8.3 %layer.1 = (bf16[1536,256]{1,0:T(8,128)(2,1)}, bf16[512,256]{1,0:T(8,128)(2,1)S(1)}, bf16[512,256]{1,0:T(8,128)(2,1)S(1)}) custom-call(s32[1]{0:T(128)} %bitcast.core_ref, bf16[1536,256]{1,0:T(8,128)(2,1)S(1)} %copy-done, bf16[1536,256]{1,0:T(8,128)(2,1)S(1)} %copy-done.2, bf16[1536,256]{1,0:T(8,128)(2,1)S(1)} %divide_convert_fusion.mean, ...), custom_call_target="tpu_custom_call" | custom-call | flops 1610612736 | bytes 4718592 | tf_op jit(solution)/shard_map/layer/pallas_call | solution.py:128
  115.1 0.1 collective-permute-start.10
  115.3 1.4 collective-permute-done.10
  116.7 14.2 %all_to_all.25 = bf16[16,64,256]{2,1,0:T(8,128)(2,1)S(1)} all-to-all(bf16[16,64,256]{2,1,0:T(8,128)(2,1)S(1)} %bitcast.50), channel_id=1, replica_groups={{0,16,32,48,64,80,96,112,128,144,160,176,192,208,224,240},{2,18,34,50,6..., dimensions={0} | all-to-all | bytes 1048576 | tf_op jit(solution)/shard_map/all_to_all | solution.py:174
  130.9 0.1 reduce_sum.21
  131.0 16.5 %all_to_all.26 = bf16[8,64,256]{2,1,0:T(8,128)(2,1)S(1)} all-to-all(bf16[8,64,256]{2,1,0:T(8,128)(2,1)S(1)} %broadcast_in_dim.12), channel_id=1, replica_groups={{0,2,4,6,8,10,12,14},{16,18,20,22,24,26,28,30},{32,34,36,38,40,42,44,46..., dimensions={0} | all-to-all | bytes 524288 | tf_op jit(solution)/shard_map/all_to_all | solution.py:174
  147.6 0.8 broadcast_in_dim.13
  148.4 5.3 %all-to-all-start.4 = ((bf16[16,64,256]{2,1,0:T(8,128)(2,1)}), bf16[16,64,256]{2,1,0:T(8,128)(2,1)S(1)}, u32[]{:S(2)}, u32[]{:S(2)}) async-start(bf16[16,64,256]{2,1,0:T(8,128)(2,1)} %broadcast_in_dim.13), calls=%async_computation.4 | async-start | bytes 1048576 | tf_op jit(solution)/shard_map/all_to_all | solution.py:174
  153.7 8.7 %all-to-all-done.4 = bf16[16,64,256]{2,1,0:T(8,128)(2,1)S(1)} async-done(((bf16[16,64,256]{2,1,0:T(8,128)(2,1)}), bf16[16,64,256]{2,1,0:T(8,128)(2,1)S(1)}, u32[]{:S(2)}, u32[]{:S(2)}) %all-to-all-start.4) | async-done | bytes 524320 | tf_op jit(solution)/shard_map/all_to_all | solution.py:174
  162.4 0.1 convert_element_type.47
  162.5 0.1 slice_select_fusion.1
  162.7 1.1 pad_maximum_fusion.2
  (48 shorter events, 0.3 us)
Async XLA Ops:
  2.7 17.6 %all-to-all-start = ((bf16[8,32,256]{2,1,0:T(8,128)(2,1)}), bf16[8,32,256]{2,1,0:T(8,128)(2,1)S(1)}, u32[]{:S(2)}, u32[]{:S(2)}) async-start(bf16[8,32,256]{2,1,0:T(8,128)(2,1)} %broadcast_in_dim.11), calls=%async_computation | async-start | bytes 262144 | tf_op jit(solution)/shard_map/all_to_all | solution.py:174
  19.2 14.7 %copy-start = (bf16[1536,256]{1,0:T(8,128)(2,1)S(1)}, bf16[1536,256]{1,0:T(8,128)(2,1)}, u32[]{:S(2)}) copy-start(bf16[1536,256]{1,0:T(8,128)(2,1)} %own.1) | copy-start | bytes 2359300
  19.2 14.9 %copy-start.5 = (bf16[256,512]{1,0:T(8,128)(2,1)S(1)}, bf16[256,512]{1,0:T(8,128)(2,1)}, u32[]{:S(2)}) copy-start(bf16[256,512]{1,0:T(8,128)(2,1)} %w_neigh.1) | copy-start | bytes 786436
  19.2 14.9 %copy-start.6 = (bf16[256,512]{1,0:T(8,128)(2,1)S(1)}, bf16[256,512]{1,0:T(8,128)(2,1)}, u32[]{:S(2)}) copy-start(bf16[256,512]{1,0:T(8,128)(2,1)} %w_self.1) | copy-start | bytes 786436
  19.2 16.2 %copy-start.16 = (s32[1536,12]{0,1:T(8,128)S(1)}, s32[1536,12]{0,1:T(8,128)}, u32[]{:S(2)}) copy-start(s32[1536,12]{0,1:T(8,128)} %param.14) | copy-start | bytes 221188
  19.2 21.1 %copy-start.17 = (s32[1536]{0:T(1024)S(1)}, s32[1536]{0:T(1024)}, u32[]{:S(2)}) copy-start(s32[1536]{0:T(1024)} %param.15) | copy-start | bytes 18436
  20.3 21.8 %copy-start.15 = (bf16[8,32,256]{2,1,0:T(8,128)(2,1)}, bf16[8,32,256]{2,1,0:T(8,128)(2,1)S(1)}, u32[]{:S(2)}) copy-start(bf16[8,32,256]{2,1,0:T(8,128)(2,1)S(1)} %all-to-all-done) | copy-start | bytes 393220
  20.3 75.3 %all-to-all-start.1 = ((bf16[128,32,256]{2,1,0:T(8,128)(2,1)}), bf16[128,32,256]{2,1,0:T(8,128)(2,1)}, u32[]{:S(2)}, u32[]{:S(2)}) async-start(bf16[128,32,256]{2,1,0:T(8,128)(2,1)} %bitcast.7), calls=%async_computation.1 | async-start | bytes 4194304 | tf_op jit(solution)/shard_map/all_to_all | solution.py:227
  34.0 28.5 %collective-permute-start = (bf16[1536,256]{1,0:T(8,128)(2,1)S(1)}, bf16[1536,256]{1,0:T(8,128)(2,1)S(1)}, u32[]{:S(2)}, u32[]{:S(2)}) collective-permute-start(bf16[1536,256]{1,0:T(8,128)(2,1)S(1)} %copy-done), channel_id=1, source_target_pairs={{0,1},{1,0},{2,3},{3,2},{4,5},{5,4},{6,7},{7,6},{8,9},{9,8},{10,11... | collective-permute-start | bytes 2359304 | tf_op jit(solution)/shard_map/ppermute | solution.py:151
  34.9 27.5 %collective-permute-start.4 = (bf16[512,512]{1,0:T(8,128)(2,1)}, bf16[512,512]{1,0:T(8,128)(2,1)S(1)}, u32[]{:S(2)}, u32[]{:S(2)}) collective-permute-start(bf16[512,512]{1,0:T(8,128)(2,1)} %pad_maximum_fusion), channel_id=1, source_target_pairs={{0,1},{1,0},{2,3},{3,2},{4,5},{5,4},{6,7},{7,6},{8,9},{9,8},{10,11... | collective-permute-start | bytes 1572872 | tf_op jit(solution)/shard_map/ppermute | solution.py:151
  35.5 21.7 %collective-permute-start.1 = (bf16[256,256]{1,0:T(8,128)(2,1)S(1)}, bf16[256,256]{1,0:T(8,128)(2,1)}, u32[]{:S(2)}, u32[]{:S(2)}) collective-permute-start(bf16[256,256]{1,0:T(8,128)(2,1)S(1)} %bitcast.51), channel_id=1, source_target_pairs={{0,48},{2,50},{4,52},{6,54},{8,56},{10,58},{12,60},{14,62},{16,0},... | collective-permute-start | bytes 393224 | tf_op jit(solution)/shard_map/ppermute | solution.py:160
  36.5 20.6 %collective-permute-start.2 = (bf16[256,256]{1,0:T(8,128)(2,1)S(1)}, bf16[256,256]{1,0:T(8,128)(2,1)}, u32[]{:S(2)}, u32[]{:S(2)}) collective-permute-start(bf16[256,256]{1,0:T(8,128)(2,1)S(1)} %bitcast.52), channel_id=1, source_target_pairs={{0,32},{2,34},{4,36},{6,38},{8,40},{10,42},{12,44},{14,46},{16,48}... | collective-permute-start | bytes 393224 | tf_op jit(solution)/shard_map/ppermute | solution.py:160
  38.5 18.7 %collective-permute-start.3 = (bf16[256,256]{1,0:T(8,128)(2,1)S(1)}, bf16[256,256]{1,0:T(8,128)(2,1)}, u32[]{:S(2)}, u32[]{:S(2)}) collective-permute-start(bf16[256,256]{1,0:T(8,128)(2,1)S(1)} %bitcast.53), channel_id=1, source_target_pairs={{0,16},{2,18},{4,20},{6,22},{8,24},{10,26},{12,28},{14,30},{16,32}... | collective-permute-start | bytes 393224 | tf_op jit(solution)/shard_map/ppermute | solution.py:160
  59.0 3.5 %copy-start.13 = (bf16[1024,256]{1,0:T(8,128)(2,1)}, bf16[1024,256]{1,0:T(8,128)(2,1)S(1)}, u32[]{:S(2)}) copy-start(bf16[1024,256]{1,0:T(8,128)(2,1)S(1)} %maximum_add_fusion.refs_6_) | copy-start | bytes 1572868
  59.0 21.3 %collective-permute-start.5 = (bf16[1024,256]{1,0:T(8,128)(2,1)S(1)}, bf16[1024,256]{1,0:T(8,128)(2,1)S(1)}, u32[]{:S(2)}, u32[]{:S(2)}) collective-permute-start(bf16[1024,256]{1,0:T(8,128)(2,1)S(1)} %maximum_add_fusion.refs_6_), channel_id=1, source_target_pairs={{0,192},{2,194},{4,196},{6,198},{8,200},{10,202},{12,204},{14,206}... | collective-permute-start | bytes 1572872 | tf_op jit(solution)/shard_map/ppermute | solution.py:160
  62.5 22.1 %collective-permute-start.6 = (bf16[1024,256]{1,0:T(8,128)(2,1)S(1)}, bf16[1024,256]{1,0:T(8,128)(2,1)S(1)}, u32[]{:S(2)}, u32[]{:S(2)}) collective-permute-start(bf16[1024,256]{1,0:T(8,128)(2,1)S(1)} %maximum_add_fusion.refs_6_), channel_id=1, source_target_pairs={{0,64},{2,66},{4,68},{6,70},{8,72},{10,74},{12,76},{14,78},{16,80}... | collective-permute-start | bytes 1572872 | tf_op jit(solution)/shard_map/ppermute | solution.py:160
  62.5 0.8 copy-start.3
  62.5 1.0 copy-start.1
  74.8 3.9 %copy-start.18 = (s32[8,128]{1,0:T(8,128)S(1)}, s32[8,128]{1,0:T(8,128)}, u32[]{:S(2)}) copy-start(s32[8,128]{1,0:T(8,128)} %get-tuple-element.32) | copy-start | bytes 12292
  74.8 4.5 %copy-start.9 = (bf16[1536,1024]{1,0:T(8,128)(2,1)S(1)}, bf16[1536,1024]{1,0:T(8,128)(2,1)}, u32[]{:S(2)}) copy-start(bf16[1536,1024]{1,0:T(8,128)(2,1)} %get-tuple-element.29) | copy-start | bytes 9437188
  74.8 4.5 %copy-start.14 = (bf16[1024,256]{1,0:T(8,128)(2,1)S(1)}, bf16[1024,256]{1,0:T(8,128)(2,1)}, u32[]{:S(2)}) copy-start(bf16[1024,256]{1,0:T(8,128)(2,1)} %copy-done.13) | copy-start | bytes 1572868
  79.3 6.0 %copy-start.10 = (bf16[1536,1024]{1,0:T(8,128)(2,1)S(1)}, bf16[1536,1024]{1,0:T(8,128)(2,1)}, u32[]{:S(2)}) copy-start(bf16[1536,1024]{1,0:T(8,128)(2,1)} %get-tuple-element.27) | copy-start | bytes 9437188
  81.0 8.2 %collective-permute-start.7 = (bf16[512,256]{1,0:T(8,128)(2,1)S(1)}, bf16[512,256]{1,0:T(8,128)(2,1)S(1)}, u32[]{:S(2)}, u32[]{:S(2)}) collective-permute-start(bf16[512,256]{1,0:T(8,128)(2,1)S(1)} %slice_add_fusion.1), channel_id=1, source_target_pairs={{0,192},{2,194},{4,196},{6,198},{8,200},{10,202},{12,204},{14,206}... | collective-permute-start | bytes 786440 | tf_op jit(solution)/shard_map/ppermute | solution.py:160
  85.2 1.9 %copy-start.11 = (bf16[1536,1024]{1,0:T(8,128)(2,1)S(1)}, bf16[1536,1024]{1,0:T(8,128)(2,1)}, u32[]{:S(2)}) copy-start(bf16[1536,1024]{1,0:T(8,128)(2,1)} %get-tuple-element.28) | copy-start | bytes 9437188
  85.2 8.1 %collective-permute-start.8 = (bf16[512,256]{1,0:T(8,128)(2,1)S(1)}, bf16[512,256]{1,0:T(8,128)(2,1)S(1)}, u32[]{:S(2)}, u32[]{:S(2)}) collective-permute-start(bf16[512,256]{1,0:T(8,128)(2,1)S(1)} %slice_add_fusion), channel_id=1, source_target_pairs={{0,64},{2,66},{4,68},{6,70},{8,72},{10,74},{12,76},{14,78},{16,80}... | collective-permute-start | bytes 786440 | tf_op jit(solution)/shard_map/ppermute | solution.py:160
  88.5 4.8 %copy-start.12 = (bf16[1536,1024]{1,0:T(8,128)(2,1)S(1)}, bf16[1536,1024]{1,0:T(8,128)(2,1)}, u32[]{:S(2)}) copy-start(bf16[1536,1024]{1,0:T(8,128)(2,1)} %get-tuple-element.31) | copy-start | bytes 9437188
  95.6 7.2 %copy-start.8 = (f32[1536,256]{1,0:T(8,128)S(1)}, f32[1536,256]{1,0:T(8,128)}, u32[]{:S(2)}) copy-start(f32[1536,256]{1,0:T(8,128)} %add.54) | copy-start | bytes 4718596
  102.8 2.9 %copy-start.2 = (bf16[1536,256]{1,0:T(8,128)(2,1)S(1)}, bf16[1536,256]{1,0:T(8,128)(2,1)}, u32[]{:S(2)}) copy-start(bf16[1536,256]{1,0:T(8,128)(2,1)} %copy-done.1) | copy-start | bytes 2359300
  102.8 2.9 %copy-start.4 = (bf16[512,512]{1,0:T(8,128)(2,1)S(1)}, bf16[512,512]{1,0:T(8,128)(2,1)}, u32[]{:S(2)}) copy-start(bf16[512,512]{1,0:T(8,128)(2,1)} %copy-done.3) | copy-start | bytes 1572868
  103.2 2.5 %collective-permute-start.9 = (bf16[1536,256]{1,0:T(8,128)(2,1)S(1)}, bf16[1536,256]{1,0:T(8,128)(2,1)}, u32[]{:S(2)}, u32[]{:S(2)}) collective-permute-start(bf16[1536,256]{1,0:T(8,128)(2,1)S(1)} %divide_convert_fusion.mean), channel_id=1, source_target_pairs={{0,1},{1,0},{2,3},{3,2},{4,5},{5,4},{6,7},{7,6},{8,9},{9,8},{10,11... | collective-permute-start | bytes 2359304 | tf_op jit(solution)/shard_map/ppermute | solution.py:151
  105.7 1.1 copy-start.7
  115.1 1.5 collective-permute-start.10
  148.4 14.0 %all-to-all-start.4 = ((bf16[16,64,256]{2,1,0:T(8,128)(2,1)}), bf16[16,64,256]{2,1,0:T(8,128)(2,1)S(1)}, u32[]{:S(2)}, u32[]{:S(2)}) async-start(bf16[16,64,256]{2,1,0:T(8,128)(2,1)} %broadcast_in_dim.13), calls=%async_computation.4 | async-start | bytes 1048576 | tf_op jit(solution)/shard_map/all_to_all | solution.py:174
